TPU v7x, 256 devices: a whole 4x4x8 slice. The times are simulated.
256 devices in a mesh: ctx: 16 (over z, x_hi), head: 8 (over y, x_lo), dp: 2 (over core).
Axes of the slice: x: 4 (x_hi: 2, x_lo: 2; x = x_hi * 2 + x_lo), y: 4, z: 8, core: 2. Of those that a mesh axis runs over, the one named last changes fastest.
Arguments:
- query: bfloat16 [2, 8192, 5120], P('dp', 'ctx', 'head'), may hold values from -6 to 6
- key: bfloat16 [2, 8192, 1024], P('dp', 'ctx', 'head'), may hold values from -6 to 6
- value: bfloat16 [2, 8192, 1024], P('dp', 'ctx', 'head'), may hold values from -6 to 6
- output: bfloat16 [2, 8192, 5120], P('dp', 'ctx', 'head'), may hold values from -1.796875 to 1.796875
- output_gradient: bfloat16 [2, 8192, 5120], P('dp', 'ctx', 'head'), may hold values from -96 to 96
- parent: int32 [2, 16], P('dp'), may hold values from -1 to 14, as said below
- owner: int32 [2, 16], P('dp'), may hold values from 0 to 15, each once within a row
Outputs:
- d_query: bfloat16 [2, 8192, 5120], P('dp', 'ctx', 'head')
- d_key: bfloat16 [2, 8192, 1024], P('dp', 'ctx', 'head')
- d_value: bfloat16 [2, 8192, 1024], P('dp', 'ctx', 'head')
- bias_q_grad: float32 [5120], P('head')
- bias_k_grad: float32 [1024], P('head')
- bias_v_grad: float32 [1024], P('head')
Inputs may be any that keep to these rules, and one draw needn't show every extreme that they name: In each tree, tiles 0 to 1 form the prompt, each with parent t - 1 (tile 0 has -1); the later tiles form 8 consecutive runs (responses) of 1 or 2 tiles, some run of 2 in every tree; a run's first tile has as parent the last prompt tile, its second tile has the run's first tile.
All inputs are finite; a program needn't handle non-finite values.
Results may differ from a plain program's by a relative error of at most 0.005.
Values may be sent and summed in bfloat16 or wider, within the bound.
A program may use at most 64 MiB of HBM per device.

v0:
```python
import jax
import jax.numpy as jnp
from jax import lax
from jax.sharding import PartitionSpec as P

HEAD_WIDTH = 128


NEGATIVE_FILL = -1e30


def passed_along(block, axis, distance):
    devices = range(lax.axis_size(axis))
    route = [((i - distance) % len(devices), i) for i in devices]
    return lax.ppermute(block, axis, route)


def tree_tables(parent_row, owner_row):
    count = parent_row.shape[0]
    tiles = jnp.arange(count, dtype=jnp.int32)
    tile_at = jnp.sum(jnp.where(owner_row[None, :] == tiles[:, None], tiles[None, :], 0), axis=1)

    def climb(step, state):
        reach, current = state
        match = current[:, None] == tiles[None, :]
        reach = jnp.logical_or(reach, match)
        upward = jnp.sum(jnp.where(match, parent_row[None, :], 0), axis=1)
        upward = jnp.where(current < 0, -1, upward)
        return (reach, upward)

    reach, _ = lax.fori_loop(0, count, climb, (jnp.zeros((count, count), bool), tiles))
    select = (tile_at[:, None] == tiles[None, :]).astype(jnp.float32)
    packed = jnp.dot(
        jnp.dot(select, reach.astype(jnp.float32), precision=lax.Precision.HIGHEST),
        select.T,
        precision=lax.Precision.HIGHEST,
    )
    seen = (packed > 0.5).astype(jnp.int32)
    return (tile_at, seen)


def pick_entry(vector, index):
    spots = jnp.arange(vector.shape[0], dtype=jnp.int32)
    return jnp.sum(jnp.where(spots == index, vector, 0), axis=0)


def block_scores(query4, keys3, scale_factor, diagonal):
    scores = (
        jnp.einsum("ignd,jgd->gnij", query4, keys3, preferred_element_type=jnp.float32)
        * scale_factor
    )
    rows = query4.shape[0]
    causal = jnp.arange(rows)[:, None] >= jnp.arange(rows)[None, :]
    keep = jnp.logical_or(jnp.logical_not(diagonal), causal)
    return (scores, keep)


def stats_update(state, query4, keys3, scale_factor, diagonal):
    top, total = state
    scores, keep = block_scores(query4, keys3, scale_factor, diagonal)
    scores = jnp.where(keep, scores, NEGATIVE_FILL)
    top_new = jnp.maximum(top, jnp.max(scores, axis=-1))
    probs = jnp.where(keep, jnp.exp(scores - top_new[..., None]), 0.0)
    return (top_new, total * jnp.exp(top - top_new) + jnp.sum(probs, axis=-1))


def block_grads(query4, upstream4, lse, delta, keys3, values3, scale_factor, diagonal):
    scores, keep = block_scores(query4, keys3, scale_factor, diagonal)
    probs = jnp.where(keep, jnp.exp(scores - lse[..., None]), 0.0)
    value_add = jnp.einsum(
        "gnij,ignd->jgd", probs.astype(jnp.bfloat16), upstream4, preferred_element_type=jnp.float32
    )
    dprobs = jnp.einsum("ignd,jgd->gnij", upstream4, values3, preferred_element_type=jnp.float32)
    dscores = (probs * (dprobs - delta[..., None])).astype(jnp.bfloat16)
    query_add = (
        jnp.einsum("gnij,jgd->ignd", dscores, keys3, preferred_element_type=jnp.float32)
        * scale_factor
    )
    key_add = (
        jnp.einsum("gnij,ignd->jgd", dscores, query4, preferred_element_type=jnp.float32)
        * scale_factor
    )
    return (query_add, key_add, value_add)


def on_device(query, key, value, output, output_gradient, parent, owner):
    count = lax.axis_size("ctx")
    me = lax.axis_index("ctx")
    tile = query.shape[1]
    width = key.shape[2]
    heads_kv = width // HEAD_WIDTH
    group = query.shape[2] // width
    scale_factor = HEAD_WIDTH ** (-0.5)
    prompt_tiles = count // 8
    tile_at, seen = tree_tables(parent[0], owner[0])
    my_tile = pick_entry(tile_at, me)
    spots = jnp.arange(count, dtype=jnp.int32)
    seen_row = jnp.sum(jnp.where((spots == me)[:, None], seen, 0), axis=0)
    trained = my_tile >= prompt_tiles
    query4 = query[0].reshape(tile, heads_kv, group, HEAD_WIDTH)
    upstream4 = output_gradient[0].reshape(tile, heads_kv, group, HEAD_WIDTH)
    output4 = output[0].reshape(tile, heads_kv, group, HEAD_WIDTH)
    delta = jnp.sum(upstream4.astype(jnp.float32) * output4.astype(jnp.float32), axis=-1).transpose(
        1, 2, 0
    )
    stats_start = (
        jnp.full((heads_kv, group, tile), NEGATIVE_FILL, jnp.float32),
        jnp.zeros((heads_kv, group, tile), jnp.float32),
    )
    dq_start = jnp.zeros((tile, heads_kv, group, HEAD_WIDTH), jnp.float32)
    kv_pair = jnp.stack([key[0], value[0]])

    def visible(block):
        return jnp.logical_and(trained, pick_entry(seen_row, block) > 0)

    def stats_step(step, state):
        keys_now, top_total = state
        block = (me - step) % count
        top_total = lax.cond(
            visible(block),
            lambda st: stats_update(
                st, query4, keys_now.reshape(tile, heads_kv, HEAD_WIDTH), scale_factor, block == me
            ),
            lambda st: st,
            top_total,
        )
        keys_now = passed_along(keys_now, "ctx", 1)
        return (keys_now, top_total)

    _, (top, total) = lax.fori_loop(0, count, stats_step, (key[0], stats_start))
    lse = top + jnp.log(total)

    def grad_step(step, state):
        pair_now, partial_value, query_gradient = state
        block = (me - step) % count

        def work(inner):
            partial_in, dq_in = inner
            query_add, key_add, value_add = block_grads(
                query4,
                upstream4,
                lse,
                delta,
                pair_now[0].reshape(tile, heads_kv, HEAD_WIDTH),
                pair_now[1].reshape(tile, heads_kv, HEAD_WIDTH),
                scale_factor,
                block == me,
            )
            terms = jnp.stack([key_add.reshape(tile, width), value_add.reshape(tile, width)])
            return (partial_in + terms, dq_in + query_add)

        partial_value, query_gradient = lax.cond(
            visible(block), work, lambda inner: inner, (partial_value, query_gradient)
        )
        pair_now = passed_along(pair_now, "ctx", 1)
        partial_value = passed_along(partial_value, "ctx", 1)
        return (pair_now, partial_value, query_gradient)

    partial_start = jnp.zeros((2, tile, width), jnp.float32)
    _, grads, query_gradient = lax.fori_loop(
        0, count, grad_step, (kv_pair, partial_start, dq_start)
    )
    dq_rows = query_gradient.reshape(tile, heads_kv * group * HEAD_WIDTH)
    total_rows = lax.axis_size("dp") * query.shape[0] * count * tile
    norm = total_rows ** (-0.5)
    sum_q, sum_k, sum_v = lax.psum(
        (jnp.sum(dq_rows, axis=0), jnp.sum(grads[0], axis=0), jnp.sum(grads[1], axis=0)),
        ("ctx", "dp"),
    )
    return (
        dq_rows.astype(jnp.bfloat16)[None],
        grads[0].astype(jnp.bfloat16)[None],
        grads[1].astype(jnp.bfloat16)[None],
        sum_q * norm,
        sum_k * norm,
        sum_v * norm,
    )


def solution(mesh):
    return jax.shard_map(
        on_device,
        mesh=mesh,
        in_specs=(
            P("dp", "ctx", "head"),
            P("dp", "ctx", "head"),
            P("dp", "ctx", "head"),
            P("dp", "ctx", "head"),
            P("dp", "ctx", "head"),
            P("dp", None),
            P("dp", None),
        ),
        out_specs=(
            P("dp", "ctx", "head"),
            P("dp", "ctx", "head"),
            P("dp", "ctx", "head"),
            P("head"),
            P("head"),
            P("head"),
        ),
        check_vma=False,
    )
```

profile of v0, /device:TPU:13, one launch (start us, length us, event | category | flops | bytes accessed | tf_op | source)
XLA Modules:
  0.0 622.0 jit_solution(18267789650303174079)
XLA Ops:
  3.6 15.1 %while.53 = (s32[]{:T(128)}, pred[16,16]{1,0:T(8,128)(4,1)S(1)}, s32[16]{0:T(128)S(1)}, s32[1,16]{1,0:T(1,128)}, s32[]{:T(128)}, /*index=5*/s32[]{:T(128)}) while((s32[]{:T(128)}, pred[16,16]{1,0:T(8,128)(4,1)S(1)}, s32[16]{0:T(128)S(1)}, s32[1,16]{1,0:T(1,128)}, s32[]{:T(128)}, /*index=5*/s32[]{:T(128)}) %tuple.121), condition=%wide.region_3.4_spmd.clone, body=%wide.region_1.3_spmd.clone.sunk | while | flops 1555 | bytes 1039 | solution.py:31
  22.3 134.2 %while.51 = (s32[]{:T(128)}, bf16[512,128]{1,0:T(8,128)(2,1)S(1)}, f32[1,5,512]{2,1,0:T(8,128)S(1)}, f32[1,5,512]{2,1,0:T(8,128)S(1)}, s32[]{:T(128)}, /*index=5...) while((s32[]{:T(128)}, bf16[512,128]{1,0:T(8,128)(2,1)S(1)}, ...), condition=%wide.region_12.13_spmd, body=%wide.region_6.12_spmd.sunk | while | flops 346559552 | bytes 12978643 | solution.py:130
  65.3 5.8 collective-permute-done
  81.9 6.0 collective-permute-done
  90.5 7.7 %collective-permute-done = bf16[512,128]{1,0:T(8,128)(2,1)S(1)} collective-permute-done((bf16[512,128]{1,0:T(8,128)(2,1)}, bf16[512,128]{1,0:T(8,128)(2,1)S(1)}, u32[]{:S(2)}, u32[]{:S(2)}) %collective-permute-start) | collective-permute-done | bytes 131104 | tf_op jit(solution)/shard_map/while/body/eval_jaxpr/ppermute | solution.py:15
  100.7 6.3 %collective-permute-done = bf16[512,128]{1,0:T(8,128)(2,1)S(1)} collective-permute-done((bf16[512,128]{1,0:T(8,128)(2,1)}, bf16[512,128]{1,0:T(8,128)(2,1)S(1)}, u32[]{:S(2)}, u32[]{:S(2)}) %collective-permute-start) | collective-permute-done | bytes 131104 | tf_op jit(solution)/shard_map/while/body/eval_jaxpr/ppermute | solution.py:15
  125.9 5.8 collective-permute-done
  150.8 5.8 collective-permute-done
  159.1 373.8 %while.52 = (s32[]{:T(128)}, bf16[2,512,128]{2,1,0:T(8,128)(2,1)S(1)}, f32[2,512,128]{2,1,0:T(8,128)S(1)}, f32[512,1,5,128]{3,0,2,1:T(8,128)S(1)}, s32[]{:T(128)...) while((s32[]{:T(128)}, ...), condition=%wide.region_18.19_spmd, body=%wide.region_14.18_spmd.sunk | while | flops 1692336128 | bytes 39490120 | solution.py:160
  161.0 6.7 %conditional.5 = ((f32[2,512,128]{2,1,0:T(8,128)S(1)}, f32[512,1,5,128]{3,0,2,1:T(8,128)S(1)})) conditional(s32[]{:T(128)} %convert_element_type.114, (f32[2,512,128]{2,1,0:T(8,128)S(1)}, f32[512,1,5,128]{3,0,2,1:T(8,128)S(1)}) %tuple.114, (s32[]{:T(128)}, s32[]{:T(128)}, bf16[2,512,128]{2,1,0:T(8,128)(2,1)S(1)}, ...), branch_computations={%region_16.16_spmd, %region_17.17_spmd} | conditional | flops 1692336128 | bytes 34771008 | solution.py:152
  167.9 11.5 %collective-permute-done.2 = f32[2,512,128]{2,1,0:T(8,128)S(1)} collective-permute-done((f32[2,512,128]{2,1,0:T(8,128)S(1)}, f32[2,512,128]{2,1,0:T(8,128)S(1)}, u32[]{:S(2)}, u32[]{:S(2)}) %collective-permute-start.2) | collective-permute-done | bytes 524320 | tf_op jit(solution)/shard_map/while/body/eval_jaxpr/ppermute | solution.py:15
  187.6 18.4 %collective-permute-done.2 = f32[2,512,128]{2,1,0:T(8,128)S(1)} collective-permute-done((f32[2,512,128]{2,1,0:T(8,128)S(1)}, f32[2,512,128]{2,1,0:T(8,128)S(1)}, u32[]{:S(2)}, u32[]{:S(2)}) %collective-permute-start.2) | collective-permute-done | bytes 524320 | tf_op jit(solution)/shard_map/while/body/eval_jaxpr/ppermute | solution.py:15
  210.7 6.7 %conditional.5 = ((f32[2,512,128]{2,1,0:T(8,128)S(1)}, f32[512,1,5,128]{3,0,2,1:T(8,128)S(1)})) conditional(s32[]{:T(128)} %convert_element_type.114, (f32[2,512,128]{2,1,0:T(8,128)S(1)}, f32[512,1,5,128]{3,0,2,1:T(8,128)S(1)}) %tuple.114, (s32[]{:T(128)}, s32[]{:T(128)}, bf16[2,512,128]{2,1,0:T(8,128)(2,1)S(1)}, ...), branch_computations={%region_16.16_spmd, %region_17.17_spmd} | conditional | flops 1692336128 | bytes 34771008 | solution.py:152
  217.6 9.6 %collective-permute-done.2 = f32[2,512,128]{2,1,0:T(8,128)S(1)} collective-permute-done((f32[2,512,128]{2,1,0:T(8,128)S(1)}, f32[2,512,128]{2,1,0:T(8,128)S(1)}, u32[]{:S(2)}, u32[]{:S(2)}) %collective-permute-start.2) | collective-permute-done | bytes 524320 | tf_op jit(solution)/shard_map/while/body/eval_jaxpr/ppermute | solution.py:15
  231.9 7.5 %collective-permute-start.2 = (f32[2,512,128]{2,1,0:T(8,128)S(1)}, f32[2,512,128]{2,1,0:T(8,128)S(1)}, u32[]{:S(2)}, u32[]{:S(2)}) collective-permute-start(f32[2,512,128]{2,1,0:T(8,128)S(1)} %get-tuple-element.818), channel_id=1, source_target_pairs={{240,0},{0,16},{16,32},{32,48},{48,64},{64,80},{80,96},{96,112},{1... | collective-permute-start | bytes 1572872 | tf_op jit(solution)/shard_map/while/body/eval_jaxpr/ppermute | solution.py:15
  239.5 10.1 %collective-permute-done.2 = f32[2,512,128]{2,1,0:T(8,128)S(1)} collective-permute-done((f32[2,512,128]{2,1,0:T(8,128)S(1)}, f32[2,512,128]{2,1,0:T(8,128)S(1)}, u32[]{:S(2)}, u32[]{:S(2)}) %collective-permute-start.2) | collective-permute-done | bytes 524320 | tf_op jit(solution)/shard_map/while/body/eval_jaxpr/ppermute | solution.py:15
  254.6 8.6 %collective-permute-start.1 = (bf16[2,512,128]{2,1,0:T(8,128)(2,1)S(1)}, bf16[2,512,128]{2,1,0:T(8,128)(2,1)S(1)}, u32[]{:S(2)}, u32[]{:S(2)}) collective-permute-start(bf16[2,512,128]{2,1,0:T(8,128)(2,1)S(1)} %copy.59), channel_id=1, source_target_pairs={{240,0},{0,16},{16,32},{32,48},{48,64},{64,80},{80,96},{96,112},{1... | collective-permute-start | bytes 786440 | tf_op jit(solution)/shard_map/while/body/eval_jaxpr/ppermute | solution.py:15
  263.2 8.9 %collective-permute-done.2 = f32[2,512,128]{2,1,0:T(8,128)S(1)} collective-permute-done((f32[2,512,128]{2,1,0:T(8,128)S(1)}, f32[2,512,128]{2,1,0:T(8,128)S(1)}, u32[]{:S(2)}, u32[]{:S(2)}) %collective-permute-start.2) | collective-permute-done | bytes 524320 | tf_op jit(solution)/shard_map/while/body/eval_jaxpr/ppermute | solution.py:15
  277.7 17.7 %collective-permute-done.2 = f32[2,512,128]{2,1,0:T(8,128)S(1)} collective-permute-done((f32[2,512,128]{2,1,0:T(8,128)S(1)}, f32[2,512,128]{2,1,0:T(8,128)S(1)}, u32[]{:S(2)}, u32[]{:S(2)}) %collective-permute-start.2) | collective-permute-done | bytes 524320 | tf_op jit(solution)/shard_map/while/body/eval_jaxpr/ppermute | solution.py:15
  302.1 17.3 %collective-permute-done.2 = f32[2,512,128]{2,1,0:T(8,128)S(1)} collective-permute-done((f32[2,512,128]{2,1,0:T(8,128)S(1)}, f32[2,512,128]{2,1,0:T(8,128)S(1)}, u32[]{:S(2)}, u32[]{:S(2)}) %collective-permute-start.2) | collective-permute-done | bytes 524320 | tf_op jit(solution)/shard_map/while/body/eval_jaxpr/ppermute | solution.py:15
  327.1 11.2 %collective-permute-done.2 = f32[2,512,128]{2,1,0:T(8,128)S(1)} collective-permute-done((f32[2,512,128]{2,1,0:T(8,128)S(1)}, f32[2,512,128]{2,1,0:T(8,128)S(1)}, u32[]{:S(2)}, u32[]{:S(2)}) %collective-permute-start.2) | collective-permute-done | bytes 524320 | tf_op jit(solution)/shard_map/while/body/eval_jaxpr/ppermute | solution.py:15
  350.0 9.1 %collective-permute-done.2 = f32[2,512,128]{2,1,0:T(8,128)S(1)} collective-permute-done((f32[2,512,128]{2,1,0:T(8,128)S(1)}, f32[2,512,128]{2,1,0:T(8,128)S(1)}, u32[]{:S(2)}, u32[]{:S(2)}) %collective-permute-start.2) | collective-permute-done | bytes 524320 | tf_op jit(solution)/shard_map/while/body/eval_jaxpr/ppermute | solution.py:15
  371.4 8.2 %collective-permute-done.2 = f32[2,512,128]{2,1,0:T(8,128)S(1)} collective-permute-done((f32[2,512,128]{2,1,0:T(8,128)S(1)}, f32[2,512,128]{2,1,0:T(8,128)S(1)}, u32[]{:S(2)}, u32[]{:S(2)}) %collective-permute-start.2) | collective-permute-done | bytes 524320 | tf_op jit(solution)/shard_map/while/body/eval_jaxpr/ppermute | solution.py:15
  403.6 8.1 %collective-permute-start.2 = (f32[2,512,128]{2,1,0:T(8,128)S(1)}, f32[2,512,128]{2,1,0:T(8,128)S(1)}, u32[]{:S(2)}, u32[]{:S(2)}) collective-permute-start(f32[2,512,128]{2,1,0:T(8,128)S(1)} %get-tuple-element.818), channel_id=1, source_target_pairs={{240,0},{0,16},{16,32},{32,48},{48,64},{64,80},{80,96},{96,112},{1... | collective-permute-start | bytes 1572872 | tf_op jit(solution)/shard_map/while/body/eval_jaxpr/ppermute | solution.py:15
  429.5 7.9 %collective-permute-start.1 = (bf16[2,512,128]{2,1,0:T(8,128)(2,1)S(1)}, bf16[2,512,128]{2,1,0:T(8,128)(2,1)S(1)}, u32[]{:S(2)}, u32[]{:S(2)}) collective-permute-start(bf16[2,512,128]{2,1,0:T(8,128)(2,1)S(1)} %copy.59), channel_id=1, source_target_pairs={{240,0},{0,16},{16,32},{32,48},{48,64},{64,80},{80,96},{96,112},{1... | collective-permute-start | bytes 786440 | tf_op jit(solution)/shard_map/while/body/eval_jaxpr/ppermute | solution.py:15
  437.3 14.2 %collective-permute-done.2 = f32[2,512,128]{2,1,0:T(8,128)S(1)} collective-permute-done((f32[2,512,128]{2,1,0:T(8,128)S(1)}, f32[2,512,128]{2,1,0:T(8,128)S(1)}, u32[]{:S(2)}, u32[]{:S(2)}) %collective-permute-start.2) | collective-permute-done | bytes 524320 | tf_op jit(solution)/shard_map/while/body/eval_jaxpr/ppermute | solution.py:15
  459.1 6.7 %conditional.5 = ((f32[2,512,128]{2,1,0:T(8,128)S(1)}, f32[512,1,5,128]{3,0,2,1:T(8,128)S(1)})) conditional(s32[]{:T(128)} %convert_element_type.114, (f32[2,512,128]{2,1,0:T(8,128)S(1)}, f32[512,1,5,128]{3,0,2,1:T(8,128)S(1)}) %tuple.114, (s32[]{:T(128)}, s32[]{:T(128)}, bf16[2,512,128]{2,1,0:T(8,128)(2,1)S(1)}, ...), branch_computations={%region_16.16_spmd, %region_17.17_spmd} | conditional | flops 1692336128 | bytes 34771008 | solution.py:152
  466.0 14.2 %collective-permute-done.2 = f32[2,512,128]{2,1,0:T(8,128)S(1)} collective-permute-done((f32[2,512,128]{2,1,0:T(8,128)S(1)}, f32[2,512,128]{2,1,0:T(8,128)S(1)}, u32[]{:S(2)}, u32[]{:S(2)}) %collective-permute-start.2) | collective-permute-done | bytes 524320 | tf_op jit(solution)/shard_map/while/body/eval_jaxpr/ppermute | solution.py:15
  487.7 7.3 %collective-permute-start.2 = (f32[2,512,128]{2,1,0:T(8,128)S(1)}, f32[2,512,128]{2,1,0:T(8,128)S(1)}, u32[]{:S(2)}, u32[]{:S(2)}) collective-permute-start(f32[2,512,128]{2,1,0:T(8,128)S(1)} %get-tuple-element.818), channel_id=1, source_target_pairs={{240,0},{0,16},{16,32},{32,48},{48,64},{64,80},{80,96},{96,112},{1... | collective-permute-start | bytes 1572872 | tf_op jit(solution)/shard_map/while/body/eval_jaxpr/ppermute | solution.py:15
  495.1 10.4 %collective-permute-done.2 = f32[2,512,128]{2,1,0:T(8,128)S(1)} collective-permute-done((f32[2,512,128]{2,1,0:T(8,128)S(1)}, f32[2,512,128]{2,1,0:T(8,128)S(1)}, u32[]{:S(2)}, u32[]{:S(2)}) %collective-permute-start.2) | collective-permute-done | bytes 524320 | tf_op jit(solution)/shard_map/while/body/eval_jaxpr/ppermute | solution.py:15
  519.9 7.4 %collective-permute-done.2 = f32[2,512,128]{2,1,0:T(8,128)S(1)} collective-permute-done((f32[2,512,128]{2,1,0:T(8,128)S(1)}, f32[2,512,128]{2,1,0:T(8,128)S(1)}, u32[]{:S(2)}, u32[]{:S(2)}) %collective-permute-start.2) | collective-permute-done | bytes 524320 | tf_op jit(solution)/shard_map/while/body/eval_jaxpr/ppermute | solution.py:15
  535.1 85.8 %all-reduce = (f32[640]{0:T(1024)S(1)}, f32[128]{0:T(128)S(1)}, f32[128]{0:T(128)S(1)}) all-reduce(f32[640]{0:T(1024)S(1)} %bitcast.138, f32[128]{0:T(128)S(1)} %get-tuple-element.619, f32[128]{0:T(128)S(1)} %get-tuple-element.618), channel_id=1, replica_groups=mesh['ctx'=16,'head'=8,'dp'=2] {'ctx','dp'}, use_global_device_ids=true, to_apply=%region_20.21 | all-reduce | flops 896 | bytes 7168 | tf_op jit(solution)/shard_map/psum | solution.py:166
  (304 shorter events, 280.3 us)
Async XLA Ops:
  167.7 11.7 %collective-permute-start.2 = (f32[2,512,128]{2,1,0:T(8,128)S(1)}, f32[2,512,128]{2,1,0:T(8,128)S(1)}, u32[]{:S(2)}, u32[]{:S(2)}) collective-permute-start(f32[2,512,128]{2,1,0:T(8,128)S(1)} %get-tuple-element.818), channel_id=1, source_target_pairs={{240,0},{0,16},{16,32},{32,48},{48,64},{64,80},{80,96},{96,112},{1... | collective-permute-start | bytes 1572872 | tf_op jit(solution)/shard_map/while/body/eval_jaxpr/ppermute | solution.py:15
  167.8 14.4 %collective-permute-start.1 = (bf16[2,512,128]{2,1,0:T(8,128)(2,1)S(1)}, bf16[2,512,128]{2,1,0:T(8,128)(2,1)S(1)}, u32[]{:S(2)}, u32[]{:S(2)}) collective-permute-start(bf16[2,512,128]{2,1,0:T(8,128)(2,1)S(1)} %copy.59), channel_id=1, source_target_pairs={{240,0},{0,16},{16,32},{32,48},{48,64},{64,80},{80,96},{96,112},{1... | collective-permute-start | bytes 786440 | tf_op jit(solution)/shard_map/while/body/eval_jaxpr/ppermute | solution.py:15
  184.2 21.8 %collective-permute-start.2 = (f32[2,512,128]{2,1,0:T(8,128)S(1)}, f32[2,512,128]{2,1,0:T(8,128)S(1)}, u32[]{:S(2)}, u32[]{:S(2)}) collective-permute-start(f32[2,512,128]{2,1,0:T(8,128)S(1)} %get-tuple-element.818), channel_id=1, source_target_pairs={{240,0},{0,16},{16,32},{32,48},{48,64},{64,80},{80,96},{96,112},{1... | collective-permute-start | bytes 1572872 | tf_op jit(solution)/shard_map/while/body/eval_jaxpr/ppermute | solution.py:15
  184.3 24.5 %collective-permute-start.1 = (bf16[2,512,128]{2,1,0:T(8,128)(2,1)S(1)}, bf16[2,512,128]{2,1,0:T(8,128)(2,1)S(1)}, u32[]{:S(2)}, u32[]{:S(2)}) collective-permute-start(bf16[2,512,128]{2,1,0:T(8,128)(2,1)S(1)} %copy.59), channel_id=1, source_target_pairs={{240,0},{0,16},{16,32},{32,48},{48,64},{64,80},{80,96},{96,112},{1... | collective-permute-start | bytes 786440 | tf_op jit(solution)/shard_map/while/body/eval_jaxpr/ppermute | solution.py:15
  217.4 9.8 %collective-permute-start.2 = (f32[2,512,128]{2,1,0:T(8,128)S(1)}, f32[2,512,128]{2,1,0:T(8,128)S(1)}, u32[]{:S(2)}, u32[]{:S(2)}) collective-permute-start(f32[2,512,128]{2,1,0:T(8,128)S(1)} %get-tuple-element.818), channel_id=1, source_target_pairs={{240,0},{0,16},{16,32},{32,48},{48,64},{64,80},{80,96},{96,112},{1... | collective-permute-start | bytes 1572872 | tf_op jit(solution)/shard_map/while/body/eval_jaxpr/ppermute | solution.py:15
  217.5 12.5 %collective-permute-start.1 = (bf16[2,512,128]{2,1,0:T(8,128)(2,1)S(1)}, bf16[2,512,128]{2,1,0:T(8,128)(2,1)S(1)}, u32[]{:S(2)}, u32[]{:S(2)}) collective-permute-start(bf16[2,512,128]{2,1,0:T(8,128)(2,1)S(1)} %copy.59), channel_id=1, source_target_pairs={{240,0},{0,16},{16,32},{32,48},{48,64},{64,80},{80,96},{96,112},{1... | collective-permute-start | bytes 786440 | tf_op jit(solution)/shard_map/while/body/eval_jaxpr/ppermute | solution.py:15
  231.9 17.7 %collective-permute-start.2 = (f32[2,512,128]{2,1,0:T(8,128)S(1)}, f32[2,512,128]{2,1,0:T(8,128)S(1)}, u32[]{:S(2)}, u32[]{:S(2)}) collective-permute-start(f32[2,512,128]{2,1,0:T(8,128)S(1)} %get-tuple-element.818), channel_id=1, source_target_pairs={{240,0},{0,16},{16,32},{32,48},{48,64},{64,80},{80,96},{96,112},{1... | collective-permute-start | bytes 1572872 | tf_op jit(solution)/shard_map/while/body/eval_jaxpr/ppermute | solution.py:15
  239.4 12.8 %collective-permute-start.1 = (bf16[2,512,128]{2,1,0:T(8,128)(2,1)S(1)}, bf16[2,512,128]{2,1,0:T(8,128)(2,1)S(1)}, u32[]{:S(2)}, u32[]{:S(2)}) collective-permute-start(bf16[2,512,128]{2,1,0:T(8,128)(2,1)S(1)} %copy.59), channel_id=1, source_target_pairs={{240,0},{0,16},{16,32},{32,48},{48,64},{64,80},{80,96},{96,112},{1... | collective-permute-start | bytes 786440 | tf_op jit(solution)/shard_map/while/body/eval_jaxpr/ppermute | solution.py:15
  254.1 18.0 %collective-permute-start.2 = (f32[2,512,128]{2,1,0:T(8,128)S(1)}, f32[2,512,128]{2,1,0:T(8,128)S(1)}, u32[]{:S(2)}, u32[]{:S(2)}) collective-permute-start(f32[2,512,128]{2,1,0:T(8,128)S(1)} %get-tuple-element.818), channel_id=1, source_target_pairs={{240,0},{0,16},{16,32},{32,48},{48,64},{64,80},{80,96},{96,112},{1... | collective-permute-start | bytes 1572872 | tf_op jit(solution)/shard_map/while/body/eval_jaxpr/ppermute | solution.py:15
  254.6 21.0 %collective-permute-start.1 = (bf16[2,512,128]{2,1,0:T(8,128)(2,1)S(1)}, bf16[2,512,128]{2,1,0:T(8,128)(2,1)S(1)}, u32[]{:S(2)}, u32[]{:S(2)}) collective-permute-start(bf16[2,512,128]{2,1,0:T(8,128)(2,1)S(1)} %copy.59), channel_id=1, source_target_pairs={{240,0},{0,16},{16,32},{32,48},{48,64},{64,80},{80,96},{96,112},{1... | collective-permute-start | bytes 786440 | tf_op jit(solution)/shard_map/while/body/eval_jaxpr/ppermute | solution.py:15
  277.5 17.9 %collective-permute-start.2 = (f32[2,512,128]{2,1,0:T(8,128)S(1)}, f32[2,512,128]{2,1,0:T(8,128)S(1)}, u32[]{:S(2)}, u32[]{:S(2)}) collective-permute-start(f32[2,512,128]{2,1,0:T(8,128)S(1)} %get-tuple-element.818), channel_id=1, source_target_pairs={{240,0},{0,16},{16,32},{32,48},{48,64},{64,80},{80,96},{96,112},{1... | collective-permute-start | bytes 1572872 | tf_op jit(solution)/shard_map/while/body/eval_jaxpr/ppermute | solution.py:15
  277.6 22.4 %collective-permute-start.1 = (bf16[2,512,128]{2,1,0:T(8,128)(2,1)S(1)}, bf16[2,512,128]{2,1,0:T(8,128)(2,1)S(1)}, u32[]{:S(2)}, u32[]{:S(2)}) collective-permute-start(bf16[2,512,128]{2,1,0:T(8,128)(2,1)S(1)} %copy.59), channel_id=1, source_target_pairs={{240,0},{0,16},{16,32},{32,48},{48,64},{64,80},{80,96},{96,112},{1... | collective-permute-start | bytes 786440 | tf_op jit(solution)/shard_map/while/body/eval_jaxpr/ppermute | solution.py:15
  301.9 17.5 %collective-permute-start.2 = (f32[2,512,128]{2,1,0:T(8,128)S(1)}, f32[2,512,128]{2,1,0:T(8,128)S(1)}, u32[]{:S(2)}, u32[]{:S(2)}) collective-permute-start(f32[2,512,128]{2,1,0:T(8,128)S(1)} %get-tuple-element.818), channel_id=1, source_target_pairs={{240,0},{0,16},{16,32},{32,48},{48,64},{64,80},{80,96},{96,112},{1... | collective-permute-start | bytes 1572872 | tf_op jit(solution)/shard_map/while/body/eval_jaxpr/ppermute | solution.py:15
  302.0 23.0 %collective-permute-start.1 = (bf16[2,512,128]{2,1,0:T(8,128)(2,1)S(1)}, bf16[2,512,128]{2,1,0:T(8,128)(2,1)S(1)}, u32[]{:S(2)}, u32[]{:S(2)}) collective-permute-start(bf16[2,512,128]{2,1,0:T(8,128)(2,1)S(1)} %copy.59), channel_id=1, source_target_pairs={{240,0},{0,16},{16,32},{32,48},{48,64},{64,80},{80,96},{96,112},{1... | collective-permute-start | bytes 786440 | tf_op jit(solution)/shard_map/while/body/eval_jaxpr/ppermute | solution.py:15
  326.9 11.4 %collective-permute-start.2 = (f32[2,512,128]{2,1,0:T(8,128)S(1)}, f32[2,512,128]{2,1,0:T(8,128)S(1)}, u32[]{:S(2)}, u32[]{:S(2)}) collective-permute-start(f32[2,512,128]{2,1,0:T(8,128)S(1)} %get-tuple-element.818), channel_id=1, source_target_pairs={{240,0},{0,16},{16,32},{32,48},{48,64},{64,80},{80,96},{96,112},{1... | collective-permute-start | bytes 1572872 | tf_op jit(solution)/shard_map/while/body/eval_jaxpr/ppermute | solution.py:15
  327.0 16.3 %collective-permute-start.1 = (bf16[2,512,128]{2,1,0:T(8,128)(2,1)S(1)}, bf16[2,512,128]{2,1,0:T(8,128)(2,1)S(1)}, u32[]{:S(2)}, u32[]{:S(2)}) collective-permute-start(bf16[2,512,128]{2,1,0:T(8,128)(2,1)S(1)} %copy.59), channel_id=1, source_target_pairs={{240,0},{0,16},{16,32},{32,48},{48,64},{64,80},{80,96},{96,112},{1... | collective-permute-start | bytes 786440 | tf_op jit(solution)/shard_map/while/body/eval_jaxpr/ppermute | solution.py:15
  345.3 13.9 %collective-permute-start.2 = (f32[2,512,128]{2,1,0:T(8,128)S(1)}, f32[2,512,128]{2,1,0:T(8,128)S(1)}, u32[]{:S(2)}, u32[]{:S(2)}) collective-permute-start(f32[2,512,128]{2,1,0:T(8,128)S(1)} %get-tuple-element.818), channel_id=1, source_target_pairs={{240,0},{0,16},{16,32},{32,48},{48,64},{64,80},{80,96},{96,112},{1... | collective-permute-start | bytes 1572872 | tf_op jit(solution)/shard_map/while/body/eval_jaxpr/ppermute | solution.py:15
  349.9 14.8 %collective-permute-start.1 = (bf16[2,512,128]{2,1,0:T(8,128)(2,1)S(1)}, bf16[2,512,128]{2,1,0:T(8,128)(2,1)S(1)}, u32[]{:S(2)}, u32[]{:S(2)}) collective-permute-start(bf16[2,512,128]{2,1,0:T(8,128)(2,1)S(1)} %copy.59), channel_id=1, source_target_pairs={{240,0},{0,16},{16,32},{32,48},{48,64},{64,80},{80,96},{96,112},{1... | collective-permute-start | bytes 786440 | tf_op jit(solution)/shard_map/while/body/eval_jaxpr/ppermute | solution.py:15
  366.7 12.9 %collective-permute-start.2 = (f32[2,512,128]{2,1,0:T(8,128)S(1)}, f32[2,512,128]{2,1,0:T(8,128)S(1)}, u32[]{:S(2)}, u32[]{:S(2)}) collective-permute-start(f32[2,512,128]{2,1,0:T(8,128)S(1)} %get-tuple-element.818), channel_id=1, source_target_pairs={{240,0},{0,16},{16,32},{32,48},{48,64},{64,80},{80,96},{96,112},{1... | collective-permute-start | bytes 1572872 | tf_op jit(solution)/shard_map/while/body/eval_jaxpr/ppermute | solution.py:15
  371.3 13.9 %collective-permute-start.1 = (bf16[2,512,128]{2,1,0:T(8,128)(2,1)S(1)}, bf16[2,512,128]{2,1,0:T(8,128)(2,1)S(1)}, u32[]{:S(2)}, u32[]{:S(2)}) collective-permute-start(bf16[2,512,128]{2,1,0:T(8,128)(2,1)S(1)} %copy.59), channel_id=1, source_target_pairs={{240,0},{0,16},{16,32},{32,48},{48,64},{64,80},{80,96},{96,112},{1... | collective-permute-start | bytes 786440 | tf_op jit(solution)/shard_map/while/body/eval_jaxpr/ppermute | solution.py:15
  387.1 11.7 %collective-permute-start.2 = (f32[2,512,128]{2,1,0:T(8,128)S(1)}, f32[2,512,128]{2,1,0:T(8,128)S(1)}, u32[]{:S(2)}, u32[]{:S(2)}) collective-permute-start(f32[2,512,128]{2,1,0:T(8,128)S(1)} %get-tuple-element.818), channel_id=1, source_target_pairs={{240,0},{0,16},{16,32},{32,48},{48,64},{64,80},{80,96},{96,112},{1... | collective-permute-start | bytes 1572872 | tf_op jit(solution)/shard_map/while/body/eval_jaxpr/ppermute | solution.py:15
  391.8 9.9 %collective-permute-start.1 = (bf16[2,512,128]{2,1,0:T(8,128)(2,1)S(1)}, bf16[2,512,128]{2,1,0:T(8,128)(2,1)S(1)}, u32[]{:S(2)}, u32[]{:S(2)}) collective-permute-start(bf16[2,512,128]{2,1,0:T(8,128)(2,1)S(1)} %copy.59), channel_id=1, source_target_pairs={{240,0},{0,16},{16,32},{32,48},{48,64},{64,80},{80,96},{96,112},{1... | collective-permute-start | bytes 786440 | tf_op jit(solution)/shard_map/while/body/eval_jaxpr/ppermute | solution.py:15
  403.6 17.9 %collective-permute-start.2 = (f32[2,512,128]{2,1,0:T(8,128)S(1)}, f32[2,512,128]{2,1,0:T(8,128)S(1)}, u32[]{:S(2)}, u32[]{:S(2)}) collective-permute-start(f32[2,512,128]{2,1,0:T(8,128)S(1)} %get-tuple-element.818), channel_id=1, source_target_pairs={{240,0},{0,16},{16,32},{32,48},{48,64},{64,80},{80,96},{96,112},{1... | collective-permute-start | bytes 1572872 | tf_op jit(solution)/shard_map/while/body/eval_jaxpr/ppermute | solution.py:15
  411.7 14.2 %collective-permute-start.1 = (bf16[2,512,128]{2,1,0:T(8,128)(2,1)S(1)}, bf16[2,512,128]{2,1,0:T(8,128)(2,1)S(1)}, u32[]{:S(2)}, u32[]{:S(2)}) collective-permute-start(bf16[2,512,128]{2,1,0:T(8,128)(2,1)S(1)} %copy.59), channel_id=1, source_target_pairs={{240,0},{0,16},{16,32},{32,48},{48,64},{64,80},{80,96},{96,112},{1... | collective-permute-start | bytes 786440 | tf_op jit(solution)/shard_map/while/body/eval_jaxpr/ppermute | solution.py:15
  427.8 23.8 %collective-permute-start.2 = (f32[2,512,128]{2,1,0:T(8,128)S(1)}, f32[2,512,128]{2,1,0:T(8,128)S(1)}, u32[]{:S(2)}, u32[]{:S(2)}) collective-permute-start(f32[2,512,128]{2,1,0:T(8,128)S(1)} %get-tuple-element.818), channel_id=1, source_target_pairs={{240,0},{0,16},{16,32},{32,48},{48,64},{64,80},{80,96},{96,112},{1... | collective-permute-start | bytes 1572872 | tf_op jit(solution)/shard_map/while/body/eval_jaxpr/ppermute | solution.py:15
  429.5 27.7 %collective-permute-start.1 = (bf16[2,512,128]{2,1,0:T(8,128)(2,1)S(1)}, bf16[2,512,128]{2,1,0:T(8,128)(2,1)S(1)}, u32[]{:S(2)}, u32[]{:S(2)}) collective-permute-start(bf16[2,512,128]{2,1,0:T(8,128)(2,1)S(1)} %copy.59), channel_id=1, source_target_pairs={{240,0},{0,16},{16,32},{32,48},{48,64},{64,80},{80,96},{96,112},{1... | collective-permute-start | bytes 786440 | tf_op jit(solution)/shard_map/while/body/eval_jaxpr/ppermute | solution.py:15
  465.8 14.4 %collective-permute-start.2 = (f32[2,512,128]{2,1,0:T(8,128)S(1)}, f32[2,512,128]{2,1,0:T(8,128)S(1)}, u32[]{:S(2)}, u32[]{:S(2)}) collective-permute-start(f32[2,512,128]{2,1,0:T(8,128)S(1)} %get-tuple-element.818), channel_id=1, source_target_pairs={{240,0},{0,16},{16,32},{32,48},{48,64},{64,80},{80,96},{96,112},{1... | collective-permute-start | bytes 1572872 | tf_op jit(solution)/shard_map/while/body/eval_jaxpr/ppermute | solution.py:15
  465.9 19.9 %collective-permute-start.1 = (bf16[2,512,128]{2,1,0:T(8,128)(2,1)S(1)}, bf16[2,512,128]{2,1,0:T(8,128)(2,1)S(1)}, u32[]{:S(2)}, u32[]{:S(2)}) collective-permute-start(bf16[2,512,128]{2,1,0:T(8,128)(2,1)S(1)} %copy.59), channel_id=1, source_target_pairs={{240,0},{0,16},{16,32},{32,48},{48,64},{64,80},{80,96},{96,112},{1... | collective-permute-start | bytes 786440 | tf_op jit(solution)/shard_map/while/body/eval_jaxpr/ppermute | solution.py:15
  487.7 17.8 %collective-permute-start.2 = (f32[2,512,128]{2,1,0:T(8,128)S(1)}, f32[2,512,128]{2,1,0:T(8,128)S(1)}, u32[]{:S(2)}, u32[]{:S(2)}) collective-permute-start(f32[2,512,128]{2,1,0:T(8,128)S(1)} %get-tuple-element.818), channel_id=1, source_target_pairs={{240,0},{0,16},{16,32},{32,48},{48,64},{64,80},{80,96},{96,112},{1... | collective-permute-start | bytes 1572872 | tf_op jit(solution)/shard_map/while/body/eval_jaxpr/ppermute | solution.py:15
  495.0 16.1 %collective-permute-start.1 = (bf16[2,512,128]{2,1,0:T(8,128)(2,1)S(1)}, bf16[2,512,128]{2,1,0:T(8,128)(2,1)S(1)}, u32[]{:S(2)}, u32[]{:S(2)}) collective-permute-start(bf16[2,512,128]{2,1,0:T(8,128)(2,1)S(1)} %copy.59), channel_id=1, source_target_pairs={{240,0},{0,16},{16,32},{32,48},{48,64},{64,80},{80,96},{96,112},{1... | collective-permute-start | bytes 786440 | tf_op jit(solution)/shard_map/while/body/eval_jaxpr/ppermute | solution.py:15
  513.0 14.2 %collective-permute-start.2 = (f32[2,512,128]{2,1,0:T(8,128)S(1)}, f32[2,512,128]{2,1,0:T(8,128)S(1)}, u32[]{:S(2)}, u32[]{:S(2)}) collective-permute-start(f32[2,512,128]{2,1,0:T(8,128)S(1)} %get-tuple-element.818), channel_id=1, source_target_pairs={{240,0},{0,16},{16,32},{32,48},{48,64},{64,80},{80,96},{96,112},{1... | collective-permute-start | bytes 1572872 | tf_op jit(solution)/shard_map/while/body/eval_jaxpr/ppermute | solution.py:15
  517.7 15.2 %collective-permute-start.1 = (bf16[2,512,128]{2,1,0:T(8,128)(2,1)S(1)}, bf16[2,512,128]{2,1,0:T(8,128)(2,1)S(1)}, u32[]{:S(2)}, u32[]{:S(2)}) collective-permute-start(bf16[2,512,128]{2,1,0:T(8,128)(2,1)S(1)} %copy.59), channel_id=1, source_target_pairs={{240,0},{0,16},{16,32},{32,48},{48,64},{64,80},{80,96},{96,112},{1... | collective-permute-start | bytes 786440 | tf_op jit(solution)/shard_map/while/body/eval_jaxpr/ppermute | solution.py:15
  (21 other events, 395.7 us)
where the time goes:
time: 630 us; the launch traced here: 622 us
  waiting for transfers between devices  323 us (51%)
  blocking collectives  85.8 us (14%)
  starting transfers between devices  82.5 us (13%)
  other arithmetic  65.2 us (10%)
  matrix products  25.6 us (4%)
  loops' own time  20 us (3%)
  local copies, waits for them, and re-layouts  18.1 us (3%)
    ppermute x48, waiting for transfers between devices, passed_along(): return lax.ppermute(block, axis, route)  323 us
    psum x1, blocking collectives, on_device(): lax.psum((jnp.sum(dq_rows, axis=0), jnp.sum(grads[0], axis=0), jnp.sum(gr...  85.8 us
    ppermute x48, starting transfers between devices, passed_along(): return lax.ppermute(block, axis, route)  82.5 us
    reduce_sum x33, other arithmetic, pick_entry(): return jnp.sum(jnp.where(spots == index, vector, 0), axis=0)  41.8 us
    reduce_sum x16, other arithmetic, climb(): upward = jnp.sum(jnp.where(match, parent_row[None, :], 0), axis=1)  13.4 us
  transfers between devices with their start and end apart: 48, of which 46 were waited for; matrix products, arithmetic and copies ran while one was open for 5% of the time, Pallas kernels for 0%

commit v1 on v0

v1 whole, which is shorter than its diff:
```python
import functools

import jax
import jax.numpy as jnp
from jax import lax
from jax.experimental import pallas as pl
from jax.experimental.pallas import tpu as pltpu
from jax.sharding import PartitionSpec as P

HEAD_WIDTH = 128

NEGATIVE_FILL = -1e30


def tree_tables(parent_row, owner_row):
    count = parent_row.shape[0]
    tiles = jnp.arange(count, dtype=jnp.int32)
    tile_at = jnp.sum(jnp.where(owner_row[None, :] == tiles[:, None], tiles[None, :], 0), axis=1)

    def climb(step, state):
        reach, current = state
        match = current[:, None] == tiles[None, :]
        reach = jnp.logical_or(reach, match)
        upward = jnp.sum(jnp.where(match, parent_row[None, :], 0), axis=1)
        upward = jnp.where(current < 0, -1, upward)
        return (reach, upward)

    reach, _ = lax.fori_loop(0, count, climb, (jnp.zeros((count, count), bool), tiles))
    return tile_at, reach


def pick_entry(vector, index):
    spots = jnp.arange(vector.shape[0], dtype=jnp.int32)
    return jnp.sum(jnp.where(spots == index, vector, 0), axis=0)


def attention_grads_kernel(flags_ref, q_ref, g_ref, o_ref, k_ref, v_ref,
                           dq_ref, dk_ref, dv_ref, s_scr, *, slots, scale):
    head = pl.program_id(0)

    @pl.when(head == 0)
    def _():
        dk_ref[...] = jnp.zeros_like(dk_ref)
        dv_ref[...] = jnp.zeros_like(dv_ref)

    q = q_ref[...]
    g = g_ref[...]
    o = o_ref[...]
    rows = q.shape[0]
    delta = jnp.sum(g.astype(jnp.float32) * o.astype(jnp.float32), axis=1, keepdims=True)
    causal = (lax.broadcasted_iota(jnp.int32, (rows, rows), 0)
              >= lax.broadcasted_iota(jnp.int32, (rows, rows), 1))
    nt = (((1,), (1,)), ((), ()))
    tn = (((0,), (0,)), ((), ()))

    top = jnp.full((rows, 1), NEGATIVE_FILL, jnp.float32)
    for j in range(slots):
        keep = flags_ref[j] > 0
        if j == slots - 1:
            keep = jnp.logical_and(keep, causal)
        scores = lax.dot_general(q, k_ref[j], nt, preferred_element_type=jnp.float32) * scale
        scores = jnp.where(keep, scores, NEGATIVE_FILL)
        s_scr[j] = scores
        top = jnp.maximum(top, jnp.max(scores, axis=1, keepdims=True))

    total = jnp.zeros((rows, 1), jnp.float32)
    for j in range(slots):
        keep = flags_ref[j] > 0
        if j == slots - 1:
            keep = jnp.logical_and(keep, causal)
        probs = jnp.where(keep, jnp.exp(s_scr[j] - top), 0.0)
        s_scr[j] = probs
        total = total + jnp.sum(probs, axis=1, keepdims=True)
    inverse = jnp.where(total > 0, 1.0 / jnp.where(total > 0, total, 1.0), 0.0)

    dq = jnp.zeros((rows, q.shape[1]), jnp.float32)
    for j in range(slots):
        probs = s_scr[j] * inverse
        dv_ref[j] += lax.dot_general(probs.astype(jnp.bfloat16), g, tn,
                                     preferred_element_type=jnp.float32)
        dprobs = lax.dot_general(g, v_ref[j], nt, preferred_element_type=jnp.float32)
        dscores = (probs * (dprobs - delta)).astype(jnp.bfloat16)
        dq = dq + jnp.dot(dscores, k_ref[j], preferred_element_type=jnp.float32)
        dk_ref[j] += lax.dot_general(dscores, q, tn, preferred_element_type=jnp.float32) * scale
    dq_ref[...] = dq * scale


def attention_grads(flags, q, g, o, keys, values, scale):
    rows, wide = q.shape
    slots = keys.shape[0]
    heads = wide // HEAD_WIDTH
    col = pl.BlockSpec((rows, HEAD_WIDTH), lambda h, f: (0, h))
    whole = pl.BlockSpec((slots, rows, HEAD_WIDTH), lambda h, f: (0, 0, 0))
    return pl.pallas_call(
        functools.partial(attention_grads_kernel, slots=slots, scale=scale),
        grid_spec=pltpu.PrefetchScalarGridSpec(
            num_scalar_prefetch=1,
            grid=(heads,),
            in_specs=[col, col, col, whole, whole],
            out_specs=[col, whole, whole],
            scratch_shapes=[pltpu.VMEM((slots, rows, rows), jnp.float32)],
        ),
        out_shape=[
            jax.ShapeDtypeStruct((rows, wide), jnp.float32),
            jax.ShapeDtypeStruct((slots, rows, HEAD_WIDTH), jnp.float32),
            jax.ShapeDtypeStruct((slots, rows, HEAD_WIDTH), jnp.float32),
        ],
        compiler_params=pltpu.CompilerParams(
            dimension_semantics=("arbitrary",), vmem_limit_bytes=48 * 1024 * 1024
        ),
    )(flags, q, g, o, keys, values)


def on_device(query, key, value, output, output_gradient, parent, owner):
    count = lax.axis_size("ctx")
    me = lax.axis_index("ctx")
    tile = query.shape[1]
    width = key.shape[2]
    scale_factor = HEAD_WIDTH ** (-0.5)
    prompt_tiles = count // 8
    parent_row = parent[0]
    owner_row = owner[0]
    tile_at, reach = tree_tables(parent_row, owner_row)
    my_tile = pick_entry(tile_at, me)
    tiles = jnp.arange(count, dtype=jnp.int32)
    reach_row = jnp.sum(jnp.where((tiles == my_tile)[:, None], reach, False), axis=0) > 0
    trained = my_tile >= prompt_tiles
    above = pick_entry(parent_row, my_tile)
    second = above >= prompt_tiles
    slot_tiles = jnp.stack(
        [jnp.int32(0), jnp.int32(1), jnp.where(second, above, 1).astype(jnp.int32)]
    )
    slot_blocks = jnp.sum(
        jnp.where(slot_tiles[:, None] == tiles[None, :], owner_row[None, :], 0), axis=1
    ).astype(jnp.int32)
    slot_seen = jnp.sum(
        jnp.where(slot_tiles[:, None] == tiles[None, :], reach_row[None, :], False), axis=1
    ) > 0
    slot_new = jnp.stack([True, slot_tiles[1] != slot_tiles[0], second])
    slot_keep = jnp.logical_and(jnp.logical_and(slot_seen, slot_new), trained)
    flags = jnp.concatenate([slot_keep, trained[None]]).astype(jnp.int32)

    pair = jnp.concatenate([key[0], value[0]], axis=1)
    gathered = lax.all_gather(pair, "ctx")
    picked = gathered[slot_blocks]
    keys = jnp.concatenate([picked[:, :, :width], key[0][None]], axis=0)
    values = jnp.concatenate([picked[:, :, width:], value[0][None]], axis=0)

    dq, dk, dv = attention_grads(
        flags, query[0], output_gradient[0], output[0], keys, values, scale_factor
    )
    partial = jnp.concatenate([dk, dv], axis=2)
    targets = jnp.concatenate([slot_blocks, me[None].astype(jnp.int32)])
    spread = jnp.zeros((count, tile, 2 * width), jnp.float32).at[targets].add(partial)
    grads = lax.psum_scatter(spread, "ctx", scatter_dimension=0, tiled=True)[0]

    total_rows = lax.axis_size("dp") * query.shape[0] * count * tile
    norm = total_rows ** (-0.5)
    sum_q, sum_k, sum_v = lax.psum(
        (jnp.sum(dq, axis=0), jnp.sum(grads[:, :width], axis=0), jnp.sum(grads[:, width:], axis=0)),
        ("ctx", "dp"),
    )
    return (
        dq.astype(jnp.bfloat16)[None],
        grads[:, :width].astype(jnp.bfloat16)[None],
        grads[:, width:].astype(jnp.bfloat16)[None],
        sum_q * norm,
        sum_k * norm,
        sum_v * norm,
    )


def solution(mesh):
    return jax.shard_map(
        on_device,
        mesh=mesh,
        in_specs=(
            P("dp", "ctx", "head"),
            P("dp", "ctx", "head"),
            P("dp", "ctx", "head"),
            P("dp", "ctx", "head"),
            P("dp", "ctx", "head"),
            P("dp", None),
            P("dp", None),
        ),
        out_specs=(
            P("dp", "ctx", "head"),
            P("dp", "ctx", "head"),
            P("dp", "ctx", "head"),
            P("head"),
            P("head"),
            P("head"),
        ),
        check_vma=False,
    )
```

time: 630 us -> 447 us (0.71)
  starting transfers between devices: 82.5 us -> 0.08 us
  other arithmetic: 65.2 us -> 30.1 us
  waiting for transfers between devices: 323 us -> 294 us
  matrix products: 25.6 us -> 0 us
  Pallas kernels: 0 us -> 21.8 us
  loops' own time: 20 us -> 0.22 us
  blocking collectives: 85.8 us -> 67.3 us
  between operations: 1.43 us -> 16.1 us
  local copies, waits for them, and re-layouts: 18.1 us -> 11.3 us
    ppermute x48 -> x0, waiting for transfers between devices: 323 us -> none  [passed_along(): return lax.ppermute(block, axis, route)]
    reduce_scatter x0 -> x1, waiting for transfers between devices: none -> 217 us  [on_device(): grads = lax.psum_scatter(spread, 'ctx', scatter_dimension=0, tiled=True)[0]]
    ppermute x48 -> x0, starting transfers between devices: 82.5 us -> none  [passed_along(): return lax.ppermute(block, axis, route)]
    all_gather x0 -> x1, waiting for transfers between devices: none -> 77.1 us  [on_device(): gathered = lax.all_gather(pair, 'ctx')]
    reduce_sum x33 -> x2, other arithmetic: 41.8 us -> 2.58 us  [pick_entry(): return jnp.sum(jnp.where(spots == index, vector, 0), axis=0)]
    dot_general x20 -> x0, matrix products: 25.6 us -> none  [the longest x6 8.31 us: block_scores(): jnp.einsum('ignd,jgd->gnij', query4, keys3, preferred_element_type=jnp.fl...]
    pallas_call x0 -> x1, Pallas kernels: none -> 21.8 us  [attention_grads(): pl.pallas_call(functools.partial(attention_grads_kernel, slots=slots, sca...]
    another operation x34 -> x0, loops' own time: 19.7 us -> none  [the longest x1 9.63 us: on_device(): lax.fori_loop(0, count, grad_step, (kv_pair, partial_start, dq_start))]
  transfers between devices with their start and end apart: 48 -> 2, of which waited for: 46 -> 2; matrix products, arithmetic and copies ran while one was open for 5% -> 5% of each run, Pallas kernels for 0% -> 0%
where the time goes in v1:
time: 447 us; the launch traced here: 441 us
  waiting for transfers between devices  294 us (66%)
  blocking collectives  67.3 us (15%)
  other arithmetic  30.1 us (7%)
  Pallas kernels  21.8 us (5%)
  between operations  16.1 us (4%)
  local copies, waits for them, and re-layouts  11.3 us (3%)
    reduce_scatter x1, waiting for transfers between devices, on_device(): grads = lax.psum_scatter(spread, 'ctx', scatter_dimension=0, tiled=True)[0]  217 us
    all_gather x1, waiting for transfers between devices, on_device(): gathered = lax.all_gather(pair, 'ctx')  77.1 us
    psum x1, blocking collectives, on_device(): lax.psum((jnp.sum(dq, axis=0), jnp.sum(grads[:, :width], axis=0), jnp.sum...  67.3 us
    pallas_call x1, Pallas kernels, attention_grads(): pl.pallas_call(functools.partial(attention_grads_kernel, slots=slots, sca...  21.8 us
    reduce_sum x16, other arithmetic, climb(): upward = jnp.sum(jnp.where(match, parent_row[None, :], 0), axis=1)  13.4 us
  transfers between devices with their start and end apart: 2, of which 2 were waited for; matrix products, arithmetic and copies ran while one was open for 5% of the time, Pallas kernels for 0%

profile of v1, /device:TPU:13, one launch (start us, length us, event | category | flops | bytes accessed | tf_op | source)
XLA Modules:
  0.0 440.6 jit_solution(11221029987007587267)
XLA Ops:
  7.2 1.7 pad_maximum_fusion.3
  11.1 1.9 fusion.11
  15.1 15.1 %while.13 = (s32[]{:T(128)}, pred[16,16]{1,0:T(8,128)(4,1)S(1)}, s32[16]{0:T(128)S(1)}, s32[1,16]{1,0:T(1,128)}, s32[]{:T(128)}, /*index=5*/s32[]{:T(128)}) while((s32[]{:T(128)}, pred[16,16]{1,0:T(8,128)(4,1)S(1)}, s32[16]{0:T(128)S(1)}, s32[1,16]{1,0:T(1,128)}, s32[]{:T(128)}, /*index=5*/s32[]{:T(128)}) %tuple.32), condition=%wide.region_5.6_spmd.clone, body=%wide.region_3.5_spmd.clone.sunk | while | flops 1555 | bytes 1039 | solution.py:28
  15.1 0.8 fusion.17
  16.0 0.8 fusion.17
  17.0 0.8 fusion.17
  17.9 0.8 fusion.17
  18.9 0.8 fusion.17
  19.8 0.8 fusion.17
  20.8 0.8 fusion.17
  21.7 0.8 fusion.17
  22.7 0.8 fusion.17
  23.6 0.8 fusion.17
  24.5 0.8 fusion.17
  25.5 0.8 fusion.17
  26.4 0.8 fusion.17
  27.4 0.8 fusion.17
  28.3 0.8 fusion.17
  29.3 0.8 fusion.17
  30.3 0.9 select_reduce_fusion.1
  31.4 77.1 %all-gather.3.cloned.1.call-done = bf16[8192,256]{1,0:T(8,128)(2,1)} async-done(((bf16[512,256]{1,0:T(8,128)(2,1)}), bf16[8192,256]{1,0:T(8,128)(2,1)}) %all-gather.3.cloned.1.call-update) | async-done | bytes 4194320 | tf_op jit(solution)/shard_map/all_gather | solution.py:144
  108.6 2.8 gather_fusion
  111.7 0.8 copy-done
  112.8 21.8 %shard_map.118 = (f32[512,640]{1,0:T(8,128)}, f32[4,512,128]{2,1,0:T(8,128)S(1)}, f32[4,512,128]{2,1,0:T(8,128)S(1)}) custom-call(s32[4]{0:T(128)S(1)} %add_convert_fusion.flags_ref, bf16[512,640]{1,0:T(8,128)(2,1)S(1)} %bitcast.31, bf16[512,640]{1,0:T(8,128)(2,1)S(1)} %bitcast.32, bf16[512,640]{1,0:T(8,128)(2,1)S(1)} %bitcast.33, ...), custom_call_target="tpu_custom_call" | custom-call | tf_op jit(solution)/shard_map/pallas_call | solution.py:94
  134.8 4.1 broadcast_in_dim.107
  138.9 4.3 scatter_fusion
  143.2 1.3 copy-done.3
  144.5 0.9 fusion.12
  145.4 216.5 %reduce-scatter.2.cloned.1.call-done = f32[1,512,256]{2,1,0:T(8,128)} async-done(((f32[16,512,256]{2,1,0:T(8,128)}), f32[1,512,256]{2,1,0:T(8,128)}) %reduce-scatter.2.cloned.1.call-update) | async-done | bytes 524304 | tf_op jit(solution)/shard_map/reduce_scatter | solution.py:155
  362.0 1.1 slice_reduce_fusion
  363.1 1.8 fusion.6
  364.8 67.3 %all-reduce.1 = (f32[640]{0:T(1024)S(1)}, f32[128]{0:T(128)S(1)}, f32[128]{0:T(128)S(1)}) all-reduce(f32[640]{0:T(1024)S(1)} %get-tuple-element.72, f32[128]{0:T(128)S(1)} %get-tuple-element.58, f32[128]{0:T(128)S(1)} %get-tuple-element.57), channel_id=1, replica_groups=mesh['ctx'=16,'head'=8,'dp'=2] {'ctx','dp'}, use_global_device_ids=true, to_apply=%region_12.13 | all-reduce | flops 896 | bytes 7168 | tf_op jit(solution)/shard_map/psum | solution.py:159
  (65 shorter events, 6.5 us)
Async XLA Ops:
  7.2 101.4 %all-gather.3.cloned.1.call-start = ((), (), s32[]{:S(2)}) async-start(), calls=%async_computation.2 | async-start | bytes 4456448 | tf_op jit(solution)/shard_map/all_gather | solution.py:144
  7.2 104.3 %copy-start.4 = (bf16[1,512,128]{2,1,0:T(8,128)(2,1)S(1)}, bf16[1,512,128]{2,1,0:T(8,128)(2,1)}, u32[]{:S(2)}) copy-start(bf16[1,512,128]{2,1,0:T(8,128)(2,1)} %param.10) | copy-start | bytes 393220
  7.2 104.3 %copy-start.5 = (bf16[1,512,128]{2,1,0:T(8,128)(2,1)S(1)}, bf16[1,512,128]{2,1,0:T(8,128)(2,1)}, u32[]{:S(2)}) copy-start(bf16[1,512,128]{2,1,0:T(8,128)(2,1)} %param.11) | copy-start | bytes 393220
  9.0 353.0 %reduce-scatter.2.cloned.1.call-start = ((), (), s32[]{:S(2)}) async-start(), calls=%async_computation.1 | async-start | bytes 8912896 | tf_op jit(solution)/shard_map/reduce_scatter | solution.py:155
  111.4 1.1 copy-start
  111.4 1.3 copy-start.1
  111.4 1.5 copy-start.2
  143.2 1.3 copy-start.3
Sparse Core Ops, SparseCore 0:
  11.2 97.3 all-gather.2
  143.3 218.5 reduce-scatter.1

commit v2 on v1

--- a/solution.py
+++ b/solution.py
@@ -12,26 +12,14 @@
 NEGATIVE_FILL = -1e30
 
 
-def tree_tables(parent_row, owner_row):
-    count = parent_row.shape[0]
-    tiles = jnp.arange(count, dtype=jnp.int32)
-    tile_at = jnp.sum(jnp.where(owner_row[None, :] == tiles[:, None], tiles[None, :], 0), axis=1)
-
-    def climb(step, state):
-        reach, current = state
-        match = current[:, None] == tiles[None, :]
-        reach = jnp.logical_or(reach, match)
-        upward = jnp.sum(jnp.where(match, parent_row[None, :], 0), axis=1)
-        upward = jnp.where(current < 0, -1, upward)
-        return (reach, upward)
-
-    reach, _ = lax.fori_loop(0, count, climb, (jnp.zeros((count, count), bool), tiles))
-    return tile_at, reach
-
-
 def pick_entry(vector, index):
     spots = jnp.arange(vector.shape[0], dtype=jnp.int32)
     return jnp.sum(jnp.where(spots == index, vector, 0), axis=0)
+
+
+def pick_rows(matrix, index):
+    spots = jnp.arange(matrix.shape[0], dtype=jnp.int32)
+    return jnp.sum(jnp.where((spots == index)[:, None], matrix, 0.0), axis=0)
 
 
 def attention_grads_kernel(flags_ref, q_ref, g_ref, o_ref, k_ref, v_ref,
@@ -120,25 +108,18 @@
     prompt_tiles = count // 8
     parent_row = parent[0]
     owner_row = owner[0]
-    tile_at, reach = tree_tables(parent_row, owner_row)
-    my_tile = pick_entry(tile_at, me)
     tiles = jnp.arange(count, dtype=jnp.int32)
-    reach_row = jnp.sum(jnp.where((tiles == my_tile)[:, None], reach, False), axis=0) > 0
+    my_tile = jnp.sum(jnp.where(owner_row == me, tiles, 0))
     trained = my_tile >= prompt_tiles
     above = pick_entry(parent_row, my_tile)
-    second = above >= prompt_tiles
+    second = jnp.logical_and(trained, above >= prompt_tiles)
     slot_tiles = jnp.stack(
         [jnp.int32(0), jnp.int32(1), jnp.where(second, above, 1).astype(jnp.int32)]
     )
     slot_blocks = jnp.sum(
         jnp.where(slot_tiles[:, None] == tiles[None, :], owner_row[None, :], 0), axis=1
     ).astype(jnp.int32)
-    slot_seen = jnp.sum(
-        jnp.where(slot_tiles[:, None] == tiles[None, :], reach_row[None, :], False), axis=1
-    ) > 0
-    slot_new = jnp.stack([True, slot_tiles[1] != slot_tiles[0], second])
-    slot_keep = jnp.logical_and(jnp.logical_and(slot_seen, slot_new), trained)
-    flags = jnp.concatenate([slot_keep, trained[None]]).astype(jnp.int32)
+    flags = jnp.stack([trained, trained, second, trained]).astype(jnp.int32)
 
     pair = jnp.concatenate([key[0], value[0]], axis=1)
     gathered = lax.all_gather(pair, "ctx")
@@ -156,17 +137,22 @@
 
     total_rows = lax.axis_size("dp") * query.shape[0] * count * tile
     norm = total_rows ** (-0.5)
-    sum_q, sum_k, sum_v = lax.psum(
-        (jnp.sum(dq, axis=0), jnp.sum(grads[:, :width], axis=0), jnp.sum(grads[:, width:], axis=0)),
-        ("ctx", "dp"),
+    sums = jnp.concatenate(
+        [jnp.sum(dq, axis=0), jnp.sum(grads[:, :width], axis=0), jnp.sum(grads[:, width:], axis=0)]
     )
+    groups = lax.axis_size("head")
+    slots = jnp.zeros((groups, sums.shape[0]), jnp.float32).at[lax.axis_index("head")].set(sums)
+    slots = lax.psum(slots, ("ctx", "head", "dp"))
+    sums = pick_rows(slots, lax.axis_index("head")) * norm
+    wide = query.shape[2]
+    sum_q, sum_k, sum_v = sums[:wide], sums[wide:wide + width], sums[wide + width:]
     return (
         dq.astype(jnp.bfloat16)[None],
         grads[:, :width].astype(jnp.bfloat16)[None],
         grads[:, width:].astype(jnp.bfloat16)[None],
-        sum_q * norm,
-        sum_k * norm,
-        sum_v * norm,
+        sum_q,
+        sum_k,
+        sum_v,
     )
 
 

time: 447 us -> 457 us (1.022)
  other arithmetic: 30.1 us -> 13.9 us
  waiting for transfers between devices: 294 us -> 310 us
  blocking collectives: 67.3 us -> 78.2 us
    all_gather x1, waiting for transfers between devices: 77.1 us -> 93.1 us  [on_device(): gathered = lax.all_gather(pair, 'ctx')]
    reduce_sum x19 -> x3, other arithmetic: 15.4 us -> 2.49 us  [the longest x1 1.29 us: on_device(): my_tile = jnp.sum(jnp.where(owner_row == me, tiles, 0))]
    psum x1, blocking collectives: 67.3 us -> 78.2 us  [on_device(): slots = lax.psum(slots, ('ctx', 'head', 'dp'))]
  transfers between devices with their start and end apart: 2 -> 2, of which waited for: 2 -> 2; matrix products, arithmetic and copies ran while one was open for 5% -> 1% of each run, Pallas kernels for 0% -> 0%
where the time goes in v2:
time: 457 us; the launch traced here: 452 us
  waiting for transfers between devices  310 us (68%)
  blocking collectives  78.2 us (17%)
  Pallas kernels  21.8 us (5%)
  between operations  16.2 us (4%)
  other arithmetic  13.9 us (3%)
  local copies, waits for them, and re-layouts  11.3 us (2%)
    reduce_scatter x1, waiting for transfers between devices, on_device(): grads = lax.psum_scatter(spread, 'ctx', scatter_dimension=0, tiled=True)[0]  217 us
    all_gather x1, waiting for transfers between devices, on_device(): gathered = lax.all_gather(pair, 'ctx')  93.1 us
    psum x1, blocking collectives, on_device(): slots = lax.psum(slots, ('ctx', 'head', 'dp'))  78.2 us
    pallas_call x1, Pallas kernels, attention_grads(): pl.pallas_call(functools.partial(attention_grads_kernel, slots=slots, sca...  21.8 us
  transfers between devices with their start and end apart: 2, of which 2 were waited for; matrix products, arithmetic and copies ran while one was open for 1% of the time, Pallas kernels for 0%

profile of v2, /device:TPU:13, one launch (start us, length us, event | category | flops | bytes accessed | tf_op | source)
XLA Modules:
  0.0 451.9 jit_solution(7610718985570309139)
XLA Ops:
  7.2 0.0 all-gather.3.cloned.1.call-start
  7.2 1.8 pad_maximum_fusion.3
  9.0 0.0 reduce-scatter.2.cloned.1.call-start
  9.1 1.3 fusion.2
  11.0 1.9 fusion.3
  14.3 0.1 add_convert_fusion.flags_ref
  14.3 0.1 pad_add_fusion
  14.4 0.8 select_reduce_fusion.1
  15.3 0.1 fusion.5
  15.3 93.1 %all-gather.3.cloned.1.call-done = bf16[8192,256]{1,0:T(8,128)(2,1)} async-done(((bf16[512,256]{1,0:T(8,128)(2,1)}), bf16[8192,256]{1,0:T(8,128)(2,1)}) %all-gather.3.cloned.1.call-update) | async-done | bytes 4194320 | tf_op jit(solution)/shard_map/all_gather | solution.py:125
  108.4 2.8 gather_fusion
  111.2 0.1 fusion.7
  111.4 0.1 pad_maximum_fusion.1
  111.5 0.8 copy-done
  112.3 0.2 copy-done.1
  112.5 0.2 copy-done.2
  112.7 21.8 %shard_map.118 = (f32[512,640]{1,0:T(8,128)}, f32[4,512,128]{2,1,0:T(8,128)S(1)}, f32[4,512,128]{2,1,0:T(8,128)S(1)}) custom-call(s32[4]{0:T(128)S(1)} %add_convert_fusion.flags_ref, bf16[512,640]{1,0:T(8,128)(2,1)S(1)} %bitcast.31, bf16[512,640]{1,0:T(8,128)(2,1)S(1)} %bitcast.32, bf16[512,640]{1,0:T(8,128)(2,1)S(1)} %bitcast.33, ...), custom_call_target="tpu_custom_call" | custom-call | tf_op jit(solution)/shard_map/pallas_call | solution.py:82
  134.5 0.1 pad_maximum_fusion
  134.7 4.1 broadcast_in_dim.53
  138.8 4.1 scatter_fusion
  142.9 0.6 copy-done.7
  143.5 0.7 and_reduce_fusion
  144.2 0.9 fusion.6
  145.2 217.4 %reduce-scatter.2.cloned.1.call-done = f32[1,512,256]{2,1,0:T(8,128)} async-done(((f32[16,512,256]{2,1,0:T(8,128)}), f32[1,512,256]{2,1,0:T(8,128)}) %reduce-scatter.2.cloned.1.call-update) | async-done | bytes 524304 | tf_op jit(solution)/shard_map/reduce_scatter | solution.py:136
  362.6 1.8 fusion.1
  364.3 1.1 slice_reduce_fusion.1
  365.4 0.7 broadcast_select_fusion
  366.1 0.1 scatter.4
  366.2 78.2 %psum.7 = f32[8,896]{1,0:T(8,128)S(1)} all-reduce(f32[8,896]{1,0:T(8,128)S(1)} %scatter.4), channel_id=1, replica_groups=mesh['ctx'=16,'head'=8,'dp'=2] {'ctx','head','dp'}, use_global_device_ids=true, to_apply=%region_9.10 | all-reduce | flops 7168 | bytes 57344 | tf_op jit(solution)/shard_map/psum | solution.py:145
  444.4 0.1 select_reduce_fusion
  444.5 0.5 fusion.8
  445.0 0.1 copy-done.6
  (19 shorter events, 0.1 us)
Async XLA Ops:
  7.2 104.2 %copy-start.5 = (bf16[1,512,128]{2,1,0:T(8,128)(2,1)S(1)}, bf16[1,512,128]{2,1,0:T(8,128)(2,1)}, u32[]{:S(2)}) copy-start(bf16[1,512,128]{2,1,0:T(8,128)(2,1)} %param.11) | copy-start | bytes 393220
  7.2 104.2 %copy-start.4 = (bf16[1,512,128]{2,1,0:T(8,128)(2,1)S(1)}, bf16[1,512,128]{2,1,0:T(8,128)(2,1)}, u32[]{:S(2)}) copy-start(bf16[1,512,128]{2,1,0:T(8,128)(2,1)} %param.10) | copy-start | bytes 393220
  7.2 101.2 %all-gather.3.cloned.1.call-start = ((), (), s32[]{:S(2)}) async-start(), calls=%async_computation.2 | async-start | bytes 4456448 | tf_op jit(solution)/shard_map/all_gather | solution.py:125
  9.0 353.5 %reduce-scatter.2.cloned.1.call-start = ((), (), s32[]{:S(2)}) async-start(), calls=%async_computation.1 | async-start | bytes 8912896 | tf_op jit(solution)/shard_map/reduce_scatter | solution.py:136
  111.2 1.1 copy-start
  111.2 1.3 copy-start.1
  111.2 1.5 copy-start.2
  142.9 0.7 copy-start.7
  142.9 1.4 copy-start.3
  444.5 0.6 copy-start.6
Sparse Core Ops, SparseCore 0:
  11.2 97.1 all-gather.2
  143.0 219.4 reduce-scatter.1

commit v3 on v2

--- a/solution.py
+++ b/solution.py
@@ -97,6 +97,54 @@
             dimension_semantics=("arbitrary",), vmem_limit_bytes=48 * 1024 * 1024
         ),
     )(flags, q, g, o, keys, values)
+
+
+def exchange_kernel(x_ref, out_ref, send_sem, recv_sem, self_sem, *, axis, n, indexed):
+    me = lax.axis_index(axis)
+    barrier = pltpu.get_barrier_semaphore()
+    for d in range(1, n):
+        pl.semaphore_signal(
+            barrier, inc=1, device_id={axis: lax.rem(me + d, n)},
+            device_id_type=pl.DeviceIdType.MESH,
+        )
+    pl.semaphore_wait(barrier, n - 1)
+    copies = []
+    for d in range(1, n):
+        peer = lax.rem(me + d, n)
+        copy = pltpu.make_async_remote_copy(
+            src_ref=x_ref.at[peer] if indexed else x_ref,
+            dst_ref=out_ref.at[me],
+            send_sem=send_sem.at[d - 1],
+            recv_sem=recv_sem.at[d - 1],
+            device_id={axis: peer},
+            device_id_type=pl.DeviceIdType.MESH,
+        )
+        copy.start()
+        copies.append(copy)
+    local = pltpu.make_async_copy(x_ref.at[me] if indexed else x_ref, out_ref.at[me], self_sem)
+    local.start()
+    for copy in copies:
+        copy.wait_send()
+    for copy in copies:
+        copy.wait_recv()
+    local.wait()
+
+
+def exchange(x, axis, indexed, collective_id):
+    n = lax.axis_size(axis)
+    piece = x.shape[1:] if indexed else x.shape
+    return pl.pallas_call(
+        functools.partial(exchange_kernel, axis=axis, n=n, indexed=indexed),
+        out_shape=jax.ShapeDtypeStruct((n,) + tuple(piece), x.dtype),
+        in_specs=[pl.BlockSpec(memory_space=pl.ANY)],
+        out_specs=pl.BlockSpec(memory_space=pl.ANY),
+        scratch_shapes=[
+            pltpu.SemaphoreType.DMA((n - 1,)),
+            pltpu.SemaphoreType.DMA((n - 1,)),
+            pltpu.SemaphoreType.DMA,
+        ],
+        compiler_params=pltpu.CompilerParams(collective_id=collective_id, has_side_effects=True),
+    )(x)
 
 
 def on_device(query, key, value, output, output_gradient, parent, owner):
@@ -122,7 +170,7 @@
     flags = jnp.stack([trained, trained, second, trained]).astype(jnp.int32)
 
     pair = jnp.concatenate([key[0], value[0]], axis=1)
-    gathered = lax.all_gather(pair, "ctx")
+    gathered = exchange(pair, "ctx", False, 0)
     picked = gathered[slot_blocks]
     keys = jnp.concatenate([picked[:, :, :width], key[0][None]], axis=0)
     values = jnp.concatenate([picked[:, :, width:], value[0][None]], axis=0)
@@ -132,20 +180,28 @@
     )
     partial = jnp.concatenate([dk, dv], axis=2)
     targets = jnp.concatenate([slot_blocks, me[None].astype(jnp.int32)])
-    spread = jnp.zeros((count, tile, 2 * width), jnp.float32).at[targets].add(partial)
-    grads = lax.psum_scatter(spread, "ctx", scatter_dimension=0, tiled=True)[0]
-
     total_rows = lax.axis_size("dp") * query.shape[0] * count * tile
     norm = total_rows ** (-0.5)
-    sums = jnp.concatenate(
-        [jnp.sum(dq, axis=0), jnp.sum(grads[:, :width], axis=0), jnp.sum(grads[:, width:], axis=0)]
-    )
-    groups = lax.axis_size("head")
-    slots = jnp.zeros((groups, sums.shape[0]), jnp.float32).at[lax.axis_index("head")].set(sums)
-    slots = lax.psum(slots, ("ctx", "head", "dp"))
-    sums = pick_rows(slots, lax.axis_index("head")) * norm
     wide = query.shape[2]
-    sum_q, sum_k, sum_v = sums[:wide], sums[wide:wide + width], sums[wide + width:]
+    dq_sum = jnp.sum(dq, axis=0)
+    kv_sum = jnp.sum(partial, axis=(0, 1))
+    tail_width = 2 * width
+    tail_rows = 8
+    tail = jnp.concatenate(
+        [dq_sum, kv_sum, jnp.zeros((tail_rows * tail_width - wide - tail_width,), jnp.float32)]
+    ).reshape(tail_rows, tail_width)
+    spread = jnp.zeros((count, tile, tail_width), jnp.float32).at[targets].add(partial)
+    spread = jnp.concatenate([spread, jnp.broadcast_to(tail, (count, tail_rows, tail_width))], axis=1)
+    landed = exchange(spread, "ctx", True, 1)
+    summed = landed[0]
+    for peer in range(1, count):
+        summed = summed + landed[peer]
+    grads = summed[:tile]
+    both = exchange(summed[tile:], "dp", False, 2)
+    sums = (both[0] + both[1]).reshape(-1) * norm
+    sum_q = sums[:wide]
+    sum_k = sums[wide:wide + width]
+    sum_v = sums[wide + width:wide + 2 * width]
     return (
         dq.astype(jnp.bfloat16)[None],
         grads[:, :width].astype(jnp.bfloat16)[None],

time: 457 us -> 370 us (0.81); the launches traced: 452 us -> 370 us
  Pallas kernels: 21.8 us -> 332 us
  waiting for transfers between devices: 310 us -> 0 us
  blocking collectives: 78.2 us -> 0 us
  between operations: 16.2 us -> 2.74 us
  other arithmetic: 13.9 us -> 25.5 us
    pallas_call x0 -> x3, Pallas kernels: none -> 310 us  [exchange(): pl.pallas_call(functools.partial(exchange_kernel, axis=axis, n=n, indexed...]
    reduce_scatter x1 -> x0, waiting for transfers between devices: 217 us -> none  [on_device(): grads = lax.psum_scatter(spread, 'ctx', scatter_dimension=0, tiled=True)[0]]
    all_gather x1 -> x0, waiting for transfers between devices: 93.1 us -> none  [on_device(): gathered = lax.all_gather(pair, 'ctx')]
    psum x1 -> x0, blocking collectives: 78.2 us -> none  [on_device(): slots = lax.psum(slots, ('ctx', 'head', 'dp'))]
    concatenate x1 -> x2, other arithmetic: 0.14 us -> 7.55 us  [the longest x1 7.54 us: on_device(): jnp.concatenate([spread, jnp.broadcast_to(tail, (count, tail_rows, tail_w...]
  transfers between devices with their start and end apart: 2 -> 0, of which waited for: 2 -> 0; matrix products, arithmetic and copies ran while one was open for 1% -> 0% of each run, Pallas kernels for 0% -> 0%
where the time goes in v3:
time: 370 us
  Pallas kernels  332 us (90%)
  other arithmetic  25.5 us (7%)
  local copies, waits for them, and re-layouts  9.65 us (3%)
    pallas_call x3, Pallas kernels, exchange(): pl.pallas_call(functools.partial(exchange_kernel, axis=axis, n=n, indexed...  310 us
    pallas_call x1, Pallas kernels, attention_grads(): pl.pallas_call(functools.partial(attention_grads_kernel, slots=slots, sca...  21.9 us
    concatenate x1, other arithmetic, on_device(): jnp.concatenate([spread, jnp.broadcast_to(tail, (count, tail_rows, tail_w...  7.54 us

profile of v3, /device:TPU:13, one launch (start us, length us, event | category | flops | bytes accessed | tf_op | source)
XLA Modules:
  0.0 369.7 jit_solution(15958730170393407209)
XLA Ops:
  0.6 0.0 copy-start.4
  0.6 0.0 copy-start.3
  0.7 1.3 fusion
  2.6 1.9 fusion.1
  5.9 0.1 add_convert_fusion.flags_ref
  6.0 0.1 pad_add_fusion
  6.0 0.8 select_reduce_fusion
  6.9 0.1 fusion.3
  7.0 1.7 pad_maximum_fusion.3.x_ref
  8.7 101.5 %shard_map.118 = bf16[16,512,256]{2,1,0:T(8,128)(2,1)} custom-call(bf16[512,256]{1,0:T(8,128)(2,1)} %pad_maximum_fusion.3.x_ref), custom_call_target="tpu_custom_call" | custom-call | tf_op jit(solution)/shard_map/pallas_call | solution.py:136
  110.2 2.8 gather_fusion
  113.0 0.1 fusion.5
  113.1 0.0 copy-done.4
  113.1 0.0 copy-done.3
  113.1 0.1 pad_maximum_fusion.1
  113.2 0.0 copy-done
  113.3 21.9 %shard_map.119 = (f32[512,640]{1,0:T(8,128)}, f32[4,512,128]{2,1,0:T(8,128)S(1)}, f32[4,512,128]{2,1,0:T(8,128)S(1)}) custom-call(s32[4]{0:T(128)S(1)} %add_convert_fusion.flags_ref, bf16[512,640]{1,0:T(8,128)(2,1)S(1)} %bitcast.32, bf16[512,640]{1,0:T(8,128)(2,1)S(1)} %bitcast.33, bf16[512,640]{1,0:T(8,128)(2,1)S(1)} %bitcast.34, ...), custom_call_target="tpu_custom_call" | custom-call | tf_op jit(solution)/shard_map/pallas_call | solution.py:82
  135.1 2.7 fusion.4
  137.8 0.1 constant_dynamic-update-slice_fusion.1
  137.9 0.1 constant_dynamic-update-slice_fusion
  138.0 0.3 reduce_sum.52
  138.3 4.1 %broadcast_in_dim.44 = f32[16,512,256]{2,1,0:T(8,128)} broadcast(f32[]{:T(128)} %constant.6.clone.1), dimensions={} | broadcast | bytes 8388612 | tf_op jit(solution)/shard_map/broadcast_in_dim | solution.py:193
  142.4 4.2 %scatter_fusion = f32[16,512,256]{2,1,0:T(8,128)} fusion(f32[16,512,256]{2,1,0:T(8,128)} %broadcast_in_dim.44, s32[4]{0:T(128)S(1)} %fusion.3, f32[4,512,256]{2,1,0:T(8,128)S(1)} %constant_dynamic-update-slice_fusion), kind=kCustom, calls=%fused_computation.1 | custom fusion | flops 524288 | bytes 6291472 | tf_op jit(solution)/shard_map/scatter-add | solution.py:193
  146.6 7.5 %pad_maximum_fusion.x_ref = f32[16,520,256]{2,1,0:T(8,128)} fusion(f32[16,8,256]{2,1,0:T(8,128)S(1)} %broadcast_in_dim.46, f32[16,512,256]{2,1,0:T(8,128)} %scatter_fusion), kind=kLoop, calls=%fused_computation.2 | loop fusion | flops 2129920 | bytes 17039360 | tf_op jit(solution)/shard_map/concatenate | solution.py:194
  154.1 204.6 %shard_map.120 = f32[16,520,256]{2,1,0:T(8,128)} custom-call(f32[16,520,256]{2,1,0:T(8,128)} %pad_maximum_fusion.x_ref), custom_call_target="tpu_custom_call" | custom-call | tf_op jit(solution)/shard_map/pallas_call | solution.py:136
  358.8 4.0 %convert_bitcast_fusion.1 = (bf16[520,256]{1,0:T(8,128)(2,1)S(1)}, f32[1,520,256]{2,1,0:T(8,128)S(1)}) fusion(f32[16,520,256]{2,1,0:T(8,128)} %shard_map.120), kind=kLoop, calls=%fused_computation.7 | loop fusion | flops 2129920 | bytes 9318400 | tf_op jit(solution)/shard_map/convert.1
  362.7 0.7 slice_bitcast_fusion
  363.4 0.6 slice_bitcast_fusion.2.x_ref
  364.0 3.8 %shard_map.121 = f32[2,8,256]{2,1,0:T(8,128)} custom-call(f32[8,256]{1,0:T(8,128)} %slice_bitcast_fusion.2.x_ref), custom_call_target="tpu_custom_call" | custom-call | tf_op jit(solution)/shard_map/pallas_call | solution.py:136
  367.9 0.7 multiply_bitcast_fusion
  368.6 0.5 fusion.6
  369.1 0.6 slice.117
  (12 shorter events, 0.1 us)
Async XLA Ops:
  0.6 112.5 %copy-start.4 = (bf16[1,512,128]{2,1,0:T(8,128)(2,1)S(1)}, bf16[1,512,128]{2,1,0:T(8,128)(2,1)}, u32[]{:S(2)}) copy-start(bf16[1,512,128]{2,1,0:T(8,128)(2,1)} %param.9) | copy-start | bytes 393220
  0.6 112.5 %copy-start.3 = (bf16[1,512,128]{2,1,0:T(8,128)(2,1)S(1)}, bf16[1,512,128]{2,1,0:T(8,128)(2,1)}, u32[]{:S(2)}) copy-start(bf16[1,512,128]{2,1,0:T(8,128)(2,1)} %param.8) | copy-start | bytes 393220
  8.7 104.6 %copy-start = (bf16[1,512,640]{2,1,0:T(8,128)(2,1)S(1)}, bf16[1,512,640]{2,1,0:T(8,128)(2,1)}, u32[]{:S(2)}) copy-start(bf16[1,512,640]{2,1,0:T(8,128)(2,1)} %param.7) | copy-start | bytes 1966084
  8.7 104.6 %copy-start.1 = (bf16[1,512,640]{2,1,0:T(8,128)(2,1)S(1)}, bf16[1,512,640]{2,1,0:T(8,128)(2,1)}, u32[]{:S(2)}) copy-start(bf16[1,512,640]{2,1,0:T(8,128)(2,1)} %param.11) | copy-start | bytes 1966084
  8.7 104.6 %copy-start.2 = (bf16[1,512,640]{2,1,0:T(8,128)(2,1)S(1)}, bf16[1,512,640]{2,1,0:T(8,128)(2,1)}, u32[]{:S(2)}) copy-start(bf16[1,512,640]{2,1,0:T(8,128)(2,1)} %param.10) | copy-start | bytes 1966084

commit v4 on v3

--- a/solution.py
+++ b/solution.py
@@ -191,11 +191,20 @@
         [dq_sum, kv_sum, jnp.zeros((tail_rows * tail_width - wide - tail_width,), jnp.float32)]
     ).reshape(tail_rows, tail_width)
     spread = jnp.zeros((count, tile, tail_width), jnp.float32).at[targets].add(partial)
-    spread = jnp.concatenate([spread, jnp.broadcast_to(tail, (count, tail_rows, tail_width))], axis=1)
+    rounded = lax.reduce_precision(tail, exponent_bits=8, mantissa_bits=7)
+    high = rounded.astype(jnp.bfloat16)
+    low = (tail - rounded).astype(jnp.bfloat16)
+    coded = jnp.concatenate([high, low], axis=0)
+    spread = jnp.concatenate(
+        [spread.astype(jnp.bfloat16), jnp.broadcast_to(coded, (count,) + coded.shape)], axis=1
+    )
     landed = exchange(spread, "ctx", True, 1)
-    summed = landed[0]
+    summed = landed[0].astype(jnp.float32)
     for peer in range(1, count):
-        summed = summed + landed[peer]
+        summed = summed + landed[peer].astype(jnp.float32)
+    summed = jnp.concatenate(
+        [summed[:tile], summed[tile:tile + tail_rows] + summed[tile + tail_rows:]], axis=0
+    )
     grads = summed[:tile]
     both = exchange(summed[tile:], "dp", False, 2)
     sums = (both[0] + both[1]).reshape(-1) * norm

time: 370 us -> 269 us (0.73)
  Pallas kernels: 332 us -> 230 us
    pallas_call x3, Pallas kernels: 310 us -> 208 us  [exchange(): pl.pallas_call(functools.partial(exchange_kernel, axis=axis, n=n, indexed...]
    concatenate x1 -> x2, other arithmetic: 7.54 us -> 2.28 us  [the longest x1 2.28 us: on_device(): jnp.concatenate([spread.astype(jnp.bfloat16), jnp.broadcast_to(coded, (co...]
    convert_element_type x0 -> x2, other arithmetic: none -> 3.9 us  [the longest x1 3.89 us: on_device(): spread.astype(jnp.bfloat16)]
where the time goes in v4:
time: 269 us; the launch traced here: 265 us
  Pallas kernels  230 us (86%)
  other arithmetic  23.5 us (9%)
  local copies, waits for them, and re-layouts  9.07 us (3%)
  between operations  2.76 us (1%)
    pallas_call x3, Pallas kernels, exchange(): pl.pallas_call(functools.partial(exchange_kernel, axis=axis, n=n, indexed...  208 us
    pallas_call x1, Pallas kernels, attention_grads(): pl.pallas_call(functools.partial(attention_grads_kernel, slots=slots, sca...  21.9 us

profile of v4, /device:TPU:13, one launch (start us, length us, event | category | flops | bytes accessed | tf_op | source)
XLA Modules:
  0.0 265.2 jit_solution(3818363586223746914)
XLA Ops:
  0.6 0.0 copy-start.4
  0.6 0.0 copy-start.3
  0.7 1.3 fusion.1
  2.6 1.9 fusion.2
  5.9 0.1 add_convert_fusion.flags_ref
  6.0 0.1 pad_add_fusion
  6.0 0.8 select_reduce_fusion
  6.9 0.1 fusion.4
  7.0 1.7 pad_maximum_fusion.3.x_ref
  8.7 101.5 %shard_map.118 = bf16[16,512,256]{2,1,0:T(8,128)(2,1)} custom-call(bf16[512,256]{1,0:T(8,128)(2,1)} %pad_maximum_fusion.3.x_ref), custom_call_target="tpu_custom_call" | custom-call | tf_op jit(solution)/shard_map/pallas_call | solution.py:136
  110.2 2.8 %gather_fusion = bf16[3,512,256]{2,1,0:T(8,128)(2,1)S(1)} fusion(bf16[16,512,256]{2,1,0:T(8,128)(2,1)} %shard_map.118, s32[1024]{0:T(1024)S(1)} %pad_clamp_fusion), kind=kCustom, calls=%fused_computation | custom fusion | bytes 1572876 | tf_op jit(solution)/shard_map/gather | solution.py:174
  113.0 0.1 fusion.7
  113.1 0.0 copy-done.4
  113.1 0.0 copy-done.3
  113.1 0.1 pad_maximum_fusion.1
  113.3 21.9 %shard_map.119 = (f32[512,640]{1,0:T(8,128)}, f32[4,512,128]{2,1,0:T(8,128)S(1)}, f32[4,512,128]{2,1,0:T(8,128)S(1)}) custom-call(s32[4]{0:T(128)S(1)} %add_convert_fusion.flags_ref, bf16[512,640]{1,0:T(8,128)(2,1)S(1)} %bitcast.35, bf16[512,640]{1,0:T(8,128)(2,1)S(1)} %bitcast.36, bf16[512,640]{1,0:T(8,128)(2,1)S(1)} %bitcast.37, ...), custom_call_target="tpu_custom_call" | custom-call | tf_op jit(solution)/shard_map/pallas_call | solution.py:82
  135.1 2.7 %fusion.6 = (f32[640]{0:T(1024)S(1)}, bf16[1,512,640]{2,1,0:T(8,128)(2,1)}) fusion(f32[512,640]{1,0:T(8,128)} %get-tuple-element.9), kind=kLoop, calls=%fused_computation.33 | loop fusion | flops 654720 | bytes 1968640 | tf_op jit(solution)/shard_map/reduce_sum | solution.py:186
  137.8 0.1 constant_dynamic-update-slice_fusion.1
  137.9 0.1 constant_dynamic-update-slice_fusion
  138.0 0.3 reduce_sum.52
  138.3 4.1 %broadcast_in_dim.44 = f32[16,512,256]{2,1,0:T(8,128)} broadcast(f32[]{:T(128)} %constant.6.clone.1), dimensions={} | broadcast | bytes 8388612 | tf_op jit(solution)/shard_map/broadcast_in_dim | solution.py:193
  142.4 4.1 %scatter_fusion = f32[16,512,256]{2,1,0:T(8,128)} fusion(f32[16,512,256]{2,1,0:T(8,128)} %broadcast_in_dim.44, s32[4]{0:T(128)S(1)} %fusion.4, f32[4,512,256]{2,1,0:T(8,128)S(1)} %constant_dynamic-update-slice_fusion), kind=kCustom, calls=%fused_computation.1 | custom fusion | flops 524288 | bytes 6291472 | tf_op jit(solution)/shard_map/scatter-add | solution.py:193
  146.5 3.9 %convert_element_type.107 = bf16[16,512,256]{2,1,0:T(8,128)(2,1)S(1)} convert(f32[16,512,256]{2,1,0:T(8,128)} %scatter_fusion) | non-fusion elementwise | flops 2097152 | bytes 12582912 | tf_op jit(solution)/shard_map/convert_element_type | solution.py:199
  150.4 2.3 pad_maximum_fusion.x_ref
  152.7 102.9 %shard_map.120 = bf16[16,528,256]{2,1,0:T(8,128)(2,1)} custom-call(bf16[16,528,256]{2,1,0:T(8,128)(2,1)} %pad_maximum_fusion.x_ref), custom_call_target="tpu_custom_call" | custom-call | tf_op jit(solution)/shard_map/pallas_call | solution.py:136
  255.6 2.8 %fusion.5 = (bf16[528,256]{1,0:T(8,128)(2,1)S(1)}, f32[528,256]{1,0:T(8,128)S(1)}) fusion(bf16[16,528,256]{2,1,0:T(8,128)(2,1)} %shard_map.120), kind=kLoop, calls=%fused_computation.32 | loop fusion | flops 4325376 | bytes 5136384 | tf_op jit(solution)/shard_map/convert.13
  258.4 0.7 slice_bitcast_fusion
  259.1 0.6 slice_add_fusion.x_ref
  259.7 3.6 %shard_map.121 = f32[2,8,256]{2,1,0:T(8,128)} custom-call(f32[8,256]{1,0:T(8,128)} %slice_add_fusion.x_ref), custom_call_target="tpu_custom_call" | custom-call | tf_op jit(solution)/shard_map/pallas_call | solution.py:136
  263.3 0.7 multiply_bitcast_fusion
  264.1 0.5 fusion.8
  264.6 0.6 slice.121
  (15 shorter events, 0.1 us)
Async XLA Ops:
  0.6 112.5 %copy-start.4 = (bf16[1,512,128]{2,1,0:T(8,128)(2,1)S(1)}, bf16[1,512,128]{2,1,0:T(8,128)(2,1)}, u32[]{:S(2)}) copy-start(bf16[1,512,128]{2,1,0:T(8,128)(2,1)} %param.9) | copy-start | bytes 393220
  0.6 112.5 %copy-start.3 = (bf16[1,512,128]{2,1,0:T(8,128)(2,1)S(1)}, bf16[1,512,128]{2,1,0:T(8,128)(2,1)}, u32[]{:S(2)}) copy-start(bf16[1,512,128]{2,1,0:T(8,128)(2,1)} %param.8) | copy-start | bytes 393220
  8.7 104.6 %copy-start = (bf16[1,512,640]{2,1,0:T(8,128)(2,1)S(1)}, bf16[1,512,640]{2,1,0:T(8,128)(2,1)}, u32[]{:S(2)}) copy-start(bf16[1,512,640]{2,1,0:T(8,128)(2,1)} %param.7) | copy-start | bytes 1966084
  8.7 104.6 %copy-start.1 = (bf16[1,512,640]{2,1,0:T(8,128)(2,1)S(1)}, bf16[1,512,640]{2,1,0:T(8,128)(2,1)}, u32[]{:S(2)}) copy-start(bf16[1,512,640]{2,1,0:T(8,128)(2,1)} %param.11) | copy-start | bytes 1966084
  8.7 104.6 %copy-start.2 = (bf16[1,512,640]{2,1,0:T(8,128)(2,1)S(1)}, bf16[1,512,640]{2,1,0:T(8,128)(2,1)}, u32[]{:S(2)}) copy-start(bf16[1,512,640]{2,1,0:T(8,128)(2,1)} %param.10) | copy-start | bytes 1966084

commit v5 on v4

--- a/solution.py
+++ b/solution.py
@@ -147,6 +147,85 @@
     )(x)
 
 
+def relay_gather_kernel(x_ref, out_ref, send_sem, recv_sem, self_sem, *, n):
+    me = lax.axis_index("ctx")
+    ring = n // 2
+    z = me // 2
+    side = me % 2
+    partner = z * 2 + (1 - side)
+    up = lax.rem(z + 1, ring) * 2 + side
+    down = lax.rem(z + ring - 1, ring) * 2 + side
+    barrier = pltpu.get_barrier_semaphore()
+    for peer in (partner, up, down):
+        pl.semaphore_signal(barrier, inc=1, device_id={"ctx": peer},
+                            device_id_type=pl.DeviceIdType.MESH)
+    pl.semaphore_wait(barrier, 3)
+    local = pltpu.make_async_copy(x_ref, out_ref.at[me], self_sem)
+    local.start()
+    sends = []
+
+    def send(slot, target, src):
+        copy = pltpu.make_async_remote_copy(
+            src_ref=src, dst_ref=out_ref.at[slot], send_sem=send_sem.at[len(sends)],
+            recv_sem=recv_sem.at[slot], device_id={"ctx": target},
+            device_id_type=pl.DeviceIdType.MESH,
+        )
+        copy.start()
+        sends.append(copy)
+
+    def arrive(slot):
+        pltpu.make_async_remote_copy(
+            src_ref=x_ref, dst_ref=out_ref.at[slot], send_sem=send_sem.at[0],
+            recv_sem=recv_sem.at[slot], device_id={"ctx": partner},
+            device_id_type=pl.DeviceIdType.MESH,
+        ).wait_recv()
+
+    def origin(step, offset):
+        return lax.rem(z + step + ring, ring) * 2 + offset
+
+    upward = ring // 2
+    downward = ring - 1 - upward
+    send(me, partner, x_ref)
+    send(me, up, x_ref)
+    send(me, down, x_ref)
+    arrive(partner)
+    send(partner, up, out_ref.at[partner])
+    send(partner, down, out_ref.at[partner])
+    for step in range(2, upward + 1):
+        for offset in (0, 1):
+            slot = origin(-(step - 1), offset)
+            arrive(slot)
+            send(slot, up, out_ref.at[slot])
+        if step <= downward:
+            for offset in (0, 1):
+                slot = origin(step - 1, offset)
+                arrive(slot)
+                send(slot, down, out_ref.at[slot])
+    for offset in (0, 1):
+        arrive(origin(-upward, offset))
+    for offset in (0, 1):
+        arrive(origin(downward, offset))
+    for copy in sends:
+        copy.wait_send()
+    local.wait()
+
+
+def relay_gather(x, collective_id):
+    n = lax.axis_size("ctx")
+    return pl.pallas_call(
+        functools.partial(relay_gather_kernel, n=n),
+        out_shape=jax.ShapeDtypeStruct((n,) + tuple(x.shape), x.dtype),
+        in_specs=[pl.BlockSpec(memory_space=pl.ANY)],
+        out_specs=pl.BlockSpec(memory_space=pl.ANY),
+        scratch_shapes=[
+            pltpu.SemaphoreType.DMA((n - 1,)),
+            pltpu.SemaphoreType.DMA((n,)),
+            pltpu.SemaphoreType.DMA,
+        ],
+        compiler_params=pltpu.CompilerParams(collective_id=collective_id, has_side_effects=True),
+    )(x)
+
+
 def on_device(query, key, value, output, output_gradient, parent, owner):
     count = lax.axis_size("ctx")
     me = lax.axis_index("ctx")
@@ -170,7 +249,7 @@
     flags = jnp.stack([trained, trained, second, trained]).astype(jnp.int32)
 
     pair = jnp.concatenate([key[0], value[0]], axis=1)
-    gathered = exchange(pair, "ctx", False, 0)
+    gathered = relay_gather(pair, 0)
     picked = gathered[slot_blocks]
     keys = jnp.concatenate([picked[:, :, :width], key[0][None]], axis=0)
     values = jnp.concatenate([picked[:, :, width:], value[0][None]], axis=0)

time: 269 us -> 217 us (0.81)
  Pallas kernels: 230 us -> 179 us
    pallas_call x3 -> x2, Pallas kernels: 208 us -> 103 us  [exchange(): pl.pallas_call(functools.partial(exchange_kernel, axis=axis, n=n, indexed...]
    pallas_call x0 -> x1, Pallas kernels: none -> 53.8 us  [relay_gather(): pl.pallas_call(functools.partial(relay_gather_kernel, n=n), out_shape=jax...]
where the time goes in v5:
time: 217 us; the launch traced here: 214 us
  Pallas kernels  179 us (82%)
  other arithmetic  23.5 us (11%)
  local copies, waits for them, and re-layouts  9.07 us (4%)
  between operations  2.76 us (1%)
    pallas_call x2, Pallas kernels, exchange(): pl.pallas_call(functools.partial(exchange_kernel, axis=axis, n=n, indexed...  103 us
    pallas_call x1, Pallas kernels, relay_gather(): pl.pallas_call(functools.partial(relay_gather_kernel, n=n), out_shape=jax...  53.8 us
    pallas_call x1, Pallas kernels, attention_grads(): pl.pallas_call(functools.partial(attention_grads_kernel, slots=slots, sca...  21.8 us

profile of v5, /device:TPU:13, one launch (start us, length us, event | category | flops | bytes accessed | tf_op | source)
XLA Modules:
  0.0 214.2 jit_solution(6867320945135402948)
XLA Ops:
  0.6 0.0 copy-start.4
  0.6 0.0 copy-start.3
  0.7 1.3 fusion.1
  2.6 1.9 fusion.2
  5.9 0.1 add_convert_fusion.flags_ref
  6.0 0.1 pad_add_fusion
  6.0 0.8 select_reduce_fusion
  6.9 0.1 fusion.4
  7.0 1.7 pad_maximum_fusion.3.x_ref
  8.7 53.8 %shard_map.118 = bf16[16,512,256]{2,1,0:T(8,128)(2,1)} custom-call(bf16[512,256]{1,0:T(8,128)(2,1)} %pad_maximum_fusion.3.x_ref), custom_call_target="tpu_custom_call" | custom-call | tf_op jit(solution)/shard_map/pallas_call | solution.py:215
  62.5 2.8 %gather_fusion = bf16[3,512,256]{2,1,0:T(8,128)(2,1)S(1)} fusion(bf16[16,512,256]{2,1,0:T(8,128)(2,1)} %shard_map.118, s32[1024]{0:T(1024)S(1)} %pad_clamp_fusion), kind=kCustom, calls=%fused_computation | custom fusion | bytes 1572876 | tf_op jit(solution)/shard_map/gather | solution.py:253
  65.3 0.1 fusion.7
  65.5 0.0 copy-done.4
  65.5 0.0 copy-done.3
  65.5 0.1 pad_maximum_fusion.1
  65.6 21.8 %shard_map.119 = (f32[512,640]{1,0:T(8,128)}, f32[4,512,128]{2,1,0:T(8,128)S(1)}, f32[4,512,128]{2,1,0:T(8,128)S(1)}) custom-call(s32[4]{0:T(128)S(1)} %add_convert_fusion.flags_ref, bf16[512,640]{1,0:T(8,128)(2,1)S(1)} %bitcast.35, bf16[512,640]{1,0:T(8,128)(2,1)S(1)} %bitcast.36, bf16[512,640]{1,0:T(8,128)(2,1)S(1)} %bitcast.37, ...), custom_call_target="tpu_custom_call" | custom-call | tf_op jit(solution)/shard_map/pallas_call | solution.py:82
  87.4 2.7 %fusion.6 = (f32[640]{0:T(1024)S(1)}, bf16[1,512,640]{2,1,0:T(8,128)(2,1)}) fusion(f32[512,640]{1,0:T(8,128)} %get-tuple-element.9), kind=kLoop, calls=%fused_computation.33 | loop fusion | flops 654720 | bytes 1968640 | tf_op jit(solution)/shard_map/reduce_sum | solution.py:265
  90.1 0.1 constant_dynamic-update-slice_fusion.1
  90.2 0.1 constant_dynamic-update-slice_fusion
  90.3 0.3 reduce_sum.52
  90.7 4.1 %broadcast_in_dim.44 = f32[16,512,256]{2,1,0:T(8,128)} broadcast(f32[]{:T(128)} %constant.6.clone.1), dimensions={} | broadcast | bytes 8388612 | tf_op jit(solution)/shard_map/broadcast_in_dim | solution.py:272
  94.8 4.1 %scatter_fusion = f32[16,512,256]{2,1,0:T(8,128)} fusion(f32[16,512,256]{2,1,0:T(8,128)} %broadcast_in_dim.44, s32[4]{0:T(128)S(1)} %fusion.4, f32[4,512,256]{2,1,0:T(8,128)S(1)} %constant_dynamic-update-slice_fusion), kind=kCustom, calls=%fused_computation.1 | custom fusion | flops 524288 | bytes 6291472 | tf_op jit(solution)/shard_map/scatter-add | solution.py:272
  98.9 3.9 %convert_element_type.107 = bf16[16,512,256]{2,1,0:T(8,128)(2,1)S(1)} convert(f32[16,512,256]{2,1,0:T(8,128)} %scatter_fusion) | non-fusion elementwise | flops 2097152 | bytes 12582912 | tf_op jit(solution)/shard_map/convert_element_type | solution.py:278
  102.8 2.3 %pad_maximum_fusion.x_ref = bf16[16,528,256]{2,1,0:T(8,128)(2,1)} fusion(bf16[16,16,256]{2,1,0:T(8,128)(2,1)S(1)} %broadcast_in_dim.46, bf16[16,512,256]{2,1,0:T(8,128)(2,1)S(1)} %convert_element_type.107), kind=kLoop, calls=%fused_computation.2 | loop fusion | flops 8650752 | bytes 8650752 | tf_op jit(solution)/shard_map/concatenate | solution.py:277
  105.1 100.2 %shard_map.120 = bf16[16,528,256]{2,1,0:T(8,128)(2,1)} custom-call(bf16[16,528,256]{2,1,0:T(8,128)(2,1)} %pad_maximum_fusion.x_ref), custom_call_target="tpu_custom_call" | custom-call | tf_op jit(solution)/shard_map/pallas_call | solution.py:136
  205.3 2.8 %fusion.5 = (bf16[528,256]{1,0:T(8,128)(2,1)S(1)}, f32[528,256]{1,0:T(8,128)S(1)}) fusion(bf16[16,528,256]{2,1,0:T(8,128)(2,1)} %shard_map.120), kind=kLoop, calls=%fused_computation.32 | loop fusion | flops 4325376 | bytes 5136384 | tf_op jit(solution)/shard_map/convert.13
  208.0 0.7 slice_bitcast_fusion
  208.7 0.6 slice_add_fusion.x_ref
  209.3 3.1 %shard_map.121 = f32[2,8,256]{2,1,0:T(8,128)} custom-call(f32[8,256]{1,0:T(8,128)} %slice_add_fusion.x_ref), custom_call_target="tpu_custom_call" | custom-call | tf_op jit(solution)/shard_map/pallas_call | solution.py:136
  212.4 0.7 multiply_bitcast_fusion
  213.1 0.5 fusion.8
  213.6 0.6 slice.121
  (15 shorter events, 0.1 us)
Async XLA Ops:
  0.6 64.8 %copy-start.4 = (bf16[1,512,128]{2,1,0:T(8,128)(2,1)S(1)}, bf16[1,512,128]{2,1,0:T(8,128)(2,1)}, u32[]{:S(2)}) copy-start(bf16[1,512,128]{2,1,0:T(8,128)(2,1)} %param.9) | copy-start | bytes 393220
  0.6 64.8 %copy-start.3 = (bf16[1,512,128]{2,1,0:T(8,128)(2,1)S(1)}, bf16[1,512,128]{2,1,0:T(8,128)(2,1)}, u32[]{:S(2)}) copy-start(bf16[1,512,128]{2,1,0:T(8,128)(2,1)} %param.8) | copy-start | bytes 393220
  8.7 56.9 %copy-start = (bf16[1,512,640]{2,1,0:T(8,128)(2,1)S(1)}, bf16[1,512,640]{2,1,0:T(8,128)(2,1)}, u32[]{:S(2)}) copy-start(bf16[1,512,640]{2,1,0:T(8,128)(2,1)} %param.7) | copy-start | bytes 1966084
  8.7 56.9 %copy-start.1 = (bf16[1,512,640]{2,1,0:T(8,128)(2,1)S(1)}, bf16[1,512,640]{2,1,0:T(8,128)(2,1)}, u32[]{:S(2)}) copy-start(bf16[1,512,640]{2,1,0:T(8,128)(2,1)} %param.11) | copy-start | bytes 1966084
  8.7 56.9 %copy-start.2 = (bf16[1,512,640]{2,1,0:T(8,128)(2,1)S(1)}, bf16[1,512,640]{2,1,0:T(8,128)(2,1)}, u32[]{:S(2)}) copy-start(bf16[1,512,640]{2,1,0:T(8,128)(2,1)} %param.10) | copy-start | bytes 1966084

commit v6 on v5

--- a/solution.py
+++ b/solution.py
@@ -226,6 +226,95 @@
     )(x)
 
 
+def relay_reduce_kernel(x_ref, out_ref, up_in, down_in, up_out, down_out, side_out, side_in,
+                        send_sem, recv_sem, *, n):
+    me = lax.axis_index("ctx")
+    ring = n // 2
+    z = me // 2
+    side = me % 2
+    partner = z * 2 + (1 - side)
+    up = lax.rem(z + 1, ring) * 2 + side
+    down = lax.rem(z + ring - 1, ring) * 2 + side
+    upward = ring // 2
+    downward = ring - 1 - upward
+    barrier = pltpu.get_barrier_semaphore()
+    for peer in (partner, up, down):
+        pl.semaphore_signal(barrier, inc=1, device_id={"ctx": peer},
+                            device_id_type=pl.DeviceIdType.MESH)
+    pl.semaphore_wait(barrier, 3)
+    sends = []
+
+    def send(src, dst, target, sem_index):
+        copy = pltpu.make_async_remote_copy(
+            src_ref=src, dst_ref=dst, send_sem=send_sem.at[len(sends)],
+            recv_sem=recv_sem.at[sem_index], device_id={"ctx": target},
+            device_id_type=pl.DeviceIdType.MESH,
+        )
+        copy.start()
+        sends.append(copy)
+        return copy
+
+    def own(target_z):
+        block = pl.multiple_of(lax.rem(target_z + 2 * ring, ring) * 2, 2)
+        return x_ref[pl.ds(block, 2)]
+
+    pending_up = None
+    pending_down = None
+    for step in range(1, upward + 1):
+        term = own(z + upward - step + 1)
+        if pending_up is not None:
+            pending_up.wait_recv()
+            term = term + up_in[step - 2].astype(jnp.float32)
+        up_out[step - 1] = term.astype(up_out.dtype)
+        pending_up = send(up_out.at[step - 1], up_in.at[step - 1], up, step - 1)
+        if step <= downward:
+            term = own(z - (downward - step + 1))
+            if pending_down is not None:
+                pending_down.wait_recv()
+                term = term + down_in[step - 2].astype(jnp.float32)
+            down_out[step - 1] = term.astype(down_out.dtype)
+            pending_down = send(down_out.at[step - 1], down_in.at[step - 1], down,
+                                upward + step - 1)
+    pending_up.wait_recv()
+    pending_down.wait_recv()
+    mine = (own(z) + up_in[upward - 1].astype(jnp.float32)
+            + down_in[downward - 1].astype(jnp.float32))
+    side_out[...] = jnp.where(side == 0, mine[1], mine[0])
+    across = send(side_out, side_in, partner, upward + downward)
+    across.wait_recv()
+    out_ref[...] = jnp.where(side == 0, mine[0], mine[1]) + side_in[...]
+    for copy in sends:
+        copy.wait_send()
+
+
+def relay_reduce(x, collective_id):
+    n, rows, cols = x.shape
+    ring = n // 2
+    upward = ring // 2
+    downward = ring - 1 - upward
+    vmem = pl.BlockSpec(memory_space=pltpu.VMEM)
+    return pl.pallas_call(
+        functools.partial(relay_reduce_kernel, n=n),
+        out_shape=jax.ShapeDtypeStruct((rows, cols), jnp.float32),
+        in_specs=[vmem],
+        out_specs=vmem,
+        scratch_shapes=[
+            pltpu.VMEM((upward, 2, rows, cols), jnp.bfloat16),
+            pltpu.VMEM((downward, 2, rows, cols), jnp.bfloat16),
+            pltpu.VMEM((upward, 2, rows, cols), jnp.bfloat16),
+            pltpu.VMEM((downward, 2, rows, cols), jnp.bfloat16),
+            pltpu.VMEM((rows, cols), jnp.float32),
+            pltpu.VMEM((rows, cols), jnp.float32),
+            pltpu.SemaphoreType.DMA((upward + downward + 1,)),
+            pltpu.SemaphoreType.DMA((upward + downward + 1,)),
+        ],
+        compiler_params=pltpu.CompilerParams(
+            collective_id=collective_id, has_side_effects=True,
+            vmem_limit_bytes=56 * 1024 * 1024,
+        ),
+    )(x)
+
+
 def on_device(query, key, value, output, output_gradient, parent, owner):
     count = lax.axis_size("ctx")
     me = lax.axis_index("ctx")
@@ -270,22 +359,12 @@
         [dq_sum, kv_sum, jnp.zeros((tail_rows * tail_width - wide - tail_width,), jnp.float32)]
     ).reshape(tail_rows, tail_width)
     spread = jnp.zeros((count, tile, tail_width), jnp.float32).at[targets].add(partial)
-    rounded = lax.reduce_precision(tail, exponent_bits=8, mantissa_bits=7)
-    high = rounded.astype(jnp.bfloat16)
-    low = (tail - rounded).astype(jnp.bfloat16)
-    coded = jnp.concatenate([high, low], axis=0)
-    spread = jnp.concatenate(
-        [spread.astype(jnp.bfloat16), jnp.broadcast_to(coded, (count,) + coded.shape)], axis=1
-    )
-    landed = exchange(spread, "ctx", True, 1)
-    summed = landed[0].astype(jnp.float32)
+    grads = relay_reduce(spread, 1)
+    landed = exchange(tail, "ctx", False, 3)
+    summed = landed[0]
     for peer in range(1, count):
-        summed = summed + landed[peer].astype(jnp.float32)
-    summed = jnp.concatenate(
-        [summed[:tile], summed[tile:tile + tail_rows] + summed[tile + tail_rows:]], axis=0
-    )
-    grads = summed[:tile]
-    both = exchange(summed[tile:], "dp", False, 2)
+        summed = summed + landed[peer]
+    both = exchange(summed, "dp", False, 2)
     sums = (both[0] + both[1]).reshape(-1) * norm
     sum_q = sums[:wide]
     sum_k = sums[wide:wide + width]

time: 217 us -> 183 us (0.84)
  Pallas kernels: 179 us -> 152 us
  other arithmetic: 23.5 us -> 15.8 us
    pallas_call x2, Pallas kernels: 103 us -> 18.6 us  [exchange(): pl.pallas_call(functools.partial(exchange_kernel, axis=axis, n=n, indexed...]
    pallas_call x0 -> x1, Pallas kernels: none -> 58.2 us  [relay_reduce(): pl.pallas_call(functools.partial(relay_reduce_kernel, n=n), out_shape=jax...]
    convert_element_type x2 -> x0, other arithmetic: 3.9 us -> none  [the longest x1 3.89 us: on_device(): spread.astype(jnp.bfloat16)]
    concatenate x2 -> x0, other arithmetic: 2.28 us -> none  [the longest x1 2.28 us: on_device(): jnp.concatenate([spread.astype(jnp.bfloat16), jnp.broadcast_to(coded, (co...]
where the time goes in v6:
time: 183 us; the launch traced here: 182 us
  Pallas kernels  152 us (83%)
  other arithmetic  15.8 us (9%)
  local copies, waits for them, and re-layouts  10.8 us (6%)
  between operations  2.78 us (2%)
    pallas_call x1, Pallas kernels, relay_reduce(): pl.pallas_call(functools.partial(relay_reduce_kernel, n=n), out_shape=jax...  58.2 us
    pallas_call x1, Pallas kernels, relay_gather(): pl.pallas_call(functools.partial(relay_gather_kernel, n=n), out_shape=jax...  53.8 us
    pallas_call x1, Pallas kernels, attention_grads(): pl.pallas_call(functools.partial(attention_grads_kernel, slots=slots, sca...  21.8 us
    pallas_call x2, Pallas kernels, exchange(): pl.pallas_call(functools.partial(exchange_kernel, axis=axis, n=n, indexed...  18.6 us
    broadcast_in_dim x1, local copies, waits for them, and re-layouts, on_device(): jnp.zeros((count, tile, tail_width), jnp.float32).at[targets].add(partial)  4.1 us
    scatter-add x1, other arithmetic, on_device(): jnp.zeros((count, tile, tail_width), jnp.float32).at[targets].add(partial)  4.07 us

profile of v6, /device:TPU:13, one launch (start us, length us, event | category | flops | bytes accessed | tf_op | source)
XLA Modules:
  0.0 181.9 jit_solution(763236017634855069)
XLA Ops:
  0.6 1.3 fusion
  2.6 1.9 %fusion.1 = s32[]{:T(128)} fusion(s32[1,16]{1,0:T(1,128)} %param.12, s32[]{:T(128)} %fusion), kind=kLoop, calls=%fused_computation.22 | loop fusion | flops 47 | bytes 72 | tf_op jit(solution)/shard_map/reduce_sum | solution.py:17
  5.2 0.1 add_convert_fusion.flags_ref
  5.3 1.7 pad_maximum_fusion.2.x_ref
  7.0 53.8 %shard_map.118 = bf16[16,512,256]{2,1,0:T(8,128)(2,1)} custom-call(bf16[512,256]{1,0:T(8,128)(2,1)} %pad_maximum_fusion.2.x_ref), custom_call_target="tpu_custom_call" | custom-call | tf_op jit(solution)/shard_map/pallas_call | solution.py:215
  60.8 0.0 copy-start.3
  61.5 0.1 pad_add_fusion
  61.6 0.2 select_reduce_fusion
  61.8 2.8 %gather_fusion = bf16[3,512,256]{2,1,0:T(8,128)(2,1)S(1)} fusion(bf16[16,512,256]{2,1,0:T(8,128)(2,1)} %shard_map.118, s32[1024]{0:T(1024)S(1)} %pad_clamp_fusion), kind=kCustom, calls=%fused_computation | custom fusion | bytes 1572876 | tf_op jit(solution)/shard_map/gather | solution.py:342
  64.6 0.1 fusion.5
  64.8 0.1 pad_maximum_fusion
  64.9 0.8 copy-done
  65.7 0.2 copy-done.1
  65.9 0.2 copy-done.2
  66.1 21.8 %shard_map.119 = (f32[512,640]{1,0:T(8,128)}, f32[4,512,128]{2,1,0:T(8,128)S(1)}, f32[4,512,128]{2,1,0:T(8,128)S(1)}) custom-call(s32[4]{0:T(128)S(1)} %add_convert_fusion.flags_ref, bf16[512,640]{1,0:T(8,128)(2,1)S(1)} %bitcast.30, bf16[512,640]{1,0:T(8,128)(2,1)S(1)} %bitcast.31, bf16[512,640]{1,0:T(8,128)(2,1)S(1)} %bitcast.32, ...), custom_call_target="tpu_custom_call" | custom-call | tf_op jit(solution)/shard_map/pallas_call | solution.py:82
  87.9 2.7 %fusion.4 = (f32[640]{0:T(1024)S(1)}, bf16[1,512,640]{2,1,0:T(8,128)(2,1)}) fusion(f32[512,640]{1,0:T(8,128)} %get-tuple-element.9), kind=kLoop, calls=%fused_computation.26 | loop fusion | flops 654720 | bytes 1968640 | tf_op jit(solution)/shard_map/reduce_sum | solution.py:354
  90.6 0.1 fusion.3
  90.7 0.1 constant_dynamic-update-slice_fusion.1
  90.8 0.1 constant_dynamic-update-slice_fusion
  90.9 4.1 %broadcast_in_dim.41 = f32[16,512,256]{2,1,0:T(8,128)} broadcast(f32[]{:T(128)} %constant.6.clone.1), dimensions={} | broadcast | bytes 8388612 | tf_op jit(solution)/shard_map/broadcast_in_dim | solution.py:361
  95.0 4.1 %scatter_fusion = f32[16,512,256]{2,1,0:T(8,128)} fusion(f32[16,512,256]{2,1,0:T(8,128)} %broadcast_in_dim.41, s32[4]{0:T(128)S(1)} %fusion.3, f32[4,512,256]{2,1,0:T(8,128)S(1)} %constant_dynamic-update-slice_fusion), kind=kCustom, calls=%fused_computation.1 | custom fusion | flops 524288 | bytes 6291472 | tf_op jit(solution)/shard_map/scatter-add | solution.py:361
  99.0 58.2 %shard_map.120 = f32[512,256]{1,0:T(8,128)} custom-call(f32[16,512,256]{2,1,0:T(8,128)} %scatter_fusion), custom_call_target="tpu_custom_call" | custom-call | tf_op jit(solution)/shard_map/pallas_call | solution.py:296
  157.3 1.1 convert.4
  158.4 0.7 slice_bitcast_fusion
  159.1 0.3 reduce_sum.52
  159.4 0.6 reshape.123.x_ref
  160.0 13.0 %shard_map.121 = f32[16,8,256]{2,1,0:T(8,128)} custom-call(f32[8,256]{1,0:T(8,128)} %reshape.123.x_ref), custom_call_target="tpu_custom_call" | custom-call | tf_op jit(solution)/shard_map/pallas_call | solution.py:136
  173.0 1.5 add_bitcast_fusion.x_ref
  174.4 5.6 %shard_map.122 = f32[2,8,256]{2,1,0:T(8,128)} custom-call(f32[8,256]{1,0:T(8,128)} %add_bitcast_fusion.x_ref), custom_call_target="tpu_custom_call" | custom-call | tf_op jit(solution)/shard_map/pallas_call | solution.py:136
  180.0 0.7 multiply_bitcast_fusion
  180.8 0.6 slice.108
  181.4 0.5 fusion.6
  (13 shorter events, 0.1 us)
Async XLA Ops:
  7.0 54.6 %copy-start.5 = (s32[1,16]{1,0:T(1,128)S(1)}, s32[1,16]{1,0:T(1,128)}, u32[]{:S(2)}) copy-start(s32[1,16]{1,0:T(1,128)} %param.13) | copy-start | bytes 196
  60.8 4.0 %copy-start.3 = (bf16[1,512,128]{2,1,0:T(8,128)(2,1)S(1)}, bf16[1,512,128]{2,1,0:T(8,128)(2,1)}, u32[]{:S(2)}) copy-start(bf16[1,512,128]{2,1,0:T(8,128)(2,1)} %param.8) | copy-start | bytes 393220
  60.8 4.0 %copy-start.4 = (bf16[1,512,128]{2,1,0:T(8,128)(2,1)S(1)}, bf16[1,512,128]{2,1,0:T(8,128)(2,1)}, u32[]{:S(2)}) copy-start(bf16[1,512,128]{2,1,0:T(8,128)(2,1)} %param.9) | copy-start | bytes 393220
  64.6 1.1 copy-start
  64.6 1.3 copy-start.1
  64.6 1.5 copy-start.2

commit v7 on v6

--- a/solution.py
+++ b/solution.py
@@ -226,8 +226,9 @@
     )(x)
 
 
-def relay_reduce_kernel(x_ref, out_ref, up_in, down_in, up_out, down_out, side_out, side_in,
-                        send_sem, recv_sem, *, n):
+def relay_reduce_kernel(t_ref, x_ref, tail_ref, out_ref, tails_ref, up_in, down_in, up_out,
+                        down_out, side_out, side_in, tails_in, send_sem, recv_sem, tail_send,
+                        tail_recv, *, n):
     me = lax.axis_index("ctx")
     ring = n // 2
     z = me // 2
@@ -238,10 +239,20 @@
     upward = ring // 2
     downward = ring - 1 - upward
     barrier = pltpu.get_barrier_semaphore()
-    for peer in (partner, up, down):
-        pl.semaphore_signal(barrier, inc=1, device_id={"ctx": peer},
+    for d in range(1, n):
+        pl.semaphore_signal(barrier, inc=1, device_id={"ctx": lax.rem(me + d, n)},
                             device_id_type=pl.DeviceIdType.MESH)
-    pl.semaphore_wait(barrier, 3)
+    pl.semaphore_wait(barrier, n - 1)
+    tail_copies = []
+    for d in range(1, n):
+        copy = pltpu.make_async_remote_copy(
+            src_ref=tail_ref, dst_ref=tails_in.at[me], send_sem=tail_send.at[d - 1],
+            recv_sem=tail_recv.at[d - 1], device_id={"ctx": lax.rem(me + d, n)},
+            device_id_type=pl.DeviceIdType.MESH,
+        )
+        copy.start()
+        tail_copies.append(copy)
+    tails_in[me] = tail_ref[...]
     sends = []
 
     def send(src, dst, target, sem_index):
@@ -255,8 +266,14 @@
         return copy
 
     def own(target_z):
-        block = pl.multiple_of(lax.rem(target_z + 2 * ring, ring) * 2, 2)
-        return x_ref[pl.ds(block, 2)]
+        base = lax.rem(target_z + 2 * ring, ring) * 2
+        pieces = []
+        for offset in (0, 1):
+            total = jnp.zeros(x_ref.shape[1:], jnp.float32)
+            for j in range(x_ref.shape[0]):
+                total = total + jnp.where(t_ref[j] == base + offset, x_ref[j], 0.0)
+            pieces.append(total)
+        return jnp.stack(pieces)
 
     pending_up = None
     pending_down = None
@@ -285,19 +302,27 @@
     out_ref[...] = jnp.where(side == 0, mine[0], mine[1]) + side_in[...]
     for copy in sends:
         copy.wait_send()
-
-
-def relay_reduce(x, collective_id):
-    n, rows, cols = x.shape
+    for copy in tail_copies:
+        copy.wait_send()
+    for copy in tail_copies:
+        copy.wait_recv()
+    tails_ref[...] = tails_in[...]
+
+
+def relay_reduce(targets, partial, tail, n, collective_id):
+    _, rows, cols = partial.shape
     ring = n // 2
     upward = ring // 2
     downward = ring - 1 - upward
     vmem = pl.BlockSpec(memory_space=pltpu.VMEM)
     return pl.pallas_call(
         functools.partial(relay_reduce_kernel, n=n),
-        out_shape=jax.ShapeDtypeStruct((rows, cols), jnp.float32),
-        in_specs=[vmem],
-        out_specs=vmem,
+        out_shape=[
+            jax.ShapeDtypeStruct((rows, cols), jnp.float32),
+            jax.ShapeDtypeStruct((n,) + tuple(tail.shape), jnp.float32),
+        ],
+        in_specs=[pl.BlockSpec(memory_space=pltpu.SMEM), vmem, vmem],
+        out_specs=[vmem, vmem],
         scratch_shapes=[
             pltpu.VMEM((upward, 2, rows, cols), jnp.bfloat16),
             pltpu.VMEM((downward, 2, rows, cols), jnp.bfloat16),
@@ -305,14 +330,17 @@
             pltpu.VMEM((downward, 2, rows, cols), jnp.bfloat16),
             pltpu.VMEM((rows, cols), jnp.float32),
             pltpu.VMEM((rows, cols), jnp.float32),
+            pltpu.VMEM((n,) + tuple(tail.shape), jnp.float32),
             pltpu.SemaphoreType.DMA((upward + downward + 1,)),
             pltpu.SemaphoreType.DMA((upward + downward + 1,)),
+            pltpu.SemaphoreType.DMA((n - 1,)),
+            pltpu.SemaphoreType.DMA((n - 1,)),
         ],
         compiler_params=pltpu.CompilerParams(
             collective_id=collective_id, has_side_effects=True,
             vmem_limit_bytes=56 * 1024 * 1024,
         ),
-    )(x)
+    )(targets, partial, tail)
 
 
 def on_device(query, key, value, output, output_gradient, parent, owner):
@@ -358,9 +386,7 @@
     tail = jnp.concatenate(
         [dq_sum, kv_sum, jnp.zeros((tail_rows * tail_width - wide - tail_width,), jnp.float32)]
     ).reshape(tail_rows, tail_width)
-    spread = jnp.zeros((count, tile, tail_width), jnp.float32).at[targets].add(partial)
-    grads = relay_reduce(spread, 1)
-    landed = exchange(tail, "ctx", False, 3)
+    grads, landed = relay_reduce(targets, partial, tail, count, 1)
     summed = landed[0]
     for peer in range(1, count):
         summed = summed + landed[peer]

time: 183 us -> 169 us (0.923); the launches traced: 182 us -> 166 us
  Pallas kernels: 152 us -> 144 us
  local copies, waits for them, and re-layouts: 10.8 us -> 7.19 us
  other arithmetic: 15.8 us -> 12.2 us
    pallas_call x2 -> x1, Pallas kernels: 18.6 us -> 7.12 us  [exchange(): pl.pallas_call(functools.partial(exchange_kernel, axis=axis, n=n, indexed...]
    broadcast_in_dim x1 -> x0, local copies, waits for them, and re-layouts: 4.1 us -> none  [on_device(): jnp.zeros((count, tile, tail_width), jnp.float32).at[targets].add(partial)]
    scatter-add x1 -> x0, other arithmetic: 4.07 us -> none  [on_device(): jnp.zeros((count, tile, tail_width), jnp.float32).at[targets].add(partial)]
    pallas_call x1, Pallas kernels: 58.2 us -> 60.8 us  [relay_reduce(): pl.pallas_call(functools.partial(relay_reduce_kernel, n=n), out_shape=[ja...]
where the time goes in v7:
time: 169 us; the launch traced here: 166 us
  Pallas kernels  144 us (85%)
  other arithmetic  12.2 us (7%)
  local copies, waits for them, and re-layouts  7.19 us (4%)
  between operations  2.78 us (2%)
    pallas_call x1, Pallas kernels, relay_reduce(): pl.pallas_call(functools.partial(relay_reduce_kernel, n=n), out_shape=[ja...  60.8 us
    pallas_call x1, Pallas kernels, relay_gather(): pl.pallas_call(functools.partial(relay_gather_kernel, n=n), out_shape=jax...  53.8 us
    pallas_call x1, Pallas kernels, attention_grads(): pl.pallas_call(functools.partial(attention_grads_kernel, slots=slots, sca...  21.8 us
    pallas_call x1, Pallas kernels, exchange(): pl.pallas_call(functools.partial(exchange_kernel, axis=axis, n=n, indexed...  7.12 us

profile of v7, /device:TPU:13, one launch (start us, length us, event | category | flops | bytes accessed | tf_op | source)
XLA Modules:
  0.0 165.7 jit_solution(5488258840598623442)
XLA Ops:
  0.6 1.3 fusion
  2.6 1.9 %fusion.1 = s32[]{:T(128)} fusion(s32[1,16]{1,0:T(1,128)} %param.12, s32[]{:T(128)} %fusion), kind=kLoop, calls=%fused_computation.20 | loop fusion | flops 47 | bytes 72 | tf_op jit(solution)/shard_map/reduce_sum | solution.py:17
  5.2 0.1 add_convert_fusion.flags_ref
  5.3 1.7 %pad_maximum_fusion.2.x_ref = bf16[512,256]{1,0:T(8,128)(2,1)} fusion(bf16[512,128]{1,0:T(8,128)(2,1)} %bitcast.32, bf16[512,128]{1,0:T(8,128)(2,1)} %bitcast.31), kind=kLoop, calls=%fused_computation.4 | loop fusion | flops 524288 | bytes 524288 | tf_op jit(solution)/shard_map/concatenate | solution.py:368
  7.0 53.8 %shard_map.118 = bf16[16,512,256]{2,1,0:T(8,128)(2,1)} custom-call(bf16[512,256]{1,0:T(8,128)(2,1)} %pad_maximum_fusion.2.x_ref), custom_call_target="tpu_custom_call" | custom-call | tf_op jit(solution)/shard_map/pallas_call | solution.py:215
  60.8 0.0 copy-start.4
  61.5 0.1 pad_add_fusion
  61.6 0.2 select_reduce_fusion
  61.8 2.8 %gather_fusion = bf16[3,512,256]{2,1,0:T(8,128)(2,1)S(1)} fusion(bf16[16,512,256]{2,1,0:T(8,128)(2,1)} %shard_map.118, s32[1024]{0:T(1024)S(1)} %pad_clamp_fusion), kind=kCustom, calls=%fused_computation | custom fusion | bytes 1572876 | tf_op jit(solution)/shard_map/gather | solution.py:370
  64.6 0.0 copy-start
  64.6 0.0 copy-start.1
  64.6 0.1 fusion.4
  64.8 0.1 pad_maximum_fusion
  64.9 0.8 copy-done
  65.7 0.2 copy-done.1
  65.9 0.2 copy-done.2
  66.1 21.8 %shard_map.119 = (f32[512,640]{1,0:T(8,128)}, f32[4,512,128]{2,1,0:T(8,128)S(1)}, f32[4,512,128]{2,1,0:T(8,128)S(1)}) custom-call(s32[4]{0:T(128)S(1)} %add_convert_fusion.flags_ref, bf16[512,640]{1,0:T(8,128)(2,1)S(1)} %bitcast.28, bf16[512,640]{1,0:T(8,128)(2,1)S(1)} %bitcast.29, bf16[512,640]{1,0:T(8,128)(2,1)S(1)} %bitcast.30, ...), custom_call_target="tpu_custom_call" | custom-call | tf_op jit(solution)/shard_map/pallas_call | solution.py:82
  87.9 2.7 %fusion.3 = (f32[640]{0:T(1024)S(1)}, bf16[1,512,640]{2,1,0:T(8,128)(2,1)}) fusion(f32[512,640]{1,0:T(8,128)} %get-tuple-element.11), kind=kLoop, calls=%fused_computation.24 | loop fusion | flops 654720 | bytes 1968640 | tf_op jit(solution)/shard_map/reduce_sum | solution.py:382
  90.6 0.6 pad_add_fusion.1.t_ref
  91.2 0.1 constant_dynamic-update-slice_fusion.1
  91.3 0.1 constant_dynamic-update-slice_fusion.x_ref
  91.4 0.3 reduce_sum.52
  91.7 0.9 reshape.39.tail_ref
  92.6 0.2 copy-done.3
  92.7 60.8 %shard_map.120 = (f32[512,256]{1,0:T(8,128)}, f32[16,8,256]{2,1,0:T(8,128)}) custom-call(s32[4]{0:T(128)} %pad_add_fusion.1.t_ref, f32[4,512,256]{2,1,0:T(8,128)} %copy-done.3, f32[8,256]{1,0:T(8,128)} %reshape.39.tail_ref), custom_call_target="tpu_custom_call" | custom-call | tf_op jit(solution)/shard_map/pallas_call | solution.py:318
  153.5 1.1 convert.4
  154.6 0.7 slice_bitcast_fusion
  155.3 1.5 add_bitcast_fusion.x_ref
  156.7 7.1 %shard_map.121 = f32[2,8,256]{2,1,0:T(8,128)} custom-call(f32[8,256]{1,0:T(8,128)} %add_bitcast_fusion.x_ref), custom_call_target="tpu_custom_call" | custom-call | tf_op jit(solution)/shard_map/pallas_call | solution.py:136
  163.9 0.7 multiply_bitcast_fusion
  164.6 0.6 slice.108
  165.2 0.5 fusion.5
  (12 shorter events, 0.1 us)
Async XLA Ops:
  7.0 54.6 %copy-start.6 = (s32[1,16]{1,0:T(1,128)S(1)}, s32[1,16]{1,0:T(1,128)}, u32[]{:S(2)}) copy-start(s32[1,16]{1,0:T(1,128)} %param.13) | copy-start | bytes 196
  60.8 4.0 %copy-start.4 = (bf16[1,512,128]{2,1,0:T(8,128)(2,1)S(1)}, bf16[1,512,128]{2,1,0:T(8,128)(2,1)}, u32[]{:S(2)}) copy-start(bf16[1,512,128]{2,1,0:T(8,128)(2,1)} %param.8) | copy-start | bytes 393220
  60.8 4.0 %copy-start.5 = (bf16[1,512,128]{2,1,0:T(8,128)(2,1)S(1)}, bf16[1,512,128]{2,1,0:T(8,128)(2,1)}, u32[]{:S(2)}) copy-start(bf16[1,512,128]{2,1,0:T(8,128)(2,1)} %param.9) | copy-start | bytes 393220
  64.6 1.1 copy-start
  64.6 1.3 copy-start.1
  64.6 1.5 copy-start.2
  91.4 1.4 copy-start.3

commit v8 on v7

--- a/solution.py
+++ b/solution.py
@@ -265,39 +265,51 @@
         sends.append(copy)
         return copy
 
-    def own(target_z):
+    chunks = up_in.shape[1]
+    part = x_ref.shape[1] // chunks
+
+    def own(target_z, chunk):
         base = lax.rem(target_z + 2 * ring, ring) * 2
         pieces = []
         for offset in (0, 1):
-            total = jnp.zeros(x_ref.shape[1:], jnp.float32)
+            total = jnp.zeros((part, x_ref.shape[2]), jnp.float32)
             for j in range(x_ref.shape[0]):
-                total = total + jnp.where(t_ref[j] == base + offset, x_ref[j], 0.0)
+                total = total + jnp.where(
+                    t_ref[j] == base + offset, x_ref[j, pl.ds(chunk * part, part)], 0.0
+                )
             pieces.append(total)
         return jnp.stack(pieces)
 
-    pending_up = None
-    pending_down = None
+    pending_up = [None] * chunks
+    pending_down = [None] * chunks
     for step in range(1, upward + 1):
-        term = own(z + upward - step + 1)
-        if pending_up is not None:
-            pending_up.wait_recv()
-            term = term + up_in[step - 2].astype(jnp.float32)
-        up_out[step - 1] = term.astype(up_out.dtype)
-        pending_up = send(up_out.at[step - 1], up_in.at[step - 1], up, step - 1)
-        if step <= downward:
-            term = own(z - (downward - step + 1))
-            if pending_down is not None:
-                pending_down.wait_recv()
-                term = term + down_in[step - 2].astype(jnp.float32)
-            down_out[step - 1] = term.astype(down_out.dtype)
-            pending_down = send(down_out.at[step - 1], down_in.at[step - 1], down,
-                                upward + step - 1)
-    pending_up.wait_recv()
-    pending_down.wait_recv()
-    mine = (own(z) + up_in[upward - 1].astype(jnp.float32)
-            + down_in[downward - 1].astype(jnp.float32))
+        for chunk in range(chunks):
+            term = own(z + upward - step + 1, chunk)
+            if pending_up[chunk] is not None:
+                pending_up[chunk].wait_recv()
+                term = term + up_in[step - 2, chunk].astype(jnp.float32)
+            up_out[step - 1, chunk] = term.astype(up_out.dtype)
+            pending_up[chunk] = send(up_out.at[step - 1, chunk], up_in.at[step - 1, chunk], up,
+                                     (step - 1) * chunks + chunk)
+            if step <= downward:
+                term = own(z - (downward - step + 1), chunk)
+                if pending_down[chunk] is not None:
+                    pending_down[chunk].wait_recv()
+                    term = term + down_in[step - 2, chunk].astype(jnp.float32)
+                down_out[step - 1, chunk] = term.astype(down_out.dtype)
+                pending_down[chunk] = send(
+                    down_out.at[step - 1, chunk], down_in.at[step - 1, chunk], down,
+                    (upward + step - 1) * chunks + chunk,
+                )
+    pieces = []
+    for chunk in range(chunks):
+        pending_up[chunk].wait_recv()
+        pending_down[chunk].wait_recv()
+        pieces.append(own(z, chunk) + up_in[upward - 1, chunk].astype(jnp.float32)
+                      + down_in[downward - 1, chunk].astype(jnp.float32))
+    mine = jnp.concatenate(pieces, axis=1)
     side_out[...] = jnp.where(side == 0, mine[1], mine[0])
-    across = send(side_out, side_in, partner, upward + downward)
+    across = send(side_out, side_in, partner, (upward + downward) * chunks)
     across.wait_recv()
     out_ref[...] = jnp.where(side == 0, mine[0], mine[1]) + side_in[...]
     for copy in sends:
@@ -309,7 +321,7 @@
     tails_ref[...] = tails_in[...]
 
 
-def relay_reduce(targets, partial, tail, n, collective_id):
+def relay_reduce(targets, partial, tail, n, collective_id, chunks=2):
     _, rows, cols = partial.shape
     ring = n // 2
     upward = ring // 2
@@ -324,15 +336,15 @@
         in_specs=[pl.BlockSpec(memory_space=pltpu.SMEM), vmem, vmem],
         out_specs=[vmem, vmem],
         scratch_shapes=[
-            pltpu.VMEM((upward, 2, rows, cols), jnp.bfloat16),
-            pltpu.VMEM((downward, 2, rows, cols), jnp.bfloat16),
-            pltpu.VMEM((upward, 2, rows, cols), jnp.bfloat16),
-            pltpu.VMEM((downward, 2, rows, cols), jnp.bfloat16),
+            pltpu.VMEM((upward, chunks, 2, rows // chunks, cols), jnp.bfloat16),
+            pltpu.VMEM((downward, chunks, 2, rows // chunks, cols), jnp.bfloat16),
+            pltpu.VMEM((upward, chunks, 2, rows // chunks, cols), jnp.bfloat16),
+            pltpu.VMEM((downward, chunks, 2, rows // chunks, cols), jnp.bfloat16),
             pltpu.VMEM((rows, cols), jnp.float32),
             pltpu.VMEM((rows, cols), jnp.float32),
             pltpu.VMEM((n,) + tuple(tail.shape), jnp.float32),
-            pltpu.SemaphoreType.DMA((upward + downward + 1,)),
-            pltpu.SemaphoreType.DMA((upward + downward + 1,)),
+            pltpu.SemaphoreType.DMA(((upward + downward) * chunks + 1,)),
+            pltpu.SemaphoreType.DMA(((upward + downward) * chunks + 1,)),
             pltpu.SemaphoreType.DMA((n - 1,)),
             pltpu.SemaphoreType.DMA((n - 1,)),
         ],

time: 169 us -> 171 us (1.012)
  Pallas kernels: 144 us -> 146 us
    pallas_call x1, Pallas kernels: 60.8 us -> 65.2 us  [relay_reduce(): pl.pallas_call(functools.partial(relay_reduce_kernel, n=n), out_shape=[ja...]
    pallas_call x1, Pallas kernels: 7.12 us -> 4.89 us  [exchange(): pl.pallas_call(functools.partial(exchange_kernel, axis=axis, n=n, indexed...]
where the time goes in v8:
time: 171 us; the launch traced here: 168 us
  Pallas kernels  146 us (85%)
  other arithmetic  12.2 us (7%)
  local copies, waits for them, and re-layouts  7.19 us (4%)
  between operations  2.78 us (2%)
    pallas_call x1, Pallas kernels, relay_reduce(): pl.pallas_call(functools.partial(relay_reduce_kernel, n=n), out_shape=[ja...  65.2 us
    pallas_call x1, Pallas kernels, relay_gather(): pl.pallas_call(functools.partial(relay_gather_kernel, n=n), out_shape=jax...  53.8 us
    pallas_call x1, Pallas kernels, attention_grads(): pl.pallas_call(functools.partial(attention_grads_kernel, slots=slots, sca...  21.8 us
    pallas_call x1, Pallas kernels, exchange(): pl.pallas_call(functools.partial(exchange_kernel, axis=axis, n=n, indexed...  4.89 us

profile of v8, /device:TPU:13, one launch (start us, length us, event | category | flops | bytes accessed | tf_op | source)
XLA Modules:
  0.0 167.9 jit_solution(9406154218078613358)
XLA Ops:
  0.6 1.3 fusion
  2.6 1.9 %fusion.1 = s32[]{:T(128)} fusion(s32[1,16]{1,0:T(1,128)} %param.12, s32[]{:T(128)} %fusion), kind=kLoop, calls=%fused_computation.20 | loop fusion | flops 47 | bytes 72 | tf_op jit(solution)/shard_map/reduce_sum | solution.py:17
  5.2 0.1 add_convert_fusion.flags_ref
  5.3 1.7 %pad_maximum_fusion.2.x_ref = bf16[512,256]{1,0:T(8,128)(2,1)} fusion(bf16[512,128]{1,0:T(8,128)(2,1)} %bitcast.32, bf16[512,128]{1,0:T(8,128)(2,1)} %bitcast.31), kind=kLoop, calls=%fused_computation.4 | loop fusion | flops 524288 | bytes 524288 | tf_op jit(solution)/shard_map/concatenate | solution.py:380
  7.0 53.8 %shard_map.118 = bf16[16,512,256]{2,1,0:T(8,128)(2,1)} custom-call(bf16[512,256]{1,0:T(8,128)(2,1)} %pad_maximum_fusion.2.x_ref), custom_call_target="tpu_custom_call" | custom-call | tf_op jit(solution)/shard_map/pallas_call | solution.py:215
  60.8 0.0 copy-start.4
  61.5 0.1 pad_add_fusion
  61.6 0.2 select_reduce_fusion
  61.8 2.8 %gather_fusion = bf16[3,512,256]{2,1,0:T(8,128)(2,1)S(1)} fusion(bf16[16,512,256]{2,1,0:T(8,128)(2,1)} %shard_map.118, s32[1024]{0:T(1024)S(1)} %pad_clamp_fusion), kind=kCustom, calls=%fused_computation | custom fusion | bytes 1572876 | tf_op jit(solution)/shard_map/gather | solution.py:382
  64.6 0.0 copy-start
  64.6 0.0 copy-start.1
  64.6 0.1 fusion.4
  64.8 0.1 pad_maximum_fusion
  64.9 0.8 copy-done
  65.7 0.2 copy-done.1
  65.9 0.2 copy-done.2
  66.1 21.8 %shard_map.119 = (f32[512,640]{1,0:T(8,128)}, f32[4,512,128]{2,1,0:T(8,128)S(1)}, f32[4,512,128]{2,1,0:T(8,128)S(1)}) custom-call(s32[4]{0:T(128)S(1)} %add_convert_fusion.flags_ref, bf16[512,640]{1,0:T(8,128)(2,1)S(1)} %bitcast.28, bf16[512,640]{1,0:T(8,128)(2,1)S(1)} %bitcast.29, bf16[512,640]{1,0:T(8,128)(2,1)S(1)} %bitcast.30, ...), custom_call_target="tpu_custom_call" | custom-call | tf_op jit(solution)/shard_map/pallas_call | solution.py:82
  87.9 2.7 %fusion.3 = (f32[640]{0:T(1024)S(1)}, bf16[1,512,640]{2,1,0:T(8,128)(2,1)}) fusion(f32[512,640]{1,0:T(8,128)} %get-tuple-element.11), kind=kLoop, calls=%fused_computation.24 | loop fusion | flops 654720 | bytes 1968640 | tf_op jit(solution)/shard_map/reduce_sum | solution.py:394
  90.6 0.6 pad_add_fusion.1.t_ref
  91.2 0.1 constant_dynamic-update-slice_fusion.1
  91.3 0.1 constant_dynamic-update-slice_fusion.x_ref
  91.4 0.3 reduce_sum.52
  91.7 0.9 reshape.39.tail_ref
  92.6 0.2 copy-done.3
  92.7 65.2 %shard_map.120 = (f32[512,256]{1,0:T(8,128)}, f32[16,8,256]{2,1,0:T(8,128)}) custom-call(s32[4]{0:T(128)} %pad_add_fusion.1.t_ref, f32[4,512,256]{2,1,0:T(8,128)} %copy-done.3, f32[8,256]{1,0:T(8,128)} %reshape.39.tail_ref), custom_call_target="tpu_custom_call" | custom-call | tf_op jit(solution)/shard_map/pallas_call | solution.py:330
  157.9 1.1 convert.4
  159.0 0.7 slice_bitcast_fusion
  159.7 1.5 add_bitcast_fusion.x_ref
  161.2 4.9 %shard_map.121 = f32[2,8,256]{2,1,0:T(8,128)} custom-call(f32[8,256]{1,0:T(8,128)} %add_bitcast_fusion.x_ref), custom_call_target="tpu_custom_call" | custom-call | tf_op jit(solution)/shard_map/pallas_call | solution.py:136
  166.1 0.7 multiply_bitcast_fusion
  166.8 0.6 slice.108
  167.4 0.5 fusion.5
  (12 shorter events, 0.1 us)
Async XLA Ops:
  7.0 54.6 %copy-start.6 = (s32[1,16]{1,0:T(1,128)S(1)}, s32[1,16]{1,0:T(1,128)}, u32[]{:S(2)}) copy-start(s32[1,16]{1,0:T(1,128)} %param.13) | copy-start | bytes 196
  60.8 4.0 %copy-start.4 = (bf16[1,512,128]{2,1,0:T(8,128)(2,1)S(1)}, bf16[1,512,128]{2,1,0:T(8,128)(2,1)}, u32[]{:S(2)}) copy-start(bf16[1,512,128]{2,1,0:T(8,128)(2,1)} %param.8) | copy-start | bytes 393220
  60.8 4.0 %copy-start.5 = (bf16[1,512,128]{2,1,0:T(8,128)(2,1)S(1)}, bf16[1,512,128]{2,1,0:T(8,128)(2,1)}, u32[]{:S(2)}) copy-start(bf16[1,512,128]{2,1,0:T(8,128)(2,1)} %param.9) | copy-start | bytes 393220
  64.6 1.1 copy-start
  64.6 1.3 copy-start.1
  64.6 1.5 copy-start.2
  91.4 1.4 copy-start.3

commit v9 on v7

--- a/solution.py
+++ b/solution.py
@@ -22,9 +22,13 @@
     return jnp.sum(jnp.where((spots == index)[:, None], matrix, 0.0), axis=0)
 
 
-def attention_grads_kernel(flags_ref, q_ref, g_ref, o_ref, k_ref, v_ref,
-                           dq_ref, dk_ref, dv_ref, s_scr, *, slots, scale):
+def attention_grads_kernel(flags_ref, blocks_ref, q_ref, g_ref, o_ref, k0, k1, k2, k3, v0, v1, v2,
+                           v3, dq_ref, dqsum_ref, dk_ref, dv_ref, ksum_ref, vsum_ref, s_scr, *,
+                           scale):
     head = pl.program_id(0)
+    k_refs = (k0, k1, k2, k3)
+    v_refs = (v0, v1, v2, v3)
+    slots = len(k_refs)
 
     @pl.when(head == 0)
     def _():
@@ -46,7 +50,7 @@
         keep = flags_ref[j] > 0
         if j == slots - 1:
             keep = jnp.logical_and(keep, causal)
-        scores = lax.dot_general(q, k_ref[j], nt, preferred_element_type=jnp.float32) * scale
+        scores = lax.dot_general(q, k_refs[j][...], nt, preferred_element_type=jnp.float32) * scale
         scores = jnp.where(keep, scores, NEGATIVE_FILL)
         s_scr[j] = scores
         top = jnp.maximum(top, jnp.max(scores, axis=1, keepdims=True))
@@ -66,37 +70,54 @@
         probs = s_scr[j] * inverse
         dv_ref[j] += lax.dot_general(probs.astype(jnp.bfloat16), g, tn,
                                      preferred_element_type=jnp.float32)
-        dprobs = lax.dot_general(g, v_ref[j], nt, preferred_element_type=jnp.float32)
+        dprobs = lax.dot_general(g, v_refs[j][...], nt, preferred_element_type=jnp.float32)
         dscores = (probs * (dprobs - delta)).astype(jnp.bfloat16)
-        dq = dq + jnp.dot(dscores, k_ref[j], preferred_element_type=jnp.float32)
+        dq = dq + jnp.dot(dscores, k_refs[j][...], preferred_element_type=jnp.float32)
         dk_ref[j] += lax.dot_general(dscores, q, tn, preferred_element_type=jnp.float32) * scale
-    dq_ref[...] = dq * scale
-
-
-def attention_grads(flags, q, g, o, keys, values, scale):
+    dq = dq * scale
+    dq_ref[...] = dq.astype(dq_ref.dtype)
+    dqsum_ref[...] = jnp.sum(dq, axis=0, keepdims=True)
+
+    @pl.when(head == pl.num_programs(0) - 1)
+    def _():
+        ksum_ref[...] = jnp.sum(jnp.sum(dk_ref[...], axis=0), axis=0, keepdims=True)
+        vsum_ref[...] = jnp.sum(jnp.sum(dv_ref[...], axis=0), axis=0, keepdims=True)
+
+
+def attention_grads(flags, blocks, q, g, o, gathered, scale):
     rows, wide = q.shape
-    slots = keys.shape[0]
+    slots = blocks.shape[0]
     heads = wide // HEAD_WIDTH
-    col = pl.BlockSpec((rows, HEAD_WIDTH), lambda h, f: (0, h))
-    whole = pl.BlockSpec((slots, rows, HEAD_WIDTH), lambda h, f: (0, 0, 0))
+    col = pl.BlockSpec((rows, HEAD_WIDTH), lambda h, f, b: (0, h))
+    line = pl.BlockSpec((1, HEAD_WIDTH), lambda h, f, b: (0, h))
+    fixed = pl.BlockSpec((1, HEAD_WIDTH), lambda h, f, b: (0, 0))
+    whole = pl.BlockSpec((slots, rows, HEAD_WIDTH), lambda h, f, b: (0, 0, 0))
+
+    def pick(j, part):
+        return pl.BlockSpec((None, rows, HEAD_WIDTH), lambda h, f, b: (b[j], 0, part))
+
     return pl.pallas_call(
-        functools.partial(attention_grads_kernel, slots=slots, scale=scale),
+        functools.partial(attention_grads_kernel, scale=scale),
         grid_spec=pltpu.PrefetchScalarGridSpec(
-            num_scalar_prefetch=1,
+            num_scalar_prefetch=2,
             grid=(heads,),
-            in_specs=[col, col, col, whole, whole],
-            out_specs=[col, whole, whole],
+            in_specs=[col, col, col] + [pick(j, 0) for j in range(slots)]
+            + [pick(j, 1) for j in range(slots)],
+            out_specs=[col, line, whole, whole, fixed, fixed],
             scratch_shapes=[pltpu.VMEM((slots, rows, rows), jnp.float32)],
         ),
         out_shape=[
-            jax.ShapeDtypeStruct((rows, wide), jnp.float32),
+            jax.ShapeDtypeStruct((rows, wide), jnp.bfloat16),
+            jax.ShapeDtypeStruct((1, wide), jnp.float32),
             jax.ShapeDtypeStruct((slots, rows, HEAD_WIDTH), jnp.float32),
             jax.ShapeDtypeStruct((slots, rows, HEAD_WIDTH), jnp.float32),
+            jax.ShapeDtypeStruct((1, HEAD_WIDTH), jnp.float32),
+            jax.ShapeDtypeStruct((1, HEAD_WIDTH), jnp.float32),
         ],
         compiler_params=pltpu.CompilerParams(
             dimension_semantics=("arbitrary",), vmem_limit_bytes=48 * 1024 * 1024
         ),
-    )(flags, q, g, o, keys, values)
+    )(flags, blocks, q, g, o, *([gathered] * (2 * slots)))
 
 
 def exchange_kernel(x_ref, out_ref, send_sem, recv_sem, self_sem, *, axis, n, indexed):
@@ -367,24 +388,19 @@
 
     pair = jnp.concatenate([key[0], value[0]], axis=1)
     gathered = relay_gather(pair, 0)
-    picked = gathered[slot_blocks]
-    keys = jnp.concatenate([picked[:, :, :width], key[0][None]], axis=0)
-    values = jnp.concatenate([picked[:, :, width:], value[0][None]], axis=0)
-
-    dq, dk, dv = attention_grads(
-        flags, query[0], output_gradient[0], output[0], keys, values, scale_factor
+    targets = jnp.concatenate([slot_blocks, me[None].astype(jnp.int32)])
+    dq, dq_sum, dk, dv, k_sum, v_sum = attention_grads(
+        flags, targets, query[0], output_gradient[0], output[0], gathered, scale_factor
     )
     partial = jnp.concatenate([dk, dv], axis=2)
-    targets = jnp.concatenate([slot_blocks, me[None].astype(jnp.int32)])
     total_rows = lax.axis_size("dp") * query.shape[0] * count * tile
     norm = total_rows ** (-0.5)
     wide = query.shape[2]
-    dq_sum = jnp.sum(dq, axis=0)
-    kv_sum = jnp.sum(partial, axis=(0, 1))
     tail_width = 2 * width
     tail_rows = 8
     tail = jnp.concatenate(
-        [dq_sum, kv_sum, jnp.zeros((tail_rows * tail_width - wide - tail_width,), jnp.float32)]
+        [dq_sum[0], k_sum[0], v_sum[0],
+         jnp.zeros((tail_rows * tail_width - wide - tail_width,), jnp.float32)]
     ).reshape(tail_rows, tail_width)
     grads, landed = relay_reduce(targets, partial, tail, count, 1)
     summed = landed[0]
@@ -396,7 +412,7 @@
     sum_k = sums[wide:wide + width]
     sum_v = sums[wide + width:wide + 2 * width]
     return (
-        dq.astype(jnp.bfloat16)[None],
+        dq[None],
         grads[:, :width].astype(jnp.bfloat16)[None],
         grads[:, width:].astype(jnp.bfloat16)[None],
         sum_q,

time: 169 us -> 165 us (0.976)
  local copies, waits for them, and re-layouts: 7.19 us -> 3.54 us
    reduce_sum x2 -> x0, other arithmetic: 2.97 us -> none  [the longest x1 2.69 us: on_device(): dq_sum = jnp.sum(dq, axis=0)]
    gather x1 -> x0, local copies, waits for them, and re-layouts: 2.78 us -> none  [on_device(): picked = gathered[slot_blocks]]
    pallas_call x1, Pallas kernels: 21.8 us -> 23.5 us  [attention_grads(): pl.pallas_call(functools.partial(attention_grads_kernel, scale=scale), gr...]
where the time goes in v9:
time: 165 us; the launch traced here: 162 us
  Pallas kernels  145 us (88%)
  other arithmetic  10.8 us (7%)
  local copies, waits for them, and re-layouts  3.54 us (2%)
  between operations  2.67 us (2%)
    pallas_call x1, Pallas kernels, relay_reduce(): pl.pallas_call(functools.partial(relay_reduce_kernel, n=n), out_shape=[ja...  60.7 us
    pallas_call x1, Pallas kernels, relay_gather(): pl.pallas_call(functools.partial(relay_gather_kernel, n=n), out_shape=jax...  53.8 us
    pallas_call x1, Pallas kernels, attention_grads(): pl.pallas_call(functools.partial(attention_grads_kernel, scale=scale), gr...  23.5 us
    pallas_call x1, Pallas kernels, exchange(): pl.pallas_call(functools.partial(exchange_kernel, axis=axis, n=n, indexed...  7.12 us

profile of v9, /device:TPU:13, one launch (start us, length us, event | category | flops | bytes accessed | tf_op | source)
XLA Modules:
  0.0 162.2 jit_solution(15865988457256198278)
XLA Ops:
  0.6 1.3 fusion
  1.9 1.9 %fusion.1 = s32[]{:T(128)} fusion(s32[1,16]{1,0:T(1,128)} %param.12, s32[]{:T(128)} %fusion), kind=kLoop, calls=%fused_computation.13 | loop fusion | flops 47 | bytes 72 | tf_op jit(solution)/shard_map/reduce_sum | solution.py:17
  5.8 0.1 pad_add_fusion
  5.9 0.8 select_reduce_fusion
  6.7 0.1 pad_add_fusion.1.blocks_ref.t_ref
  6.8 0.0 copy-start.3
  6.8 0.1 add_convert_fusion.flags_ref
  6.9 1.7 %pad_maximum_fusion.1.x_ref = bf16[512,256]{1,0:T(8,128)(2,1)} fusion(bf16[512,128]{1,0:T(8,128)(2,1)} %bitcast.30, bf16[512,128]{1,0:T(8,128)(2,1)} %bitcast.31), kind=kLoop, calls=%fused_computation.1 | loop fusion | flops 524288 | bytes 524288 | tf_op jit(solution)/shard_map/concatenate | solution.py:389
  8.6 0.0 copy-start
  8.6 0.0 copy-start.1
  8.6 53.8 %shard_map.118.k0.k1.k2.k3.v0.v1.v2.v3 = bf16[16,512,256]{2,1,0:T(8,128)(2,1)} custom-call(bf16[512,256]{1,0:T(8,128)(2,1)} %pad_maximum_fusion.1.x_ref), custom_call_target="tpu_custom_call" | custom-call | tf_op jit(solution)/shard_map/pallas_call | solution.py:236
  62.4 0.0 copy-done.3
  62.4 0.0 copy-done
  62.4 0.0 copy-done.1
  62.5 0.0 copy-start.2
  62.5 1.1 copy-done.2
  63.5 23.5 %shard_map.119 = (bf16[512,640]{1,0:T(8,128)(2,1)}, f32[1,640]{1,0:T(1,128)S(1)}, f32[4,512,128]{2,1,0:T(8,128)S(1)}, f32[4,512,128]{2,1,0:T(8,128)S(1)}, f32[1,128]{1,0:T(1,128)S(1)}, /*index=5*/f32[1,128]{1,0:T(1,128)S(1)}) custom-call(s32[4]{0:T(128)S(1)} %add_convert_fusion.flags_ref, s32[4]{0:T(128)S(1)} %pad_add_fusion.1.blocks_ref.t_ref, ...), custom_call_target="tpu_custom_call" | custom-call | tf_op jit(solution)/shard_map/pallas_call | solution.py:99
  87.1 0.6 reshape.26.tail_ref
  87.7 1.5 pad_maximum_fusion.x_ref
  89.2 60.7 %shard_map.120 = (f32[512,256]{1,0:T(8,128)}, f32[16,8,256]{2,1,0:T(8,128)}) custom-call(s32[4]{0:T(128)} %copy-done.3, f32[4,512,256]{2,1,0:T(8,128)} %pad_maximum_fusion.x_ref, f32[8,256]{1,0:T(8,128)} %reshape.26.tail_ref), custom_call_target="tpu_custom_call" | custom-call | tf_op jit(solution)/shard_map/pallas_call | solution.py:339
  150.0 1.1 convert.4
  151.1 0.7 slice_bitcast_fusion
  151.8 1.5 add_bitcast_fusion.x_ref
  153.2 7.1 %shard_map.121 = f32[2,8,256]{2,1,0:T(8,128)} custom-call(f32[8,256]{1,0:T(8,128)} %add_bitcast_fusion.x_ref), custom_call_target="tpu_custom_call" | custom-call | tf_op jit(solution)/shard_map/pallas_call | solution.py:157
  160.4 0.7 multiply_bitcast_fusion
  161.1 0.6 slice.96
  161.7 0.5 fusion.2
  (4 shorter events, 0.0 us)
Async XLA Ops:
  6.8 55.6 %copy-start.3 = (s32[4]{0:T(128)}, s32[4]{0:T(128)S(1)}, u32[]{:S(2)}) copy-start(s32[4]{0:T(128)S(1)} %pad_add_fusion.1.blocks_ref.t_ref) | copy-start | bytes 52
  8.6 53.8 %copy-start = (bf16[1,512,640]{2,1,0:T(8,128)(2,1)S(1)}, bf16[1,512,640]{2,1,0:T(8,128)(2,1)}, u32[]{:S(2)}) copy-start(bf16[1,512,640]{2,1,0:T(8,128)(2,1)} %param.7) | copy-start | bytes 1966084
  8.6 53.9 %copy-start.1 = (bf16[1,512,640]{2,1,0:T(8,128)(2,1)S(1)}, bf16[1,512,640]{2,1,0:T(8,128)(2,1)}, u32[]{:S(2)}) copy-start(bf16[1,512,640]{2,1,0:T(8,128)(2,1)} %param.11) | copy-start | bytes 1966084
  62.5 1.1 copy-start.2

commit v10 on v9

--- a/solution.py
+++ b/solution.py
@@ -202,10 +202,28 @@
         ).wait_recv()
 
     def origin(step, offset):
-        return lax.rem(z + step + ring, ring) * 2 + offset
+        return lax.rem(z + step + 2 * ring, ring) * 2 + offset
+
+    def send_part(slot, target, rows, sem_index):
+        copy = pltpu.make_async_remote_copy(
+            src_ref=out_ref.at[slot, rows], dst_ref=out_ref.at[slot, rows],
+            send_sem=send_sem.at[len(sends)], recv_sem=recv_sem.at[sem_index],
+            device_id={"ctx": target}, device_id_type=pl.DeviceIdType.MESH,
+        )
+        copy.start()
+        sends.append(copy)
+
+    def arrive_part(slot, rows, sem_index):
+        pltpu.make_async_remote_copy(
+            src_ref=out_ref.at[slot, rows], dst_ref=out_ref.at[slot, rows],
+            send_sem=send_sem.at[0], recv_sem=recv_sem.at[sem_index],
+            device_id={"ctx": partner}, device_id_type=pl.DeviceIdType.MESH,
+        ).wait_recv()
 
     upward = ring // 2
-    downward = ring - 1 - upward
+    half = x_ref.shape[0] // 2
+    top = pl.ds(0, half)
+    bottom = pl.ds(half, half)
     send(me, partner, x_ref)
     send(me, up, x_ref)
     send(me, down, x_ref)
@@ -216,16 +234,20 @@
         for offset in (0, 1):
             slot = origin(-(step - 1), offset)
             arrive(slot)
-            send(slot, up, out_ref.at[slot])
-        if step <= downward:
-            for offset in (0, 1):
-                slot = origin(step - 1, offset)
-                arrive(slot)
+            if step < upward:
+                send(slot, up, out_ref.at[slot])
+            else:
+                send_part(slot, up, top, slot)
+        for offset in (0, 1):
+            slot = origin(step - 1, offset)
+            arrive(slot)
+            if step < upward:
                 send(slot, down, out_ref.at[slot])
+            else:
+                send_part(slot, down, bottom, n + offset)
     for offset in (0, 1):
-        arrive(origin(-upward, offset))
-    for offset in (0, 1):
-        arrive(origin(downward, offset))
+        arrive_part(origin(-upward, offset), top, origin(-upward, offset))
+        arrive_part(origin(upward, offset), bottom, n + offset)
     for copy in sends:
         copy.wait_send()
     local.wait()
@@ -239,8 +261,8 @@
         in_specs=[pl.BlockSpec(memory_space=pl.ANY)],
         out_specs=pl.BlockSpec(memory_space=pl.ANY),
         scratch_shapes=[
-            pltpu.SemaphoreType.DMA((n - 1,)),
-            pltpu.SemaphoreType.DMA((n,)),
+            pltpu.SemaphoreType.DMA((n + 1,)),
+            pltpu.SemaphoreType.DMA((n + 2,)),
             pltpu.SemaphoreType.DMA,
         ],
         compiler_params=pltpu.CompilerParams(collective_id=collective_id, has_side_effects=True),
@@ -258,7 +280,6 @@
     up = lax.rem(z + 1, ring) * 2 + side
     down = lax.rem(z + ring - 1, ring) * 2 + side
     upward = ring // 2
-    downward = ring - 1 - upward
     barrier = pltpu.get_barrier_semaphore()
     for d in range(1, n):
         pl.semaphore_signal(barrier, inc=1, device_id={"ctx": lax.rem(me + d, n)},
@@ -296,19 +317,39 @@
             pieces.append(total)
         return jnp.stack(pieces)
 
+    half = x_ref.shape[1] // 2
+    top = pl.ds(0, half)
+    bottom = pl.ds(half, half)
     pending_up = None
     pending_down = None
     for step in range(1, upward + 1):
         term = own(z + upward - step + 1)
-        if pending_up is not None:
+        if step == 1:
+            up_out[0, :, top] = term[:, :half].astype(up_out.dtype)
+            pending_up = send(up_out.at[0, :, top], up_in.at[0, :, top], up, 0)
+        else:
             pending_up.wait_recv()
-            term = term + up_in[step - 2].astype(jnp.float32)
-        up_out[step - 1] = term.astype(up_out.dtype)
-        pending_up = send(up_out.at[step - 1], up_in.at[step - 1], up, step - 1)
-        if step <= downward:
-            term = own(z - (downward - step + 1))
-            if pending_down is not None:
-                pending_down.wait_recv()
+            if step == 2:
+                term = jnp.concatenate(
+                    [term[:, :half] + up_in[0, :, top].astype(jnp.float32), term[:, half:]], axis=1
+                )
+            else:
+                term = term + up_in[step - 2].astype(jnp.float32)
+            up_out[step - 1] = term.astype(up_out.dtype)
+            pending_up = send(up_out.at[step - 1], up_in.at[step - 1], up, step - 1)
+        term = own(z - (upward - step + 1))
+        if step == 1:
+            down_out[0, :, bottom] = term[:, half:].astype(down_out.dtype)
+            pending_down = send(down_out.at[0, :, bottom], down_in.at[0, :, bottom], down,
+                                upward)
+        else:
+            pending_down.wait_recv()
+            if step == 2:
+                term = jnp.concatenate(
+                    [term[:, :half], term[:, half:] + down_in[0, :, bottom].astype(jnp.float32)],
+                    axis=1,
+                )
+            else:
                 term = term + down_in[step - 2].astype(jnp.float32)
             down_out[step - 1] = term.astype(down_out.dtype)
             pending_down = send(down_out.at[step - 1], down_in.at[step - 1], down,
@@ -316,9 +357,9 @@
     pending_up.wait_recv()
     pending_down.wait_recv()
     mine = (own(z) + up_in[upward - 1].astype(jnp.float32)
-            + down_in[downward - 1].astype(jnp.float32))
+            + down_in[upward - 1].astype(jnp.float32))
     side_out[...] = jnp.where(side == 0, mine[1], mine[0])
-    across = send(side_out, side_in, partner, upward + downward)
+    across = send(side_out, side_in, partner, 2 * upward)
     across.wait_recv()
     out_ref[...] = jnp.where(side == 0, mine[0], mine[1]) + side_in[...]
     for copy in sends:
@@ -334,7 +375,7 @@
     _, rows, cols = partial.shape
     ring = n // 2
     upward = ring // 2
-    downward = ring - 1 - upward
+    downward = upward
     vmem = pl.BlockSpec(memory_space=pltpu.VMEM)
     return pl.pallas_call(
         functools.partial(relay_reduce_kernel, n=n),

time: 165 us -> 159 us (0.964)
  Pallas kernels: 145 us -> 140 us
    pallas_call x1, Pallas kernels: 53.8 us -> 48.2 us  [relay_gather(): pl.pallas_call(functools.partial(relay_gather_kernel, n=n), out_shape=jax...]
    pallas_call x1, Pallas kernels: 7.12 us -> 11.9 us  [exchange(): pl.pallas_call(functools.partial(exchange_kernel, axis=axis, n=n, indexed...]
    pallas_call x1, Pallas kernels: 60.7 us -> 56.5 us  [relay_reduce(): pl.pallas_call(functools.partial(relay_reduce_kernel, n=n), out_shape=[ja...]
where the time goes in v10:
time: 159 us; the launch traced here: 157 us
  Pallas kernels  140 us (88%)
  other arithmetic  10.8 us (7%)
  local copies, waits for them, and re-layouts  3.54 us (2%)
  between operations  2.67 us (2%)
    pallas_call x1, Pallas kernels, relay_reduce(): pl.pallas_call(functools.partial(relay_reduce_kernel, n=n), out_shape=[ja...  56.5 us
    pallas_call x1, Pallas kernels, relay_gather(): pl.pallas_call(functools.partial(relay_gather_kernel, n=n), out_shape=jax...  48.2 us
    pallas_call x1, Pallas kernels, attention_grads(): pl.pallas_call(functools.partial(attention_grads_kernel, scale=scale), gr...  23.5 us
    pallas_call x1, Pallas kernels, exchange(): pl.pallas_call(functools.partial(exchange_kernel, axis=axis, n=n, indexed...  11.9 us

profile of v10, /device:TPU:13, one launch (start us, length us, event | category | flops | bytes accessed | tf_op | source)
XLA Modules:
  0.0 157.2 jit_solution(5819639296562312202)
XLA Ops:
  0.6 1.3 fusion
  1.9 1.9 %fusion.1 = s32[]{:T(128)} fusion(s32[1,16]{1,0:T(1,128)} %param.12, s32[]{:T(128)} %fusion), kind=kLoop, calls=%fused_computation.13 | loop fusion | flops 47 | bytes 72 | tf_op jit(solution)/shard_map/reduce_sum | solution.py:17
  5.8 0.1 pad_add_fusion
  5.9 0.8 select_reduce_fusion
  6.7 0.1 pad_add_fusion.1.blocks_ref.t_ref
  6.8 0.0 copy-start.3
  6.8 0.1 add_convert_fusion.flags_ref
  6.9 1.7 %pad_maximum_fusion.1.x_ref = bf16[512,256]{1,0:T(8,128)(2,1)} fusion(bf16[512,128]{1,0:T(8,128)(2,1)} %bitcast.30, bf16[512,128]{1,0:T(8,128)(2,1)} %bitcast.31), kind=kLoop, calls=%fused_computation.1 | loop fusion | flops 524288 | bytes 524288 | tf_op jit(solution)/shard_map/concatenate | solution.py:430
  8.6 0.0 copy-start
  8.6 0.0 copy-start.1
  8.6 48.2 %shard_map.118.k0.k1.k2.k3.v0.v1.v2.v3 = bf16[16,512,256]{2,1,0:T(8,128)(2,1)} custom-call(bf16[512,256]{1,0:T(8,128)(2,1)} %pad_maximum_fusion.1.x_ref), custom_call_target="tpu_custom_call" | custom-call | tf_op jit(solution)/shard_map/pallas_call | solution.py:258
  56.8 0.0 copy-done.3
  56.9 0.0 copy-done
  56.9 0.0 copy-done.1
  56.9 0.0 copy-start.2
  56.9 1.1 copy-done.2
  58.0 23.5 %shard_map.119 = (bf16[512,640]{1,0:T(8,128)(2,1)}, f32[1,640]{1,0:T(1,128)S(1)}, f32[4,512,128]{2,1,0:T(8,128)S(1)}, f32[4,512,128]{2,1,0:T(8,128)S(1)}, f32[1,128]{1,0:T(1,128)S(1)}, /*index=5*/f32[1,128]{1,0:T(1,128)S(1)}) custom-call(s32[4]{0:T(128)S(1)} %add_convert_fusion.flags_ref, s32[4]{0:T(128)S(1)} %pad_add_fusion.1.blocks_ref.t_ref, ...), custom_call_target="tpu_custom_call" | custom-call | tf_op jit(solution)/shard_map/pallas_call | solution.py:99
  81.6 0.6 reshape.26.tail_ref
  82.2 1.5 pad_maximum_fusion.x_ref
  83.6 56.5 %shard_map.120 = (f32[512,256]{1,0:T(8,128)}, f32[16,8,256]{2,1,0:T(8,128)}) custom-call(s32[4]{0:T(128)} %copy-done.3, f32[4,512,256]{2,1,0:T(8,128)} %pad_maximum_fusion.x_ref, f32[8,256]{1,0:T(8,128)} %reshape.26.tail_ref), custom_call_target="tpu_custom_call" | custom-call | tf_op jit(solution)/shard_map/pallas_call | solution.py:380
  140.2 1.1 convert.4
  141.3 0.7 slice_bitcast_fusion
  142.0 1.5 add_bitcast_fusion.x_ref
  143.5 11.9 %shard_map.121 = f32[2,8,256]{2,1,0:T(8,128)} custom-call(f32[8,256]{1,0:T(8,128)} %add_bitcast_fusion.x_ref), custom_call_target="tpu_custom_call" | custom-call | tf_op jit(solution)/shard_map/pallas_call | solution.py:157
  155.4 0.7 multiply_bitcast_fusion
  156.1 0.6 slice.96
  156.7 0.5 fusion.2
  (4 shorter events, 0.0 us)
Async XLA Ops:
  6.8 50.0 %copy-start.3 = (s32[4]{0:T(128)}, s32[4]{0:T(128)S(1)}, u32[]{:S(2)}) copy-start(s32[4]{0:T(128)S(1)} %pad_add_fusion.1.blocks_ref.t_ref) | copy-start | bytes 52
  8.6 48.3 %copy-start = (bf16[1,512,640]{2,1,0:T(8,128)(2,1)S(1)}, bf16[1,512,640]{2,1,0:T(8,128)(2,1)}, u32[]{:S(2)}) copy-start(bf16[1,512,640]{2,1,0:T(8,128)(2,1)} %param.7) | copy-start | bytes 1966084
  8.6 48.3 %copy-start.1 = (bf16[1,512,640]{2,1,0:T(8,128)(2,1)S(1)}, bf16[1,512,640]{2,1,0:T(8,128)(2,1)}, u32[]{:S(2)}) copy-start(bf16[1,512,640]{2,1,0:T(8,128)(2,1)} %param.11) | copy-start | bytes 1966084
  56.9 1.1 copy-start.2

commit v11 on v10

--- a/solution.py
+++ b/solution.py
@@ -23,17 +23,19 @@
 
 
 def attention_grads_kernel(flags_ref, blocks_ref, q_ref, g_ref, o_ref, k0, k1, k2, k3, v0, v1, v2,
-                           v3, dq_ref, dqsum_ref, dk_ref, dv_ref, ksum_ref, vsum_ref, s_scr, *,
-                           scale):
+                           v3, dq_ref, dqsum_ref, kv_ref, ksum_ref, vsum_ref, s_scr, *, scale):
     head = pl.program_id(0)
     k_refs = (k0, k1, k2, k3)
     v_refs = (v0, v1, v2, v3)
     slots = len(k_refs)
 
+    width = q_ref.shape[1]
+    dk_ref = kv_ref.at[:, :, pl.ds(0, width)]
+    dv_ref = kv_ref.at[:, :, pl.ds(width, width)]
+
     @pl.when(head == 0)
     def _():
-        dk_ref[...] = jnp.zeros_like(dk_ref)
-        dv_ref[...] = jnp.zeros_like(dv_ref)
+        kv_ref[...] = jnp.zeros_like(kv_ref)
 
     q = q_ref[...]
     g = g_ref[...]
@@ -91,7 +93,7 @@
     col = pl.BlockSpec((rows, HEAD_WIDTH), lambda h, f, b: (0, h))
     line = pl.BlockSpec((1, HEAD_WIDTH), lambda h, f, b: (0, h))
     fixed = pl.BlockSpec((1, HEAD_WIDTH), lambda h, f, b: (0, 0))
-    whole = pl.BlockSpec((slots, rows, HEAD_WIDTH), lambda h, f, b: (0, 0, 0))
+    pair_spec = pl.BlockSpec((slots, rows, 2 * HEAD_WIDTH), lambda h, f, b: (0, 0, 0))
 
     def pick(j, part):
         return pl.BlockSpec((None, rows, HEAD_WIDTH), lambda h, f, b: (b[j], 0, part))
@@ -103,14 +105,13 @@
             grid=(heads,),
             in_specs=[col, col, col] + [pick(j, 0) for j in range(slots)]
             + [pick(j, 1) for j in range(slots)],
-            out_specs=[col, line, whole, whole, fixed, fixed],
+            out_specs=[col, line, pair_spec, fixed, fixed],
             scratch_shapes=[pltpu.VMEM((slots, rows, rows), jnp.float32)],
         ),
         out_shape=[
             jax.ShapeDtypeStruct((rows, wide), jnp.bfloat16),
             jax.ShapeDtypeStruct((1, wide), jnp.float32),
-            jax.ShapeDtypeStruct((slots, rows, HEAD_WIDTH), jnp.float32),
-            jax.ShapeDtypeStruct((slots, rows, HEAD_WIDTH), jnp.float32),
+            jax.ShapeDtypeStruct((slots, rows, 2 * HEAD_WIDTH), jnp.float32),
             jax.ShapeDtypeStruct((1, HEAD_WIDTH), jnp.float32),
             jax.ShapeDtypeStruct((1, HEAD_WIDTH), jnp.float32),
         ],
@@ -269,7 +270,7 @@
     )(x)
 
 
-def relay_reduce_kernel(t_ref, x_ref, tail_ref, out_ref, tails_ref, up_in, down_in, up_out,
+def relay_reduce_kernel(t_ref, x_ref, tail_ref, dk_ref, dv_ref, tails_ref, up_in, down_in, up_out,
                         down_out, side_out, side_in, tails_in, send_sem, recv_sem, tail_send,
                         tail_recv, *, n):
     me = lax.axis_index("ctx")
@@ -361,14 +362,20 @@
     side_out[...] = jnp.where(side == 0, mine[1], mine[0])
     across = send(side_out, side_in, partner, 2 * upward)
     across.wait_recv()
-    out_ref[...] = jnp.where(side == 0, mine[0], mine[1]) + side_in[...]
+    grads = jnp.where(side == 0, mine[0], mine[1]) + side_in[...]
+    width = dk_ref.shape[1]
+    dk_ref[...] = grads[:, :width].astype(dk_ref.dtype)
+    dv_ref[...] = grads[:, width:].astype(dv_ref.dtype)
     for copy in sends:
         copy.wait_send()
     for copy in tail_copies:
         copy.wait_send()
     for copy in tail_copies:
         copy.wait_recv()
-    tails_ref[...] = tails_in[...]
+    summed = tails_in[0]
+    for peer in range(1, n):
+        summed = summed + tails_in[peer]
+    tails_ref[...] = summed
 
 
 def relay_reduce(targets, partial, tail, n, collective_id):
@@ -380,11 +387,12 @@
     return pl.pallas_call(
         functools.partial(relay_reduce_kernel, n=n),
         out_shape=[
-            jax.ShapeDtypeStruct((rows, cols), jnp.float32),
-            jax.ShapeDtypeStruct((n,) + tuple(tail.shape), jnp.float32),
+            jax.ShapeDtypeStruct((rows, cols // 2), jnp.bfloat16),
+            jax.ShapeDtypeStruct((rows, cols // 2), jnp.bfloat16),
+            jax.ShapeDtypeStruct(tuple(tail.shape), jnp.float32),
         ],
         in_specs=[pl.BlockSpec(memory_space=pltpu.SMEM), vmem, vmem],
-        out_specs=[vmem, vmem],
+        out_specs=[vmem, vmem, vmem],
         scratch_shapes=[
             pltpu.VMEM((upward, 2, rows, cols), jnp.bfloat16),
             pltpu.VMEM((downward, 2, rows, cols), jnp.bfloat16),
@@ -430,10 +438,9 @@
     pair = jnp.concatenate([key[0], value[0]], axis=1)
     gathered = relay_gather(pair, 0)
     targets = jnp.concatenate([slot_blocks, me[None].astype(jnp.int32)])
-    dq, dq_sum, dk, dv, k_sum, v_sum = attention_grads(
+    dq, dq_sum, partial, k_sum, v_sum = attention_grads(
         flags, targets, query[0], output_gradient[0], output[0], gathered, scale_factor
     )
-    partial = jnp.concatenate([dk, dv], axis=2)
     total_rows = lax.axis_size("dp") * query.shape[0] * count * tile
     norm = total_rows ** (-0.5)
     wide = query.shape[2]
@@ -443,10 +450,7 @@
         [dq_sum[0], k_sum[0], v_sum[0],
          jnp.zeros((tail_rows * tail_width - wide - tail_width,), jnp.float32)]
     ).reshape(tail_rows, tail_width)
-    grads, landed = relay_reduce(targets, partial, tail, count, 1)
-    summed = landed[0]
-    for peer in range(1, count):
-        summed = summed + landed[peer]
+    d_key, d_value, summed = relay_reduce(targets, partial, tail, count, 1)
     both = exchange(summed, "dp", False, 2)
     sums = (both[0] + both[1]).reshape(-1) * norm
     sum_q = sums[:wide]
@@ -454,8 +458,8 @@
     sum_v = sums[wide + width:wide + 2 * width]
     return (
         dq[None],
-        grads[:, :width].astype(jnp.bfloat16)[None],
-        grads[:, width:].astype(jnp.bfloat16)[None],
+        d_key[None],
+        d_value[None],
         sum_q,
         sum_k,
         sum_v,

time: 159 us -> 158 us (level)
  other arithmetic: 10.8 us -> 6.88 us
  local copies, waits for them, and re-layouts: 3.54 us -> 6.23 us
    unnamed x9 -> x13, local copies, waits for them, and re-layouts: 1.1 us -> 4.51 us
where the time goes in v11:
time: 158 us; the launch traced here: 156 us
  Pallas kernels  140 us (89%)
  other arithmetic  6.88 us (4%)
  local copies, waits for them, and re-layouts  6.23 us (4%)
  between operations  2.68 us (2%)
    pallas_call x1, Pallas kernels, relay_reduce(): pl.pallas_call(functools.partial(relay_reduce_kernel, n=n), out_shape=[ja...  56.4 us
    pallas_call x1, Pallas kernels, relay_gather(): pl.pallas_call(functools.partial(relay_gather_kernel, n=n), out_shape=jax...  48.2 us
    pallas_call x1, Pallas kernels, attention_grads(): pl.pallas_call(functools.partial(attention_grads_kernel, scale=scale), gr...  23.6 us
    pallas_call x1, Pallas kernels, exchange(): pl.pallas_call(functools.partial(exchange_kernel, axis=axis, n=n, indexed...  12.1 us
    unnamed x13, local copies, waits for them, and re-layouts  4.51 us

profile of v11, /device:TPU:13, one launch (start us, length us, event | category | flops | bytes accessed | tf_op | source)
XLA Modules:
  0.0 156.1 jit_solution(12888205500349917528)
XLA Ops:
  0.6 0.0 copy-start.1
  0.6 0.0 copy-start.2
  0.7 0.0 copy-start.3
  0.7 1.4 fusion
  2.1 1.9 %fusion.1 = s32[]{:T(128)} fusion(s32[1,16]{1,0:T(1,128)} %param.12, s32[]{:T(128)} %fusion), kind=kLoop, calls=%fused_computation.9 | loop fusion | flops 47 | bytes 72 | tf_op jit(solution)/shard_map/reduce_sum | solution.py:17
  6.0 0.1 pad_add_fusion
  6.1 0.8 select_reduce_fusion
  6.9 0.1 pad_add_fusion.1.blocks_ref.t_ref
  7.0 0.0 copy-start.4
  7.0 0.1 add_convert_fusion.flags_ref
  7.1 1.7 %pad_maximum_fusion.x_ref = bf16[512,256]{1,0:T(8,128)(2,1)} fusion(bf16[512,128]{1,0:T(8,128)(2,1)} %bitcast.28, bf16[512,128]{1,0:T(8,128)(2,1)} %bitcast.29), kind=kLoop, calls=%fused_computation | loop fusion | flops 524288 | bytes 524288 | tf_op jit(solution)/shard_map/concatenate | solution.py:438
  8.8 48.2 %shard_map.118.k0.k1.k2.k3.v0.v1.v2.v3 = bf16[16,512,256]{2,1,0:T(8,128)(2,1)} custom-call(bf16[512,256]{1,0:T(8,128)(2,1)} %pad_maximum_fusion.x_ref), custom_call_target="tpu_custom_call" | custom-call | tf_op jit(solution)/shard_map/pallas_call | solution.py:259
  57.0 0.0 copy-done.1
  57.0 0.0 copy-done.2
  57.0 0.0 copy-done.3
  57.0 23.6 %shard_map.119 = (bf16[512,640]{1,0:T(8,128)(2,1)}, f32[1,640]{1,0:T(1,128)S(1)}, f32[4,512,256]{2,1,0:T(8,128)S(1)}, f32[1,128]{1,0:T(1,128)S(1)}, f32[1,128]{1,0:T(1,128)S(1)}) custom-call(s32[4]{0:T(128)S(1)} %add_convert_fusion.flags_ref, s32[4]{0:T(128)S(1)} %pad_add_fusion.1.blocks_ref.t_ref, bf16[512,640]{1,0:T(8,128)(2,1)S(1)} %bitcast.21, ...), custom_call_target="tpu_custom_call" | custom-call | tf_op jit(solution)/shard_map/pallas_call | solution.py:101
  80.6 0.0 copy-done.4
  80.6 0.0 copy-start
  80.6 1.3 copy-done
  82.0 0.6 reshape.22.tail_ref
  82.6 56.4 %shard_map.120 = (bf16[512,128]{1,0:T(8,128)(2,1)}, bf16[512,128]{1,0:T(8,128)(2,1)}, f32[8,256]{1,0:T(8,128)}) custom-call(s32[4]{0:T(128)} %copy-done.4, f32[4,512,256]{2,1,0:T(8,128)} %copy-done, f32[8,256]{1,0:T(8,128)} %reshape.22.tail_ref), custom_call_target="tpu_custom_call" | custom-call | tf_op jit(solution)/shard_map/pallas_call | solution.py:387
  139.0 12.1 %shard_map.121 = f32[2,8,256]{2,1,0:T(8,128)} custom-call(f32[8,256]{1,0:T(8,128)} %get-tuple-element.21.x_ref), custom_call_target="tpu_custom_call" | custom-call | tf_op jit(solution)/shard_map/pallas_call | solution.py:158
  151.1 0.7 multiply_bitcast_fusion
  151.8 0.6 slice.20
  152.4 0.5 fusion.2
  152.9 1.6 %copy.16 = bf16[1,512,128]{2,1,0:T(8,128)(2,1)} copy(bf16[1,512,128]{2,1,0:T(8,128)(2,1)} %bitcast.27) | data formatting | bytes 262144
  154.5 1.6 %copy.17 = bf16[1,512,128]{2,1,0:T(8,128)(2,1)} copy(bf16[1,512,128]{2,1,0:T(8,128)(2,1)} %bitcast.26) | data formatting | bytes 262144
  (4 shorter events, 0.0 us)
Async XLA Ops:
  0.6 56.4 %copy-start.1 = (bf16[1,512,640]{2,1,0:T(8,128)(2,1)S(1)}, bf16[1,512,640]{2,1,0:T(8,128)(2,1)}, u32[]{:S(2)}) copy-start(bf16[1,512,640]{2,1,0:T(8,128)(2,1)} %param.7) | copy-start | bytes 1966084
  0.6 56.4 %copy-start.2 = (bf16[1,512,640]{2,1,0:T(8,128)(2,1)S(1)}, bf16[1,512,640]{2,1,0:T(8,128)(2,1)}, u32[]{:S(2)}) copy-start(bf16[1,512,640]{2,1,0:T(8,128)(2,1)} %param.11) | copy-start | bytes 1966084
  0.7 56.4 %copy-start.3 = (bf16[1,512,640]{2,1,0:T(8,128)(2,1)S(1)}, bf16[1,512,640]{2,1,0:T(8,128)(2,1)}, u32[]{:S(2)}) copy-start(bf16[1,512,640]{2,1,0:T(8,128)(2,1)} %param.10) | copy-start | bytes 1966084
  7.0 73.6 %copy-start.4 = (s32[4]{0:T(128)}, s32[4]{0:T(128)S(1)}, u32[]{:S(2)}) copy-start(s32[4]{0:T(128)S(1)} %pad_add_fusion.1.blocks_ref.t_ref) | copy-start | bytes 52
  80.6 1.4 copy-start

commit v12 on v11

--- a/solution.py
+++ b/solution.py
@@ -270,7 +270,7 @@
     )(x)
 
 
-def relay_reduce_kernel(t_ref, x_ref, tail_ref, dk_ref, dv_ref, tails_ref, up_in, down_in, up_out,
+def relay_reduce_kernel(t_ref, x_ref, tail_ref, out_ref, tails_ref, up_in, down_in, up_out,
                         down_out, side_out, side_in, tails_in, send_sem, recv_sem, tail_send,
                         tail_recv, *, n):
     me = lax.axis_index("ctx")
@@ -362,10 +362,7 @@
     side_out[...] = jnp.where(side == 0, mine[1], mine[0])
     across = send(side_out, side_in, partner, 2 * upward)
     across.wait_recv()
-    grads = jnp.where(side == 0, mine[0], mine[1]) + side_in[...]
-    width = dk_ref.shape[1]
-    dk_ref[...] = grads[:, :width].astype(dk_ref.dtype)
-    dv_ref[...] = grads[:, width:].astype(dv_ref.dtype)
+    out_ref[...] = jnp.where(side == 0, mine[0], mine[1]) + side_in[...]
     for copy in sends:
         copy.wait_send()
     for copy in tail_copies:
@@ -387,12 +384,11 @@
     return pl.pallas_call(
         functools.partial(relay_reduce_kernel, n=n),
         out_shape=[
-            jax.ShapeDtypeStruct((rows, cols // 2), jnp.bfloat16),
-            jax.ShapeDtypeStruct((rows, cols // 2), jnp.bfloat16),
+            jax.ShapeDtypeStruct((rows, cols), jnp.float32),
             jax.ShapeDtypeStruct(tuple(tail.shape), jnp.float32),
         ],
         in_specs=[pl.BlockSpec(memory_space=pltpu.SMEM), vmem, vmem],
-        out_specs=[vmem, vmem, vmem],
+        out_specs=[vmem, vmem],
         scratch_shapes=[
             pltpu.VMEM((upward, 2, rows, cols), jnp.bfloat16),
             pltpu.VMEM((downward, 2, rows, cols), jnp.bfloat16),
@@ -450,7 +446,7 @@
         [dq_sum[0], k_sum[0], v_sum[0],
          jnp.zeros((tail_rows * tail_width - wide - tail_width,), jnp.float32)]
     ).reshape(tail_rows, tail_width)
-    d_key, d_value, summed = relay_reduce(targets, partial, tail, count, 1)
+    grads, summed = relay_reduce(targets, partial, tail, count, 1)
     both = exchange(summed, "dp", False, 2)
     sums = (both[0] + both[1]).reshape(-1) * norm
     sum_q = sums[:wide]
@@ -458,8 +454,8 @@
     sum_v = sums[wide + width:wide + 2 * width]
     return (
         dq[None],
-        d_key[None],
-        d_value[None],
+        grads[:, :width].astype(jnp.bfloat16)[None],
+        grads[:, width:].astype(jnp.bfloat16)[None],
         sum_q,
         sum_k,
         sum_v,

time: 158 us -> 157 us (level)
  local copies, waits for them, and re-layouts: 6.23 us -> 3.81 us
    unnamed x13 -> x11, local copies, waits for them, and re-layouts: 4.51 us -> 1.37 us
where the time goes in v12:
time: 157 us; the launch traced here: 155 us
  Pallas kernels  140 us (89%)
  other arithmetic  7.95 us (5%)
  local copies, waits for them, and re-layouts  3.81 us (2%)
  between operations  2.69 us (2%)
    pallas_call x1, Pallas kernels, relay_reduce(): pl.pallas_call(functools.partial(relay_reduce_kernel, n=n), out_shape=[ja...  56.5 us
    pallas_call x1, Pallas kernels, relay_gather(): pl.pallas_call(functools.partial(relay_gather_kernel, n=n), out_shape=jax...  48.2 us
    pallas_call x1, Pallas kernels, attention_grads(): pl.pallas_call(functools.partial(attention_grads_kernel, scale=scale), gr...  23.6 us
    pallas_call x1, Pallas kernels, exchange(): pl.pallas_call(functools.partial(exchange_kernel, axis=axis, n=n, indexed...  11.9 us

profile of v12, /device:TPU:13, one launch (start us, length us, event | category | flops | bytes accessed | tf_op | source)
XLA Modules:
  0.0 154.7 jit_solution(8103530077830790418)
XLA Ops:
  0.6 0.0 copy-start.1
  0.6 0.0 copy-start.2
  0.7 0.0 copy-start.3
  0.7 1.4 fusion
  2.1 1.9 %fusion.1 = s32[]{:T(128)} fusion(s32[1,16]{1,0:T(1,128)} %param.12, s32[]{:T(128)} %fusion), kind=kLoop, calls=%fused_computation.11 | loop fusion | flops 47 | bytes 72 | tf_op jit(solution)/shard_map/reduce_sum | solution.py:17
  6.0 0.1 pad_add_fusion
  6.1 0.8 select_reduce_fusion
  6.9 0.1 pad_add_fusion.1.blocks_ref.t_ref
  7.0 0.0 copy-start.4
  7.0 0.1 add_convert_fusion.flags_ref
  7.1 1.7 %pad_maximum_fusion.x_ref = bf16[512,256]{1,0:T(8,128)(2,1)} fusion(bf16[512,128]{1,0:T(8,128)(2,1)} %bitcast.28, bf16[512,128]{1,0:T(8,128)(2,1)} %bitcast.29), kind=kLoop, calls=%fused_computation | loop fusion | flops 524288 | bytes 524288 | tf_op jit(solution)/shard_map/concatenate | solution.py:434
  8.8 48.2 %shard_map.118.k0.k1.k2.k3.v0.v1.v2.v3 = bf16[16,512,256]{2,1,0:T(8,128)(2,1)} custom-call(bf16[512,256]{1,0:T(8,128)(2,1)} %pad_maximum_fusion.x_ref), custom_call_target="tpu_custom_call" | custom-call | tf_op jit(solution)/shard_map/pallas_call | solution.py:259
  57.0 0.0 copy-done.1
  57.0 0.0 copy-done.2
  57.0 0.0 copy-done.3
  57.0 23.6 %shard_map.119 = (bf16[512,640]{1,0:T(8,128)(2,1)}, f32[1,640]{1,0:T(1,128)S(1)}, f32[4,512,256]{2,1,0:T(8,128)S(1)}, f32[1,128]{1,0:T(1,128)S(1)}, f32[1,128]{1,0:T(1,128)S(1)}) custom-call(s32[4]{0:T(128)S(1)} %add_convert_fusion.flags_ref, s32[4]{0:T(128)S(1)} %pad_add_fusion.1.blocks_ref.t_ref, bf16[512,640]{1,0:T(8,128)(2,1)S(1)} %bitcast.23, ...), custom_call_target="tpu_custom_call" | custom-call | tf_op jit(solution)/shard_map/pallas_call | solution.py:101
  80.6 0.0 copy-done.4
  80.6 0.0 copy-start
  80.6 1.3 copy-done
  82.0 0.6 reshape.22.tail_ref
  82.6 56.5 %shard_map.120 = (f32[512,256]{1,0:T(8,128)}, f32[8,256]{1,0:T(8,128)}) custom-call(s32[4]{0:T(128)} %copy-done.4, f32[4,512,256]{2,1,0:T(8,128)} %copy-done, f32[8,256]{1,0:T(8,128)} %reshape.22.tail_ref), custom_call_target="tpu_custom_call" | custom-call | tf_op jit(solution)/shard_map/pallas_call | solution.py:384
  139.1 1.1 convert.4
  140.2 0.7 slice_bitcast_fusion
  140.9 11.9 %shard_map.121 = f32[2,8,256]{2,1,0:T(8,128)} custom-call(f32[8,256]{1,0:T(8,128)} %get-tuple-element.19.x_ref), custom_call_target="tpu_custom_call" | custom-call | tf_op jit(solution)/shard_map/pallas_call | solution.py:158
  152.8 0.7 multiply_bitcast_fusion
  153.5 0.6 slice.32
  154.1 0.5 fusion.2
  (4 shorter events, 0.0 us)
Async XLA Ops:
  0.6 56.4 %copy-start.1 = (bf16[1,512,640]{2,1,0:T(8,128)(2,1)S(1)}, bf16[1,512,640]{2,1,0:T(8,128)(2,1)}, u32[]{:S(2)}) copy-start(bf16[1,512,640]{2,1,0:T(8,128)(2,1)} %param.7) | copy-start | bytes 1966084
  0.6 56.4 %copy-start.2 = (bf16[1,512,640]{2,1,0:T(8,128)(2,1)S(1)}, bf16[1,512,640]{2,1,0:T(8,128)(2,1)}, u32[]{:S(2)}) copy-start(bf16[1,512,640]{2,1,0:T(8,128)(2,1)} %param.11) | copy-start | bytes 1966084
  0.7 56.4 %copy-start.3 = (bf16[1,512,640]{2,1,0:T(8,128)(2,1)S(1)}, bf16[1,512,640]{2,1,0:T(8,128)(2,1)}, u32[]{:S(2)}) copy-start(bf16[1,512,640]{2,1,0:T(8,128)(2,1)} %param.10) | copy-start | bytes 1966084
  7.0 73.6 %copy-start.4 = (s32[4]{0:T(128)}, s32[4]{0:T(128)S(1)}, u32[]{:S(2)}) copy-start(s32[4]{0:T(128)S(1)} %pad_add_fusion.1.blocks_ref.t_ref) | copy-start | bytes 52
  80.6 1.4 copy-start

commit v13 on v12

--- a/solution.py
+++ b/solution.py
@@ -49,7 +49,7 @@
 
     top = jnp.full((rows, 1), NEGATIVE_FILL, jnp.float32)
     for j in range(slots):
-        keep = flags_ref[j] > 0
+        keep = flags_ref[slots + j] > 0
         if j == slots - 1:
             keep = jnp.logical_and(keep, causal)
         scores = lax.dot_general(q, k_refs[j][...], nt, preferred_element_type=jnp.float32) * scale
@@ -59,7 +59,7 @@
 
     total = jnp.zeros((rows, 1), jnp.float32)
     for j in range(slots):
-        keep = flags_ref[j] > 0
+        keep = flags_ref[slots + j] > 0
         if j == slots - 1:
             keep = jnp.logical_and(keep, causal)
         probs = jnp.where(keep, jnp.exp(s_scr[j] - top), 0.0)
@@ -88,7 +88,7 @@
 
 def attention_grads(flags, blocks, q, g, o, gathered, scale):
     rows, wide = q.shape
-    slots = blocks.shape[0]
+    slots = blocks.shape[0] // 2
     heads = wide // HEAD_WIDTH
     col = pl.BlockSpec((rows, HEAD_WIDTH), lambda h, f, b: (0, h))
     line = pl.BlockSpec((1, HEAD_WIDTH), lambda h, f, b: (0, h))
@@ -169,7 +169,8 @@
     )(x)
 
 
-def relay_gather_kernel(x_ref, out_ref, send_sem, recv_sem, self_sem, *, n):
+def relay_gather_kernel(owner_ref, parent_ref, x_ref, out_ref, info_ref, send_sem, recv_sem,
+                        self_sem, *, n, prompt):
     me = lax.axis_index("ctx")
     ring = n // 2
     z = me // 2
@@ -231,6 +232,21 @@
     arrive(partner)
     send(partner, up, out_ref.at[partner])
     send(partner, down, out_ref.at[partner])
+    my_tile = jnp.int32(0)
+    for tile in range(owner_ref.shape[1]):
+        my_tile = my_tile + jnp.where(owner_ref[0, tile] == me, tile, 0)
+    trained = my_tile >= prompt
+    last = owner_ref.shape[1] - 1
+    above = parent_ref[0, jnp.clip(my_tile, 0, last)]
+    second = jnp.logical_and(trained, above >= prompt)
+    info_ref[0] = owner_ref[0, 0]
+    info_ref[1] = owner_ref[0, 1]
+    info_ref[2] = owner_ref[0, jnp.clip(jnp.where(second, above, 1), 0, last)]
+    info_ref[3] = me
+    info_ref[4] = trained.astype(jnp.int32)
+    info_ref[5] = trained.astype(jnp.int32)
+    info_ref[6] = second.astype(jnp.int32)
+    info_ref[7] = trained.astype(jnp.int32)
     for step in range(2, upward + 1):
         for offset in (0, 1):
             slot = origin(-(step - 1), offset)
@@ -254,20 +270,24 @@
     local.wait()
 
 
-def relay_gather(x, collective_id):
+def relay_gather(owner, parent, x, prompt, collective_id):
     n = lax.axis_size("ctx")
+    smem = pl.BlockSpec(memory_space=pltpu.SMEM)
     return pl.pallas_call(
-        functools.partial(relay_gather_kernel, n=n),
-        out_shape=jax.ShapeDtypeStruct((n,) + tuple(x.shape), x.dtype),
-        in_specs=[pl.BlockSpec(memory_space=pl.ANY)],
-        out_specs=pl.BlockSpec(memory_space=pl.ANY),
+        functools.partial(relay_gather_kernel, n=n, prompt=prompt),
+        out_shape=[
+            jax.ShapeDtypeStruct((n,) + tuple(x.shape), x.dtype),
+            jax.ShapeDtypeStruct((8,), jnp.int32),
+        ],
+        in_specs=[smem, smem, pl.BlockSpec(memory_space=pl.ANY)],
+        out_specs=[pl.BlockSpec(memory_space=pl.ANY), smem],
         scratch_shapes=[
             pltpu.SemaphoreType.DMA((n + 1,)),
             pltpu.SemaphoreType.DMA((n + 2,)),
             pltpu.SemaphoreType.DMA,
         ],
         compiler_params=pltpu.CompilerParams(collective_id=collective_id, has_side_effects=True),
-    )(x)
+    )(owner, parent, x)
 
 
 def relay_reduce_kernel(t_ref, x_ref, tail_ref, out_ref, tails_ref, up_in, down_in, up_out,
@@ -416,26 +436,10 @@
     width = key.shape[2]
     scale_factor = HEAD_WIDTH ** (-0.5)
     prompt_tiles = count // 8
-    parent_row = parent[0]
-    owner_row = owner[0]
-    tiles = jnp.arange(count, dtype=jnp.int32)
-    my_tile = jnp.sum(jnp.where(owner_row == me, tiles, 0))
-    trained = my_tile >= prompt_tiles
-    above = pick_entry(parent_row, my_tile)
-    second = jnp.logical_and(trained, above >= prompt_tiles)
-    slot_tiles = jnp.stack(
-        [jnp.int32(0), jnp.int32(1), jnp.where(second, above, 1).astype(jnp.int32)]
-    )
-    slot_blocks = jnp.sum(
-        jnp.where(slot_tiles[:, None] == tiles[None, :], owner_row[None, :], 0), axis=1
-    ).astype(jnp.int32)
-    flags = jnp.stack([trained, trained, second, trained]).astype(jnp.int32)
-
     pair = jnp.concatenate([key[0], value[0]], axis=1)
-    gathered = relay_gather(pair, 0)
-    targets = jnp.concatenate([slot_blocks, me[None].astype(jnp.int32)])
+    gathered, info = relay_gather(owner, parent, pair, prompt_tiles, 0)
     dq, dq_sum, partial, k_sum, v_sum = attention_grads(
-        flags, targets, query[0], output_gradient[0], output[0], gathered, scale_factor
+        info, info, query[0], output_gradient[0], output[0], gathered, scale_factor
     )
     total_rows = lax.axis_size("dp") * query.shape[0] * count * tile
     norm = total_rows ** (-0.5)
@@ -446,7 +450,7 @@
         [dq_sum[0], k_sum[0], v_sum[0],
          jnp.zeros((tail_rows * tail_width - wide - tail_width,), jnp.float32)]
     ).reshape(tail_rows, tail_width)
-    grads, summed = relay_reduce(targets, partial, tail, count, 1)
+    grads, summed = relay_reduce(info, partial, tail, count, 1)
     both = exchange(summed, "dp", False, 2)
     sums = (both[0] + both[1]).reshape(-1) * norm
     sum_q = sums[:wide]

time: 157 us -> 155 us (0.987)
  other arithmetic: 7.95 us -> 3.51 us
  local copies, waits for them, and re-layouts: 3.81 us -> 7.68 us
  Pallas kernels: 140 us -> 142 us
  between operations: 2.69 us -> 0.69 us
    reduce_sum x3 -> x0, other arithmetic: 4.2 us -> none  [the longest x1 1.94 us: pick_entry(): return jnp.sum(jnp.where(spots == index, vector, 0), axis=0)]
    unnamed x11, local copies, waits for them, and re-layouts: 1.37 us -> 5.24 us
where the time goes in v13:
time: 155 us; the launch traced here: 153 us
  Pallas kernels  142 us (92%)
  local copies, waits for them, and re-layouts  7.68 us (5%)
  other arithmetic  3.51 us (2%)
    pallas_call x1, Pallas kernels, relay_reduce(): pl.pallas_call(functools.partial(relay_reduce_kernel, n=n), out_shape=[ja...  56.5 us
    pallas_call x1, Pallas kernels, relay_gather(): pl.pallas_call(functools.partial(relay_gather_kernel, n=n, prompt=prompt)...  49.5 us
    pallas_call x1, Pallas kernels, attention_grads(): pl.pallas_call(functools.partial(attention_grads_kernel, scale=scale), gr...  23.6 us
    pallas_call x1, Pallas kernels, exchange(): pl.pallas_call(functools.partial(exchange_kernel, axis=axis, n=n, indexed...  12.1 us
    unnamed x11, local copies, waits for them, and re-layouts  5.24 us

profile of v13, /device:TPU:13, one launch (start us, length us, event | category | flops | bytes accessed | tf_op | source)
XLA Modules:
  0.0 153.5 jit_solution(12674973985712316030)
XLA Ops:
  0.6 1.7 %pad_maximum_fusion.x_ref = bf16[512,256]{1,0:T(8,128)(2,1)} fusion(bf16[512,128]{1,0:T(8,128)(2,1)} %bitcast.20, bf16[512,128]{1,0:T(8,128)(2,1)} %bitcast.21), kind=kLoop, calls=%fused_computation | loop fusion | flops 524288 | bytes 524288 | tf_op jit(solution)/shard_map/concatenate | solution.py:439
  2.3 49.5 %shard_map.118 = (bf16[16,512,256]{2,1,0:T(8,128)(2,1)}, s32[8]{0:T(128)}) custom-call(s32[1,16]{1,0:T(1,128)} %owner_ref.1, s32[1,16]{1,0:T(1,128)} %parent_ref.1, bf16[512,256]{1,0:T(8,128)(2,1)} %pad_maximum_fusion.x_ref), custom_call_target="tpu_custom_call" | custom-call | tf_op jit(solution)/shard_map/pallas_call | solution.py:276
  51.8 0.0 copy-start.1
  51.8 1.1 copy-done.1
  52.9 0.0 copy-start.2
  52.9 1.1 copy-done.2
  54.0 0.0 copy-start.3
  54.0 1.1 copy-done.3
  55.1 0.0 copy-start.4
  55.1 0.6 copy-done.4
  55.7 23.6 %shard_map.119 = (bf16[512,640]{1,0:T(8,128)(2,1)}, f32[1,640]{1,0:T(1,128)S(1)}, f32[4,512,256]{2,1,0:T(8,128)S(1)}, f32[1,128]{1,0:T(1,128)S(1)}, f32[1,128]{1,0:T(1,128)S(1)}) custom-call(s32[8]{0:T(128)S(1)} %copy-done.4, s32[8]{0:T(128)S(1)} %copy-done.4, bf16[512,640]{1,0:T(8,128)(2,1)S(1)} %bitcast.15, bf16[512,640]{1,0:T(8,128)(2,1)S(1)} %bitcast.16, ...), custom_call_target="tpu_custom_call" | custom-call | tf_op jit(solution)/shard_map/pallas_call | solution.py:101
  79.3 0.0 copy-start
  79.3 1.3 copy-done
  80.6 0.6 reshape.21.tail_ref
  81.2 56.5 %shard_map.120 = (f32[512,256]{1,0:T(8,128)}, f32[8,256]{1,0:T(8,128)}) custom-call(s32[8]{0:T(128)} %get-tuple-element.15.flags_ref.blocks_ref.t_ref, f32[4,512,256]{2,1,0:T(8,128)} %copy-done, f32[8,256]{1,0:T(8,128)} %reshape.21.tail_ref), custom_call_target="tpu_custom_call" | custom-call | tf_op jit(solution)/shard_map/pallas_call | solution.py:404
  137.8 12.1 %shard_map.121 = f32[2,8,256]{2,1,0:T(8,128)} custom-call(f32[8,256]{1,0:T(8,128)} %get-tuple-element.23.x_ref), custom_call_target="tpu_custom_call" | custom-call | tf_op jit(solution)/shard_map/pallas_call | solution.py:158
  149.8 0.7 multiply_bitcast_fusion
  150.6 0.5 fusion
  151.1 1.1 convert.4
  152.2 0.7 slice_bitcast_fusion
  152.9 0.6 slice.32
  (4 shorter events, 0.0 us)
Async XLA Ops:
  51.8 1.1 copy-start.1
  52.9 1.1 copy-start.2
  54.0 1.1 copy-start.3
  55.1 0.6 copy-start.4
  79.3 1.3 copy-start

commit v14 on v13

--- a/solution.py
+++ b/solution.py
@@ -22,7 +22,7 @@
     return jnp.sum(jnp.where((spots == index)[:, None], matrix, 0.0), axis=0)
 
 
-def attention_grads_kernel(flags_ref, blocks_ref, q_ref, g_ref, o_ref, k0, k1, k2, k3, v0, v1, v2,
+def attention_grads_kernel(flags_ref, q_ref, g_ref, o_ref, k0, k1, k2, k3, v0, v1, v2,
                            v3, dq_ref, dqsum_ref, kv_ref, ksum_ref, vsum_ref, s_scr, *, scale):
     head = pl.program_id(0)
     k_refs = (k0, k1, k2, k3)
@@ -86,22 +86,22 @@
         vsum_ref[...] = jnp.sum(jnp.sum(dv_ref[...], axis=0), axis=0, keepdims=True)
 
 
-def attention_grads(flags, blocks, q, g, o, gathered, scale):
+def attention_grads(blocks, q, g, o, gathered, scale):
     rows, wide = q.shape
     slots = blocks.shape[0] // 2
     heads = wide // HEAD_WIDTH
-    col = pl.BlockSpec((rows, HEAD_WIDTH), lambda h, f, b: (0, h))
-    line = pl.BlockSpec((1, HEAD_WIDTH), lambda h, f, b: (0, h))
-    fixed = pl.BlockSpec((1, HEAD_WIDTH), lambda h, f, b: (0, 0))
-    pair_spec = pl.BlockSpec((slots, rows, 2 * HEAD_WIDTH), lambda h, f, b: (0, 0, 0))
+    col = pl.BlockSpec((rows, HEAD_WIDTH), lambda h, b: (0, h))
+    line = pl.BlockSpec((1, HEAD_WIDTH), lambda h, b: (0, h))
+    fixed = pl.BlockSpec((1, HEAD_WIDTH), lambda h, b: (0, 0))
+    pair_spec = pl.BlockSpec((slots, rows, 2 * HEAD_WIDTH), lambda h, b: (0, 0, 0))
 
     def pick(j, part):
-        return pl.BlockSpec((None, rows, HEAD_WIDTH), lambda h, f, b: (b[j], 0, part))
+        return pl.BlockSpec((None, rows, HEAD_WIDTH), lambda h, b: (b[j], 0, part))
 
     return pl.pallas_call(
         functools.partial(attention_grads_kernel, scale=scale),
         grid_spec=pltpu.PrefetchScalarGridSpec(
-            num_scalar_prefetch=2,
+            num_scalar_prefetch=1,
             grid=(heads,),
             in_specs=[col, col, col] + [pick(j, 0) for j in range(slots)]
             + [pick(j, 1) for j in range(slots)],
@@ -118,7 +118,7 @@
         compiler_params=pltpu.CompilerParams(
             dimension_semantics=("arbitrary",), vmem_limit_bytes=48 * 1024 * 1024
         ),
-    )(flags, blocks, q, g, o, *([gathered] * (2 * slots)))
+    )(blocks, q, g, o, *([gathered] * (2 * slots)))
 
 
 def exchange_kernel(x_ref, out_ref, send_sem, recv_sem, self_sem, *, axis, n, indexed):
@@ -439,7 +439,7 @@
     pair = jnp.concatenate([key[0], value[0]], axis=1)
     gathered, info = relay_gather(owner, parent, pair, prompt_tiles, 0)
     dq, dq_sum, partial, k_sum, v_sum = attention_grads(
-        info, info, query[0], output_gradient[0], output[0], gathered, scale_factor
+        info, query[0], output_gradient[0], output[0], gathered, scale_factor
     )
     total_rows = lax.axis_size("dp") * query.shape[0] * count * tile
     norm = total_rows ** (-0.5)

time: 155 us -> 155 us (level)
  no operation moved by 1% of the time
where the time goes in v14:
time: 155 us; the launch traced here: 153 us
  Pallas kernels  142 us (92%)
  local copies, waits for them, and re-layouts  7.68 us (5%)
  other arithmetic  3.51 us (2%)
    pallas_call x1, Pallas kernels, relay_reduce(): pl.pallas_call(functools.partial(relay_reduce_kernel, n=n), out_shape=[ja...  56.5 us
    pallas_call x1, Pallas kernels, relay_gather(): pl.pallas_call(functools.partial(relay_gather_kernel, n=n, prompt=prompt)...  49.5 us
    pallas_call x1, Pallas kernels, attention_grads(): pl.pallas_call(functools.partial(attention_grads_kernel, scale=scale), gr...  23.6 us
    pallas_call x1, Pallas kernels, exchange(): pl.pallas_call(functools.partial(exchange_kernel, axis=axis, n=n, indexed...  12.1 us
    unnamed x11, local copies, waits for them, and re-layouts  5.24 us

profile of v14, /device:TPU:13, one launch (start us, length us, event | category | flops | bytes accessed | tf_op | source)
XLA Modules:
  0.0 153.5 jit_solution(12404590527660975562)
XLA Ops:
  0.6 1.7 %pad_maximum_fusion.x_ref = bf16[512,256]{1,0:T(8,128)(2,1)} fusion(bf16[512,128]{1,0:T(8,128)(2,1)} %bitcast.20, bf16[512,128]{1,0:T(8,128)(2,1)} %bitcast.21), kind=kLoop, calls=%fused_computation | loop fusion | flops 524288 | bytes 524288 | tf_op jit(solution)/shard_map/concatenate | solution.py:439
  2.3 49.5 %shard_map.118 = (bf16[16,512,256]{2,1,0:T(8,128)(2,1)}, s32[8]{0:T(128)}) custom-call(s32[1,16]{1,0:T(1,128)} %owner_ref.1, s32[1,16]{1,0:T(1,128)} %parent_ref.1, bf16[512,256]{1,0:T(8,128)(2,1)} %pad_maximum_fusion.x_ref), custom_call_target="tpu_custom_call" | custom-call | tf_op jit(solution)/shard_map/pallas_call | solution.py:276
  51.8 0.0 copy-start.1
  51.8 1.1 copy-done.1
  52.9 0.0 copy-start.2
  52.9 1.1 copy-done.2
  54.0 0.0 copy-start.3
  54.0 1.1 copy-done.3
  55.1 0.0 copy-start.4
  55.1 0.6 copy-done.4
  55.7 23.6 %shard_map.119 = (bf16[512,640]{1,0:T(8,128)(2,1)}, f32[1,640]{1,0:T(1,128)S(1)}, f32[4,512,256]{2,1,0:T(8,128)S(1)}, f32[1,128]{1,0:T(1,128)S(1)}, f32[1,128]{1,0:T(1,128)S(1)}) custom-call(s32[8]{0:T(128)S(1)} %copy-done.4, bf16[512,640]{1,0:T(8,128)(2,1)S(1)} %bitcast.15, bf16[512,640]{1,0:T(8,128)(2,1)S(1)} %bitcast.16, bf16[512,640]{1,0:T(8,128)(2,1)S(1)} %bitcast.17, ...), custom_call_target="tpu_custom_call" | custom-call | tf_op jit(solution)/shard_map/pallas_call | solution.py:101
  79.3 0.0 copy-start
  79.3 1.3 copy-done
  80.6 0.6 reshape.21.tail_ref
  81.2 56.5 %shard_map.120 = (f32[512,256]{1,0:T(8,128)}, f32[8,256]{1,0:T(8,128)}) custom-call(s32[8]{0:T(128)} %get-tuple-element.15.flags_ref.t_ref, f32[4,512,256]{2,1,0:T(8,128)} %copy-done, f32[8,256]{1,0:T(8,128)} %reshape.21.tail_ref), custom_call_target="tpu_custom_call" | custom-call | tf_op jit(solution)/shard_map/pallas_call | solution.py:404
  137.8 12.1 %shard_map.121 = f32[2,8,256]{2,1,0:T(8,128)} custom-call(f32[8,256]{1,0:T(8,128)} %get-tuple-element.23.x_ref), custom_call_target="tpu_custom_call" | custom-call | tf_op jit(solution)/shard_map/pallas_call | solution.py:158
  149.8 0.7 multiply_bitcast_fusion
  150.6 0.5 fusion
  151.1 1.1 convert.4
  152.2 0.7 slice_bitcast_fusion
  152.9 0.6 slice.32
  (4 shorter events, 0.0 us)
Async XLA Ops:
  51.8 1.1 copy-start.1
  52.9 1.1 copy-start.2
  54.0 1.1 copy-start.3
  55.1 0.6 copy-start.4
  79.3 1.3 copy-start

commit v15 on v14

--- a/solution.py
+++ b/solution.py
@@ -116,7 +116,7 @@
             jax.ShapeDtypeStruct((1, HEAD_WIDTH), jnp.float32),
         ],
         compiler_params=pltpu.CompilerParams(
-            dimension_semantics=("arbitrary",), vmem_limit_bytes=48 * 1024 * 1024
+            dimension_semantics=("arbitrary",), vmem_limit_bytes=63 * 1024 * 1024
         ),
     )(blocks, q, g, o, *([gathered] * (2 * slots)))
 

time: 155 us -> 152 us (0.981)
  local copies, waits for them, and re-layouts: 7.68 us -> 2.44 us
    unnamed x11 -> x1, local copies, waits for them, and re-layouts: 5.24 us -> 0.01 us
where the time goes in v15:
time: 152 us; the launch traced here: 150 us
  Pallas kernels  142 us (93%)
  other arithmetic  4.87 us (3%)
  local copies, waits for them, and re-layouts  2.44 us (2%)
    pallas_call x1, Pallas kernels, relay_reduce(): pl.pallas_call(functools.partial(relay_reduce_kernel, n=n), out_shape=[ja...  56.5 us
    pallas_call x1, Pallas kernels, relay_gather(): pl.pallas_call(functools.partial(relay_gather_kernel, n=n, prompt=prompt)...  49.5 us
    pallas_call x1, Pallas kernels, attention_grads(): pl.pallas_call(functools.partial(attention_grads_kernel, scale=scale), gr...  24.3 us
    pallas_call x1, Pallas kernels, exchange(): pl.pallas_call(functools.partial(exchange_kernel, axis=axis, n=n, indexed...  12.1 us

profile of v15, /device:TPU:13, one launch (start us, length us, event | category | flops | bytes accessed | tf_op | source)
XLA Modules:
  0.0 150.3 jit_solution(5435802225665711294)
XLA Ops:
  0.6 1.7 %pad_maximum_fusion.x_ref = bf16[512,256]{1,0:T(8,128)(2,1)} fusion(bf16[512,128]{1,0:T(8,128)(2,1)} %bitcast.18, bf16[512,128]{1,0:T(8,128)(2,1)} %bitcast.19), kind=kLoop, calls=%fused_computation | loop fusion | flops 524288 | bytes 524288 | tf_op jit(solution)/shard_map/concatenate | solution.py:439
  2.3 49.5 %shard_map.118 = (bf16[16,512,256]{2,1,0:T(8,128)(2,1)}, s32[8]{0:T(128)}) custom-call(s32[1,16]{1,0:T(1,128)} %owner_ref.1, s32[1,16]{1,0:T(1,128)} %parent_ref.1, bf16[512,256]{1,0:T(8,128)(2,1)} %pad_maximum_fusion.x_ref), custom_call_target="tpu_custom_call" | custom-call | tf_op jit(solution)/shard_map/pallas_call | solution.py:276
  51.8 24.3 %shard_map.119 = (bf16[512,640]{1,0:T(8,128)(2,1)}, f32[1,640]{1,0:T(1,128)}, f32[4,512,256]{2,1,0:T(8,128)}, f32[1,128]{1,0:T(1,128)}, f32[1,128]{1,0:T(1,128)}) custom-call(s32[8]{0:T(128)} %get-tuple-element.15.flags_ref.t_ref, bf16[512,640]{1,0:T(8,128)(2,1)} %bitcast.15, bf16[512,640]{1,0:T(8,128)(2,1)} %bitcast.16, bf16[512,640]{1,0:T(8,128)(2,1)} %bitcast.17, ...), custom_call_target="tpu_custom_call" | custom-call | tf_op jit(solution)/shard_map/pallas_call | solution.py:101
  76.1 0.7 reduce
  76.8 0.7 pad_maximum_fusion.1
  77.5 0.6 reshape.21.tail_ref
  78.1 56.5 %shard_map.120 = (f32[512,256]{1,0:T(8,128)}, f32[8,256]{1,0:T(8,128)}) custom-call(s32[8]{0:T(128)} %get-tuple-element.15.flags_ref.t_ref, f32[4,512,256]{2,1,0:T(8,128)} %get-tuple-element.18.x_ref, f32[8,256]{1,0:T(8,128)} %reshape.21.tail_ref), custom_call_target="tpu_custom_call" | custom-call | tf_op jit(solution)/shard_map/pallas_call | solution.py:404
  134.6 12.1 %shard_map.121 = f32[2,8,256]{2,1,0:T(8,128)} custom-call(f32[8,256]{1,0:T(8,128)} %get-tuple-element.23.x_ref), custom_call_target="tpu_custom_call" | custom-call | tf_op jit(solution)/shard_map/pallas_call | solution.py:158
  146.7 0.7 multiply_bitcast_fusion
  147.4 0.5 fusion
  147.9 1.1 convert.4
  149.0 0.7 slice_bitcast_fusion
  149.7 0.6 slice.32
  (2 shorter events, 0.0 us)

commit v16 on v15

--- a/solution.py
+++ b/solution.py
@@ -23,7 +23,7 @@
 
 
 def attention_grads_kernel(flags_ref, q_ref, g_ref, o_ref, k0, k1, k2, k3, v0, v1, v2,
-                           v3, dq_ref, dqsum_ref, kv_ref, ksum_ref, vsum_ref, s_scr, *, scale):
+                           v3, dq_ref, kv_ref, tail_ref, s_scr, *, scale):
     head = pl.program_id(0)
     k_refs = (k0, k1, k2, k3)
     v_refs = (v0, v1, v2, v3)
@@ -36,6 +36,7 @@
     @pl.when(head == 0)
     def _():
         kv_ref[...] = jnp.zeros_like(kv_ref)
+        tail_ref[...] = jnp.zeros_like(tail_ref)
 
     q = q_ref[...]
     g = g_ref[...]
@@ -78,12 +79,15 @@
         dk_ref[j] += lax.dot_general(dscores, q, tn, preferred_element_type=jnp.float32) * scale
     dq = dq * scale
     dq_ref[...] = dq.astype(dq_ref.dtype)
-    dqsum_ref[...] = jnp.sum(dq, axis=0, keepdims=True)
+    tail_ref[pl.ds(head, 1), :] = jnp.sum(dq, axis=0, keepdims=True)
 
     @pl.when(head == pl.num_programs(0) - 1)
     def _():
-        ksum_ref[...] = jnp.sum(jnp.sum(dk_ref[...], axis=0), axis=0, keepdims=True)
-        vsum_ref[...] = jnp.sum(jnp.sum(dv_ref[...], axis=0), axis=0, keepdims=True)
+        heads = pl.num_programs(0)
+        tail_ref[pl.ds(heads, 1), :] = jnp.sum(jnp.sum(dk_ref[...], axis=0), axis=0, keepdims=True)
+        tail_ref[pl.ds(heads + 1, 1), :] = jnp.sum(
+            jnp.sum(dv_ref[...], axis=0), axis=0, keepdims=True
+        )
 
 
 def attention_grads(blocks, q, g, o, gathered, scale):
@@ -91,8 +95,7 @@
     slots = blocks.shape[0] // 2
     heads = wide // HEAD_WIDTH
     col = pl.BlockSpec((rows, HEAD_WIDTH), lambda h, b: (0, h))
-    line = pl.BlockSpec((1, HEAD_WIDTH), lambda h, b: (0, h))
-    fixed = pl.BlockSpec((1, HEAD_WIDTH), lambda h, b: (0, 0))
+    tail_spec = pl.BlockSpec((8, HEAD_WIDTH), lambda h, b: (0, 0))
     pair_spec = pl.BlockSpec((slots, rows, 2 * HEAD_WIDTH), lambda h, b: (0, 0, 0))
 
     def pick(j, part):
@@ -105,15 +108,13 @@
             grid=(heads,),
             in_specs=[col, col, col] + [pick(j, 0) for j in range(slots)]
             + [pick(j, 1) for j in range(slots)],
-            out_specs=[col, line, pair_spec, fixed, fixed],
+            out_specs=[col, pair_spec, tail_spec],
             scratch_shapes=[pltpu.VMEM((slots, rows, rows), jnp.float32)],
         ),
         out_shape=[
             jax.ShapeDtypeStruct((rows, wide), jnp.bfloat16),
-            jax.ShapeDtypeStruct((1, wide), jnp.float32),
             jax.ShapeDtypeStruct((slots, rows, 2 * HEAD_WIDTH), jnp.float32),
-            jax.ShapeDtypeStruct((1, HEAD_WIDTH), jnp.float32),
-            jax.ShapeDtypeStruct((1, HEAD_WIDTH), jnp.float32),
+            jax.ShapeDtypeStruct((8, HEAD_WIDTH), jnp.float32),
         ],
         compiler_params=pltpu.CompilerParams(
             dimension_semantics=("arbitrary",), vmem_limit_bytes=63 * 1024 * 1024
@@ -438,24 +439,18 @@
     prompt_tiles = count // 8
     pair = jnp.concatenate([key[0], value[0]], axis=1)
     gathered, info = relay_gather(owner, parent, pair, prompt_tiles, 0)
-    dq, dq_sum, partial, k_sum, v_sum = attention_grads(
+    dq, partial, tail = attention_grads(
         info, query[0], output_gradient[0], output[0], gathered, scale_factor
     )
     total_rows = lax.axis_size("dp") * query.shape[0] * count * tile
     norm = total_rows ** (-0.5)
     wide = query.shape[2]
-    tail_width = 2 * width
-    tail_rows = 8
-    tail = jnp.concatenate(
-        [dq_sum[0], k_sum[0], v_sum[0],
-         jnp.zeros((tail_rows * tail_width - wide - tail_width,), jnp.float32)]
-    ).reshape(tail_rows, tail_width)
     grads, summed = relay_reduce(info, partial, tail, count, 1)
     both = exchange(summed, "dp", False, 2)
     sums = (both[0] + both[1]).reshape(-1) * norm
     sum_q = sums[:wide]
-    sum_k = sums[wide:wide + width]
-    sum_v = sums[wide + width:wide + 2 * width]
+    sum_k = sums[wide:wide + HEAD_WIDTH]
+    sum_v = sums[wide + HEAD_WIDTH:wide + 2 * HEAD_WIDTH]
     return (
         dq[None],
         grads[:, :width].astype(jnp.bfloat16)[None],

time: 152 us -> 149 us (0.980)
    pallas_call x1, Pallas kernels: 12.1 us -> 10.4 us  [exchange(): pl.pallas_call(functools.partial(exchange_kernel, axis=axis, n=n, indexed...]
where the time goes in v16:
time: 149 us; the launch traced here: 146 us
  Pallas kernels  141 us (95%)
  other arithmetic  3.46 us (2%)
  local copies, waits for them, and re-layouts  1.83 us (1%)
    pallas_call x1, Pallas kernels, relay_reduce(): pl.pallas_call(functools.partial(relay_reduce_kernel, n=n), out_shape=[ja...  56.4 us
    pallas_call x1, Pallas kernels, relay_gather(): pl.pallas_call(functools.partial(relay_gather_kernel, n=n, prompt=prompt)...  49.5 us
    pallas_call x1, Pallas kernels, attention_grads(): pl.pallas_call(functools.partial(attention_grads_kernel, scale=scale), gr...  24.3 us
    pallas_call x1, Pallas kernels, exchange(): pl.pallas_call(functools.partial(exchange_kernel, axis=axis, n=n, indexed...  10.4 us

profile of v16, /device:TPU:13, one launch (start us, length us, event | category | flops | bytes accessed | tf_op | source)
XLA Modules:
  0.0 146.5 jit_solution(4391572901678350182)
XLA Ops:
  0.6 1.7 %pad_maximum_fusion.x_ref = bf16[512,256]{1,0:T(8,128)(2,1)} fusion(bf16[512,128]{1,0:T(8,128)(2,1)} %bitcast.19, bf16[512,128]{1,0:T(8,128)(2,1)} %bitcast.20), kind=kLoop, calls=%fused_computation | loop fusion | flops 524288 | bytes 524288 | tf_op jit(solution)/shard_map/concatenate | solution.py:440
  2.3 49.5 %shard_map.118 = (bf16[16,512,256]{2,1,0:T(8,128)(2,1)}, s32[8]{0:T(128)}) custom-call(s32[1,16]{1,0:T(1,128)} %owner_ref.1, s32[1,16]{1,0:T(1,128)} %parent_ref.1, bf16[512,256]{1,0:T(8,128)(2,1)} %pad_maximum_fusion.x_ref), custom_call_target="tpu_custom_call" | custom-call | tf_op jit(solution)/shard_map/pallas_call | solution.py:277
  51.8 24.3 %shard_map.119 = (bf16[512,640]{1,0:T(8,128)(2,1)}, f32[4,512,256]{2,1,0:T(8,128)}, f32[8,128]{1,0:T(8,128)}) custom-call(s32[8]{0:T(128)} %get-tuple-element.13.flags_ref.t_ref, bf16[512,640]{1,0:T(8,128)(2,1)} %bitcast.16, bf16[512,640]{1,0:T(8,128)(2,1)} %bitcast.17, bf16[512,640]{1,0:T(8,128)(2,1)} %bitcast.18, ...), custom_call_target="tpu_custom_call" | custom-call | tf_op jit(solution)/shard_map/pallas_call | solution.py:104
  76.1 56.4 %shard_map.120 = (f32[512,256]{1,0:T(8,128)}, f32[8,128]{1,0:T(8,128)}) custom-call(s32[8]{0:T(128)} %get-tuple-element.13.flags_ref.t_ref, f32[4,512,256]{2,1,0:T(8,128)} %get-tuple-element.16.x_ref, f32[8,128]{1,0:T(8,128)} %get-tuple-element.17.tail_ref), custom_call_target="tpu_custom_call" | custom-call | tf_op jit(solution)/shard_map/pallas_call | solution.py:405
  132.5 1.1 convert.4
  133.5 0.7 slice_bitcast_fusion
  134.2 10.4 %shard_map.121 = f32[2,8,128]{2,1,0:T(8,128)} custom-call(f32[8,128]{1,0:T(8,128)} %get-tuple-element.19.x_ref), custom_call_target="tpu_custom_call" | custom-call | tf_op jit(solution)/shard_map/pallas_call | solution.py:159
  144.7 0.7 add_multiply_fusion
  145.4 0.5 slice_bitcast_fusion.3
  145.9 0.6 slice_bitcast_fusion.2

commit v17 on v16

--- a/solution.py
+++ b/solution.py
@@ -292,8 +292,8 @@
 
 
 def relay_reduce_kernel(t_ref, x_ref, tail_ref, out_ref, tails_ref, up_in, down_in, up_out,
-                        down_out, side_out, side_in, tails_in, send_sem, recv_sem, tail_send,
-                        tail_recv, *, n):
+                        down_out, side_out, side_in, tails_in, pair_out, pair_in, send_sem,
+                        recv_sem, tail_send, tail_recv, pair_sem, *, n):
     me = lax.axis_index("ctx")
     ring = n // 2
     z = me // 2
@@ -306,7 +306,10 @@
     for d in range(1, n):
         pl.semaphore_signal(barrier, inc=1, device_id={"ctx": lax.rem(me + d, n)},
                             device_id_type=pl.DeviceIdType.MESH)
-    pl.semaphore_wait(barrier, n - 1)
+    other = 1 - lax.axis_index("dp")
+    pl.semaphore_signal(barrier, inc=1, device_id={"dp": other},
+                        device_id_type=pl.DeviceIdType.MESH)
+    pl.semaphore_wait(barrier, n)
     tail_copies = []
     for d in range(1, n):
         copy = pltpu.make_async_remote_copy(
@@ -393,7 +396,15 @@
     summed = tails_in[0]
     for peer in range(1, n):
         summed = summed + tails_in[peer]
-    tails_ref[...] = summed
+    pair_out[...] = summed
+    swap = pltpu.make_async_remote_copy(
+        src_ref=pair_out, dst_ref=pair_in, send_sem=pair_sem.at[0], recv_sem=pair_sem.at[1],
+        device_id={"dp": other}, device_id_type=pl.DeviceIdType.MESH,
+    )
+    swap.start()
+    swap.wait_send()
+    swap.wait_recv()
+    tails_ref[...] = summed + pair_in[...]
 
 
 def relay_reduce(targets, partial, tail, n, collective_id):
@@ -418,10 +429,13 @@
             pltpu.VMEM((rows, cols), jnp.float32),
             pltpu.VMEM((rows, cols), jnp.float32),
             pltpu.VMEM((n,) + tuple(tail.shape), jnp.float32),
+            pltpu.VMEM(tuple(tail.shape), jnp.float32),
+            pltpu.VMEM(tuple(tail.shape), jnp.float32),
             pltpu.SemaphoreType.DMA((upward + downward + 1,)),
             pltpu.SemaphoreType.DMA((upward + downward + 1,)),
             pltpu.SemaphoreType.DMA((n - 1,)),
             pltpu.SemaphoreType.DMA((n - 1,)),
+            pltpu.SemaphoreType.DMA((2,)),
         ],
         compiler_params=pltpu.CompilerParams(
             collective_id=collective_id, has_side_effects=True,
@@ -446,8 +460,7 @@
     norm = total_rows ** (-0.5)
     wide = query.shape[2]
     grads, summed = relay_reduce(info, partial, tail, count, 1)
-    both = exchange(summed, "dp", False, 2)
-    sums = (both[0] + both[1]).reshape(-1) * norm
+    sums = summed.reshape(-1) * norm
     sum_q = sums[:wide]
     sum_k = sums[wide:wide + HEAD_WIDTH]
     sum_v = sums[wide + HEAD_WIDTH:wide + 2 * HEAD_WIDTH]

time: 149 us -> 149 us (level)
    pallas_call x1 -> x0, Pallas kernels: 10.4 us -> none  [exchange(): pl.pallas_call(functools.partial(exchange_kernel, axis=axis, n=n, indexed...]
    pallas_call x1, Pallas kernels: 56.4 us -> 66.2 us  [relay_reduce(): pl.pallas_call(functools.partial(relay_reduce_kernel, n=n), out_shape=[ja...]
where the time goes in v17:
time: 149 us; the launch traced here: 146 us
  Pallas kernels  140 us (94%)
  other arithmetic  3.45 us (2%)
  local copies, waits for them, and re-layouts  1.83 us (1%)
    pallas_call x1, Pallas kernels, relay_reduce(): pl.pallas_call(functools.partial(relay_reduce_kernel, n=n), out_shape=[ja...  66.2 us
    pallas_call x1, Pallas kernels, relay_gather(): pl.pallas_call(functools.partial(relay_gather_kernel, n=n, prompt=prompt)...  49.5 us
    pallas_call x1, Pallas kernels, attention_grads(): pl.pallas_call(functools.partial(attention_grads_kernel, scale=scale), gr...  24.3 us

profile of v17, /device:TPU:13, one launch (start us, length us, event | category | flops | bytes accessed | tf_op | source)
XLA Modules:
  0.0 145.9 jit_solution(2496554465670419812)
XLA Ops:
  0.6 1.7 %pad_maximum_fusion.x_ref = bf16[512,256]{1,0:T(8,128)(2,1)} fusion(bf16[512,128]{1,0:T(8,128)(2,1)} %bitcast.19, bf16[512,128]{1,0:T(8,128)(2,1)} %bitcast.20), kind=kLoop, calls=%fused_computation | loop fusion | flops 524288 | bytes 524288 | tf_op jit(solution)/shard_map/concatenate | solution.py:454
  2.3 49.5 %shard_map.118 = (bf16[16,512,256]{2,1,0:T(8,128)(2,1)}, s32[8]{0:T(128)}) custom-call(s32[1,16]{1,0:T(1,128)} %owner_ref.1, s32[1,16]{1,0:T(1,128)} %parent_ref.1, bf16[512,256]{1,0:T(8,128)(2,1)} %pad_maximum_fusion.x_ref), custom_call_target="tpu_custom_call" | custom-call | tf_op jit(solution)/shard_map/pallas_call | solution.py:277
  51.8 24.3 %shard_map.119 = (bf16[512,640]{1,0:T(8,128)(2,1)}, f32[4,512,256]{2,1,0:T(8,128)}, f32[8,128]{1,0:T(8,128)}) custom-call(s32[8]{0:T(128)} %get-tuple-element.13.flags_ref.t_ref, bf16[512,640]{1,0:T(8,128)(2,1)} %bitcast.16, bf16[512,640]{1,0:T(8,128)(2,1)} %bitcast.17, bf16[512,640]{1,0:T(8,128)(2,1)} %bitcast.18, ...), custom_call_target="tpu_custom_call" | custom-call | tf_op jit(solution)/shard_map/pallas_call | solution.py:104
  76.1 66.2 %shard_map.120 = (f32[512,256]{1,0:T(8,128)}, f32[8,128]{1,0:T(8,128)}) custom-call(s32[8]{0:T(128)} %get-tuple-element.13.flags_ref.t_ref, f32[4,512,256]{2,1,0:T(8,128)} %get-tuple-element.16.x_ref, f32[8,128]{1,0:T(8,128)} %get-tuple-element.17.tail_ref), custom_call_target="tpu_custom_call" | custom-call | tf_op jit(solution)/shard_map/pallas_call | solution.py:416
  142.3 1.1 convert.4
  143.4 0.7 slice_bitcast_fusion
  144.1 0.7 broadcast_multiply_fusion
  144.8 0.5 slice_bitcast_fusion.3
  145.3 0.6 slice_bitcast_fusion.2

commit v18 on v17

--- a/solution.py
+++ b/solution.py
@@ -170,8 +170,8 @@
     )(x)
 
 
-def relay_gather_kernel(owner_ref, parent_ref, x_ref, out_ref, info_ref, send_sem, recv_sem,
-                        self_sem, *, n, prompt):
+def relay_gather_kernel(owner_ref, parent_ref, k_ref, v_ref, out_ref, info_ref, send_sem,
+                        recv_sem, self_sem, *, n, prompt):
     me = lax.axis_index("ctx")
     ring = n // 2
     z = me // 2
@@ -184,8 +184,15 @@
         pl.semaphore_signal(barrier, inc=1, device_id={"ctx": peer},
                             device_id_type=pl.DeviceIdType.MESH)
     pl.semaphore_wait(barrier, 3)
-    local = pltpu.make_async_copy(x_ref, out_ref.at[me], self_sem)
-    local.start()
+    width = k_ref.shape[1]
+    left = pl.ds(0, width)
+    right = pl.ds(width, width)
+    locals_ = [
+        pltpu.make_async_copy(k_ref, out_ref.at[me, :, left], self_sem.at[0]),
+        pltpu.make_async_copy(v_ref, out_ref.at[me, :, right], self_sem.at[1]),
+    ]
+    for copy in locals_:
+        copy.start()
     sends = []
 
     def send(slot, target, src):
@@ -197,9 +204,19 @@
         copy.start()
         sends.append(copy)
 
+    def send_own(target):
+        for src, cols in ((k_ref, left), (v_ref, right)):
+            copy = pltpu.make_async_remote_copy(
+                src_ref=src, dst_ref=out_ref.at[me, :, cols], send_sem=send_sem.at[len(sends)],
+                recv_sem=recv_sem.at[me], device_id={"ctx": target},
+                device_id_type=pl.DeviceIdType.MESH,
+            )
+            copy.start()
+            sends.append(copy)
+
     def arrive(slot):
         pltpu.make_async_remote_copy(
-            src_ref=x_ref, dst_ref=out_ref.at[slot], send_sem=send_sem.at[0],
+            src_ref=out_ref.at[slot], dst_ref=out_ref.at[slot], send_sem=send_sem.at[0],
             recv_sem=recv_sem.at[slot], device_id={"ctx": partner},
             device_id_type=pl.DeviceIdType.MESH,
         ).wait_recv()
@@ -224,12 +241,12 @@
         ).wait_recv()
 
     upward = ring // 2
-    half = x_ref.shape[0] // 2
+    half = k_ref.shape[0] // 2
     top = pl.ds(0, half)
     bottom = pl.ds(half, half)
-    send(me, partner, x_ref)
-    send(me, up, x_ref)
-    send(me, down, x_ref)
+    send_own(partner)
+    send_own(up)
+    send_own(down)
     arrive(partner)
     send(partner, up, out_ref.at[partner])
     send(partner, down, out_ref.at[partner])
@@ -268,27 +285,28 @@
         arrive_part(origin(upward, offset), bottom, n + offset)
     for copy in sends:
         copy.wait_send()
-    local.wait()
-
-
-def relay_gather(owner, parent, x, prompt, collective_id):
+    for copy in locals_:
+        copy.wait()
+
+
+def relay_gather(owner, parent, k, v, prompt, collective_id):
     n = lax.axis_size("ctx")
     smem = pl.BlockSpec(memory_space=pltpu.SMEM)
     return pl.pallas_call(
         functools.partial(relay_gather_kernel, n=n, prompt=prompt),
         out_shape=[
-            jax.ShapeDtypeStruct((n,) + tuple(x.shape), x.dtype),
+            jax.ShapeDtypeStruct((n, k.shape[0], 2 * k.shape[1]), k.dtype),
             jax.ShapeDtypeStruct((8,), jnp.int32),
         ],
-        in_specs=[smem, smem, pl.BlockSpec(memory_space=pl.ANY)],
+        in_specs=[smem, smem, pl.BlockSpec(memory_space=pl.ANY), pl.BlockSpec(memory_space=pl.ANY)],
         out_specs=[pl.BlockSpec(memory_space=pl.ANY), smem],
         scratch_shapes=[
-            pltpu.SemaphoreType.DMA((n + 1,)),
+            pltpu.SemaphoreType.DMA((n + 4,)),
             pltpu.SemaphoreType.DMA((n + 2,)),
-            pltpu.SemaphoreType.DMA,
+            pltpu.SemaphoreType.DMA((2,)),
         ],
         compiler_params=pltpu.CompilerParams(collective_id=collective_id, has_side_effects=True),
-    )(owner, parent, x)
+    )(owner, parent, k, v)
 
 
 def relay_reduce_kernel(t_ref, x_ref, tail_ref, out_ref, tails_ref, up_in, down_in, up_out,
@@ -451,8 +469,7 @@
     width = key.shape[2]
     scale_factor = HEAD_WIDTH ** (-0.5)
     prompt_tiles = count // 8
-    pair = jnp.concatenate([key[0], value[0]], axis=1)
-    gathered, info = relay_gather(owner, parent, pair, prompt_tiles, 0)
+    gathered, info = relay_gather(owner, parent, key[0], value[0], prompt_tiles, 0)
     dq, partial, tail = attention_grads(
         info, query[0], output_gradient[0], output[0], gathered, scale_factor
     )

time: 149 us -> 147 us (0.987)
  other arithmetic: 3.45 us -> 1.74 us
    concatenate x1 -> x0, other arithmetic: 1.7 us -> none  [on_device(): pair = jnp.concatenate([key[0], value[0]], axis=1)]
where the time goes in v18:
time: 147 us; the launch traced here: 144 us
  Pallas kernels  140 us (95%)
  local copies, waits for them, and re-layouts  1.83 us (1%)
  other arithmetic  1.74 us (1%)
    pallas_call x1, Pallas kernels, relay_reduce(): pl.pallas_call(functools.partial(relay_reduce_kernel, n=n), out_shape=[ja...  66.2 us
    pallas_call x1, Pallas kernels, relay_gather(): pl.pallas_call(functools.partial(relay_gather_kernel, n=n, prompt=prompt)...  49.6 us
    pallas_call x1, Pallas kernels, attention_grads(): pl.pallas_call(functools.partial(attention_grads_kernel, scale=scale), gr...  24.3 us

profile of v18, /device:TPU:13, one launch (start us, length us, event | category | flops | bytes accessed | tf_op | source)
XLA Modules:
  0.0 144.4 jit_solution(9734184547007662607)
XLA Ops:
  0.6 49.6 %shard_map.118 = (bf16[16,512,256]{2,1,0:T(8,128)(2,1)}, s32[8]{0:T(128)}) custom-call(s32[1,16]{1,0:T(1,128)} %owner_ref.1, s32[1,16]{1,0:T(1,128)} %parent_ref.1, bf16[512,128]{1,0:T(8,128)(2,1)} %bitcast.19, bf16[512,128]{1,0:T(8,128)(2,1)} %bitcast.20), custom_call_target="tpu_custom_call" | custom-call | tf_op jit(solution)/shard_map/pallas_call | solution.py:295
  50.3 24.3 %shard_map.119 = (bf16[512,640]{1,0:T(8,128)(2,1)}, f32[4,512,256]{2,1,0:T(8,128)}, f32[8,128]{1,0:T(8,128)}) custom-call(s32[8]{0:T(128)} %get-tuple-element.13.flags_ref.t_ref, bf16[512,640]{1,0:T(8,128)(2,1)} %bitcast.16, bf16[512,640]{1,0:T(8,128)(2,1)} %bitcast.17, bf16[512,640]{1,0:T(8,128)(2,1)} %bitcast.18, ...), custom_call_target="tpu_custom_call" | custom-call | tf_op jit(solution)/shard_map/pallas_call | solution.py:104
  74.5 66.2 %shard_map.120 = (f32[512,256]{1,0:T(8,128)}, f32[8,128]{1,0:T(8,128)}) custom-call(s32[8]{0:T(128)} %get-tuple-element.13.flags_ref.t_ref, f32[4,512,256]{2,1,0:T(8,128)} %get-tuple-element.16.x_ref, f32[8,128]{1,0:T(8,128)} %get-tuple-element.17.tail_ref), custom_call_target="tpu_custom_call" | custom-call | tf_op jit(solution)/shard_map/pallas_call | solution.py:434
  140.8 1.1 convert.4
  141.9 0.7 slice_bitcast_fusion
  142.6 0.7 broadcast_multiply_fusion
  143.3 0.5 slice_bitcast_fusion.3
  143.8 0.6 slice_bitcast_fusion.2
